TPU v7x, 256 devices: a whole 4x4x8 slice. The times are simulated.
256 devices in a mesh: branch: 2 (over x_hi), row: 16 (over z, core), chan: 8 (over x_lo, y).
Axes of the slice: x: 4 (x_hi: 2, x_lo: 2; x = x_hi * 2 + x_lo), y: 4, z: 8, core: 2. Of those that a mesh axis runs over, the one named last changes fastest.
Arguments:
- homolog_stack: bfloat16 [256, 1024, 256], P(('branch', 'row'), 'chan'), may hold values from -6 to 6
- couple_tensor: bfloat16 [1024, 1024, 128], P(('branch', 'row'), 'chan'), may hold values from -6 to 6
- amino_occupancy: int32 [1024], replicated, may hold values 0 or 1
- homolog_occupancy: int32 [256, 1024], P(('branch', 'row'), 'chan'), may hold values 0 or 1
- focus_entry_coefficients: bfloat16 [256, 1024], replicated, may hold values from -0.375 to 0.375
- couple_offset_coefficients: bfloat16 [128, 8], replicated, may hold values from -0.5 to 0.5
- focus_exit_coefficients: bfloat16 [256, 256], replicated, may hold values from -0.375 to 0.375
- tensor_entry_coefficients: bfloat16 [256, 64], replicated, may hold values from -0.375 to 0.375
- tensor_exit_coefficients: bfloat16 [1024, 128], replicated, may hold values from -1 to 1
- trio_entry_coefficients: bfloat16 [128, 512], replicated, may hold values from -0.5 to 0.5
- trio_exit_switch: bfloat16 [128, 128], replicated, may hold values from -0.5 to 0.5
- trio_exit_coefficients: bfloat16 [128, 128], replicated, may hold values from -0.5 to 0.5
Outputs:
- homolog_after_update: bfloat16 [256, 1024, 256], P(('branch', 'row'), 'chan')
- pair_result: bfloat16 [1024, 1024, 128], P(('branch', 'row'), 'chan')
All inputs are finite; a program needn't handle non-finite values. No bound on the sum of `homolog_occupancy` on one device may be relied on, other than what follows from the above.
Results may differ from a plain program's by a relative error of at most 0.012.
Values may be sent and summed in bfloat16 or wider, within the bound.
No kernel may reach another device: no remote copies, remote signals or barrier semaphores. Data moves between devices by JAX's collectives and lax.ppermute only.
A program may use at most 128 MiB of HBM per device.

v0:
```python
import jax
import jax.numpy as jnp
from jax import lax
from jax.sharding import Mesh
from jax.sharding import PartitionSpec as P

BRANCH_ROW = ("branch", "row_0", "row_1")


norm_epsilon = 1e-05
masked_logit = 1000000000.0


def side_by_side(arrays, axis, dim, along):
    ends, at = ([], 0)
    for a in arrays[:-1]:
        at += a.shape[along]
        ends.append(at)
    both = jnp.concatenate(arrays, axis=along)
    return tuple(jnp.split(lax.all_gather(both, axis, axis=dim, tiled=True), ends, axis=along))


def joined_along(blocks, dim):
    lengths = list(blocks.shape[1:])
    lengths[dim] *= blocks.shape[0]
    return jnp.moveaxis(blocks, 0, dim).reshape(lengths)


def one_gather(arrays, axis, dims):
    ravelled = jnp.concatenate([a.reshape(-1) for a in arrays])
    lines, at, gathered = (lax.all_gather(ravelled, axis), 0, [])
    for a, dim in zip(arrays, dims):
        blocks = lines[:, at : at + a.size].reshape(-1, *a.shape)
        gathered.append(joined_along(blocks, dim))
        at += a.size
    return tuple(gathered)


def in_blocks(x, dim, length):
    lengths = x.shape
    blocks = x.reshape(*lengths[:dim], length, lengths[dim] // length, *lengths[dim + 1 :])
    return jnp.moveaxis(blocks, dim, 0)


def exchange_in_order(blocks, axes, order):
    inside = blocks.shape[1:]
    filled = blocks.reshape(*(lax.axis_size(a) for a in axes), *inside)
    for k in order:
        filled = lax.all_to_all(filled, axes[k], k, k, tiled=True)
    return filled.reshape(-1, *inside)


def exchange_by_chip(x, groups, order, split_dim, concat_dim):
    length = lax.axis_size(groups[0]) * lax.axis_size(groups[1])
    blocks = in_blocks(x, split_dim, length)
    return joined_along(exchange_in_order(blocks, groups, order), concat_dim)


def standardize_features(values, axis):
    values = values.astype(jnp.float32)
    average = jnp.mean(values, axis=axis, keepdims=True)
    centered = values - average
    spread = jnp.mean(centered * centered, axis=axis, keepdims=True)
    return centered * lax.rsqrt(spread + norm_epsilon)


def shards(
    homolog_stack,
    couple_tensor,
    amino_occupancy,
    homolog_occupancy,
    focus_entry_coefficients,
    couple_offset_coefficients,
    focus_exit_coefficients,
    tensor_entry_coefficients,
    tensor_exit_coefficients,
    trio_entry_coefficients,
    trio_exit_switch,
    trio_exit_coefficients,
):
    homolog_entries, amino_positions, homolog_feature_count = homolog_stack.shape
    pair_rows, pair_cols, pair_width = couple_tensor.shape
    every_head_output = couple_offset_coefficients.shape[1]
    channels_per_head = homolog_feature_count // every_head_output
    live_mask = amino_occupancy.astype(jnp.float32)
    row_start = lax.axis_index(BRANCH_ROW) * pair_rows
    col_start = lax.axis_index("chan") * pair_cols
    live_rows = lax.dynamic_slice_in_dim(live_mask, row_start, pair_rows)
    live_cols = lax.dynamic_slice_in_dim(live_mask, col_start, pair_cols)
    homolog_standardized = standardize_features(homolog_stack, -1).astype(jnp.bfloat16)
    combined_linear_map = jnp.dot(
        homolog_standardized.reshape(-1, homolog_feature_count),
        focus_entry_coefficients,
        preferred_element_type=jnp.float32,
    )
    combined_linear_map = combined_linear_map.astype(jnp.bfloat16).reshape(
        homolog_entries, amino_positions, 4 * homolog_feature_count
    )
    combined_linear_map = lax.all_to_all(
        combined_linear_map, "chan", split_axis=2, concat_axis=1, tiled=True
    )
    combined_linear_map = combined_linear_map.reshape(
        homolog_entries, combined_linear_map.shape[1], -1, 4 * channels_per_head
    )
    pair_norm = standardize_features(couple_tensor, -1).astype(jnp.bfloat16)
    pair_bias = jnp.einsum(
        "ijc,ch->hij", pair_norm, couple_offset_coefficients, preferred_element_type=jnp.float32
    ).astype(jnp.bfloat16)
    pair_bias = lax.all_to_all(pair_bias, "chan", split_axis=0, concat_axis=2, tiled=True)
    pair_bias = lax.all_gather(pair_bias, BRANCH_ROW, axis=1, tiled=True)
    bias_float = pair_bias.astype(jnp.float32)
    key_penalty = (live_mask - 1.0) * masked_logit
    scaling = channels_per_head ** (-0.5)

    def row_attention(alignment_row):
        query_rows = alignment_row[:, :, :channels_per_head]
        key_rows = alignment_row[:, :, channels_per_head : 2 * channels_per_head]
        value_portion = alignment_row[:, :, 2 * channels_per_head : 3 * channels_per_head]
        gate_values = alignment_row[:, :, 3 * channels_per_head :].astype(jnp.float32)
        logits = (
            jnp.einsum("ihd,jhd->hij", query_rows, key_rows, preferred_element_type=jnp.float32)
            * scaling
        )
        logits = logits + bias_float + key_penalty
        weights = jax.nn.softmax(logits, axis=-1).astype(jnp.bfloat16)
        blended = jnp.einsum(
            "hij,jhd->ihd", weights, value_portion, preferred_element_type=jnp.float32
        )
        gated = (blended * jax.nn.sigmoid(gate_values)).astype(jnp.bfloat16)
        return gated.reshape(gated.shape[0], -1)

    focus_outcome = lax.map(row_attention, combined_linear_map)
    focus_outcome = lax.all_to_all(focus_outcome, "chan", split_axis=1, concat_axis=2, tiled=True)
    homolog_blended_update = jnp.dot(
        focus_outcome.reshape(-1, homolog_feature_count),
        focus_exit_coefficients,
        preferred_element_type=jnp.float32,
    )
    homolog_after_update = (
        homolog_stack.astype(jnp.float32) + homolog_blended_update.reshape(homolog_stack.shape)
    ).astype(jnp.bfloat16)
    tensor_standardized = standardize_features(homolog_after_update, -1).astype(jnp.bfloat16)
    source_target_couple = jnp.dot(
        tensor_standardized.reshape(-1, homolog_feature_count),
        tensor_entry_coefficients,
        preferred_element_type=jnp.float32,
    )
    source_target_couple = source_target_couple.reshape(homolog_entries, amino_positions, -1)
    opm_width = source_target_couple.shape[-1] // 2
    row_present = homolog_occupancy.astype(jnp.float32)[..., None]
    left_projected = (
        (source_target_couple[..., :opm_width] * row_present)
        .astype(jnp.bfloat16)
        .reshape(homolog_entries, amino_positions * opm_width)
    )
    right_projected = (
        (source_target_couple[..., opm_width:] * row_present)
        .astype(jnp.bfloat16)
        .reshape(homolog_entries, amino_positions * opm_width)
    )
    mask_portion = homolog_occupancy.astype(jnp.bfloat16)
    right_all, right_mask = side_by_side((right_projected, mask_portion), BRANCH_ROW, 0, 1)
    left_wide, left_mask = one_gather((left_projected, mask_portion), "chan", (1, 1))
    left_all, left_mask = (
        exchange_by_chip(left_wide, (("branch", "row_0"), "row_1"), (1, 0), 1, 0),
        exchange_by_chip(left_mask, (("branch", "row_0"), "row_1"), (1, 0), 1, 0),
    )
    outer_sum = lax.dot_general(
        left_all, right_all, (((0,), (0,)), ((), ())), preferred_element_type=jnp.float32
    )
    outer_sum = outer_sum.astype(jnp.bfloat16).reshape(pair_rows, opm_width, pair_cols, opm_width)
    weight_grid = tensor_exit_coefficients.reshape(opm_width, opm_width, pair_width)
    update = jnp.einsum("icjd,cdz->ijz", outer_sum, weight_grid, preferred_element_type=jnp.float32)
    counts = (
        lax.dot_general(
            left_mask, right_mask, (((0,), (0,)), ((), ())), preferred_element_type=jnp.float32
        )
        + 1.0
    )
    pair_mid = couple_tensor.astype(jnp.float32) + update / counts[..., None]
    tri_norm = standardize_features(pair_mid, -1).astype(jnp.bfloat16)
    projected = jnp.einsum(
        "ijc,cz->zij", tri_norm, trio_entry_coefficients, preferred_element_type=jnp.float32
    )
    projected = projected.reshape(4, pair_width, pair_rows, pair_cols)
    tile_live = live_rows[:, None] * live_cols[None, :]
    left_tri = (jax.nn.sigmoid(projected[0]) * projected[1] * tile_live).astype(jnp.bfloat16)
    right_tri = (jax.nn.sigmoid(projected[2]) * projected[3] * tile_live).astype(jnp.bfloat16)
    left_spread, right_spread = (
        lax.all_to_all(
            lax.all_to_all(left_tri, BRANCH_ROW, split_axis=0, concat_axis=1, tiled=True),
            "chan",
            split_axis=1,
            concat_axis=2,
            tiled=True,
        ),
        lax.all_to_all(
            lax.all_to_all(right_tri, BRANCH_ROW, split_axis=0, concat_axis=1, tiled=True),
            "chan",
            split_axis=1,
            concat_axis=2,
            tiled=True,
        ),
    )
    product = jnp.einsum(
        "cik,cjk->cij",
        left_spread,
        lax.all_gather(right_spread, "chan", axis=1, tiled=True),
        preferred_element_type=jnp.float32,
    )
    product = lax.all_to_all(
        product.astype(jnp.bfloat16), "chan", split_axis=2, concat_axis=1, tiled=True
    )
    product = exchange_by_chip(product, (("branch", "row_0"), "row_1"), (1, 0), 1, 0)
    tri_mixed = standardize_features(product, 0).astype(jnp.bfloat16)
    gating_pair = jax.nn.sigmoid(
        jnp.dot(
            tri_norm.reshape(-1, pair_width), trio_exit_switch, preferred_element_type=jnp.float32
        )
    )
    gating_pair = gating_pair.reshape(pair_rows, pair_cols, pair_width)
    triangle_update = jnp.einsum(
        "cij,cz->ijz", tri_mixed, trio_exit_coefficients, preferred_element_type=jnp.float32
    )
    pair_result = (pair_mid + triangle_update * gating_pair).astype(jnp.bfloat16)
    return (homolog_after_update, pair_result)


def solution(mesh):
    torus = Mesh(
        mesh.devices.reshape(mesh.shape["branch"], 8, 2, mesh.shape["chan"]),
        ("branch", "row_0", "row_1", "chan"),
    )
    return jax.shard_map(
        shards,
        mesh=torus,
        in_specs=(
            P(BRANCH_ROW, "chan", None),
            P(BRANCH_ROW, "chan", None),
            P(),
            P(BRANCH_ROW, "chan"),
            P(),
            P(),
            P(),
            P(),
            P(),
            P(),
            P(),
            P(),
        ),
        out_specs=(P(BRANCH_ROW, "chan", None), P(BRANCH_ROW, "chan", None)),
        check_vma=False,
    )
```

profile of v0, /device:TPU:32, one launch (start us, length us, event | category | flops | bytes accessed | tf_op | source)
XLA Modules:
  0.0 578.8 jit_solution(2463664861258584990)
XLA Ops:
  9.0 2.3 fusion.13
  12.8 11.5 %all_to_all.165 = bf16[8,32,128]{2,1,0:T(8,128)(2,1)S(1)} all-to-all(bf16[8,32,128]{2,1,0:T(8,128)(2,1)S(1)} %copy.114), channel_id=1, replica_groups=mesh['branch'=2,'row_0'=8,'row_1'=2,'chan'=8] {'chan'}, dimensions={0} | all-to-all | bytes 131072 | tf_op jit(solution)/shard_map/all_to_all | solution.py:109
  26.8 2.9 copy.112
  29.7 3.7 all-to-all-start
  33.4 24.8 %all-to-all-done = bf16[8,128,1024]{1,0,2:T(8,128)(2,1)S(1)} async-done(((bf16[8,128,1024]{1,0,2:T(8,128)(2,1)}), bf16[8,128,1024]{1,0,2:T(8,128)(2,1)S(1)}, u32[]{:S(2)}, u32[]{:S(2)}) %all-to-all-start) | async-done | bytes 2097184 | tf_op jit(solution)/shard_map/all_to_all | solution.py:99
  58.2 2.7 copy.113
  60.9 2.8 reshape.200
  63.7 40.9 %all-gather.5.cloned.1.call-done = bf16[1,1024,1024]{2,1,0:T(8,128)(2,1)} async-done(((bf16[1,32,1024]{2,1,0:T(8,128)(2,1)}), bf16[1,1024,1024]{2,1,0:T(8,128)(2,1)}) %all-gather.5.cloned.1.call-update) | async-done | bytes 2097168 | tf_op jit(solution)/shard_map/all_gather | solution.py:110
  104.7 4.1 copy.116
  108.8 40.8 %while.10 = (s32[]{:T(128)}, bf16[8,1024,32]{1,2,0:T(8,128)(2,1)}, bf16[8,1024,1,128]{1,3,2,0:T(8,128)(2,1)S(1)}, f32[1,1024,1024]{1,2,0:T(8,128)}, f32[1024]{0:T(1024)S(1)}, /*index=5*/s32[]{:T(128)}) while((s32[]{:T(128)}, bf16[8,1024,32]{1,2,0:T(8,128)(2,1)}, bf16[8,1024,1,128]{1,3,2,0:T(8,128)(2,1)S(1)}, f32[1,1024,1024]{1,2,0:T(8,128)}, ...), condition=%wide.region_7.8_spmd, body=%wide.region_4.7_spmd.sunk | while | flops 143849472 | bytes 17653844 | solution.py:132
  108.8 3.0 fusion.74
  113.9 3.0 fusion.74
  119.0 3.0 fusion.74
  124.1 3.0 fusion.74
  129.2 3.0 fusion.74
  134.3 3.0 fusion.74
  139.4 3.0 fusion.74
  144.5 3.0 fusion.74
  149.6 2.5 copy.117
  152.1 2.7 reshape.222
  154.8 4.3 all-to-all-start.2
  159.4 9.5 %all-to-all-done.2 = bf16[8,2,16384]{2,1,0:T(2,128)(2,1)S(1)} async-done(((bf16[8,2,16384]{2,1,0:T(2,128)(2,1)}), bf16[8,2,16384]{2,1,0:T(2,128)(2,1)S(1)}, u32[]{:S(2)}, u32[]{:S(2)}) %all-to-all-start.2) | async-done | bytes 524320 | tf_op jit(solution)/shard_map/all_to_all | solution.py:133
  174.7 29.9 %all-gather = bf16[270336]{0:T(1024)(128)(2,1)S(1)} all-gather(bf16[33792]{0:T(1024)(128)(2,1)S(1)} %pad_maximum_fusion), channel_id=2, replica_groups=mesh['branch'=2,'row_0'=8,'row_1'=2,'chan'=8] {'chan'}, dimensions={0}, use_global_device_ids=true | all-gather | bytes 608256 | tf_op jit(solution)/shard_map/all_gather | solution.py:31
  205.1 3.7 all_to_all.166
  210.5 4.2 all_to_all.167
  214.7 6.0 %all-to-all-start.6 = ((bf16[16,2,256]{2,1,0:T(2,128)(2,1)}), bf16[16,2,256]{2,1,0:T(2,128)(2,1)S(1)}, u32[]{:S(2)}, u32[]{:S(2)}) async-start(bf16[16,2,256]{2,1,0:T(2,128)(2,1)} %reshape.226), calls=%async_computation.6 | async-start | bytes 32768 | tf_op jit(solution)/shard_map/all_to_all | solution.py:49
  221.6 7.9 %all-to-all-done.6 = bf16[16,2,256]{2,1,0:T(2,128)(2,1)S(1)} async-done(((bf16[16,2,256]{2,1,0:T(2,128)(2,1)}), bf16[16,2,256]{2,1,0:T(2,128)(2,1)S(1)}, u32[]{:S(2)}, u32[]{:S(2)}) %all-to-all-start.6) | async-done | bytes 16416 | tf_op jit(solution)/shard_map/all_to_all | solution.py:49
  229.4 4.7 all-to-all-start.4
  234.6 17.1 %all-to-all-done.4 = bf16[16,2,8,1024]{3,2,1,0:T(8,128)(2,1)S(1)} async-done(((bf16[16,2,8,1024]{3,2,1,0:T(8,128)(2,1)}), bf16[16,2,8,1024]{3,2,1,0:T(8,128)(2,1)S(1)}, u32[]{:S(2)}, u32[]{:S(2)}) %all-to-all-start.4) | async-done | bytes 524320 | tf_op jit(solution)/shard_map/all_to_all | solution.py:49
  253.4 7.2 %convolution_convert_fusion = bf16[1024,4096]{1,0:T(8,128)(2,1)} fusion(bf16[256,1024]{1,0:T(8,128)(2,1)S(1)} %bitcast.183, bf16[256,4224]{1,0:T(8,128)(2,1)} %all-gather.7.cloned.1.call-done), kind=kOutput, calls=%fused_computation.15 | convolution fusion | flops 2151677952 | bytes 11010048 | tf_op jit(solution)/shard_map/dot_general | solution.py:168
  260.6 32.9 %reshape.205 = bf16[32,32,128,32]{3,2,1,0:T(8,128)(2,1)} reshape(bf16[1024,4096]{1,0:T(8,128)(2,1)} %convolution_convert_fusion) | data formatting | bytes 16777216 | tf_op jit(solution)/shard_map/reshape | solution.py:171
  294.5 14.5 %fusion.58 = (f32[32,128]{1,0:T(8,128)S(1)}, f32[32,128,128]{2,1,0:T(8,128)S(1)}) fusion(f32[32,128]{1,0:T(8,128)S(1)} %convolution_add_fusion, bf16[32,32,128,32]{3,2,1,0:T(8,128)(2,1)} %reshape.205, bf16[32,32,128,1]{2,1,0,3:T(8,128)(2,1)S(1)} %bitcast.194, bf16[32,128,128]{2,1,0:T(8,128)(2,1)} %param.15), kind=kOutput, calls=%fused_computation.108 | convolution fusion | flops 1075834880 | bytes 11829248 | tf_op jit(solution)/shard_map/icjd,cdz->ijz/dot_general | solution.py:173
  313.8 2.2 fusion.21
  316.0 2.7 copy.133
  318.7 36.6 %all_to_all.168 = bf16[128,32,128]{2,1,0:T(8,128)(2,1)S(1)} all-to-all(bf16[128,32,128]{2,1,0:T(8,128)(2,1)} %copy.133), channel_id=1, replica_groups=mesh['branch'=2,'row_0'=8,'row_1'=2,'chan'=8] {'branch','row_0','row_1'}, dimensions={0} | all-to-all | bytes 2097152 | tf_op jit(solution)/shard_map/all_to_all | solution.py:198
  356.2 19.0 %all_to_all.169 = bf16[4,1024,128]{2,0,1:T(4,128)(2,1)S(1)} all-to-all(bf16[4,1024,128]{2,0,1:T(4,128)(2,1)S(1)} %copy.135), channel_id=1, replica_groups=mesh['branch'=2,'row_0'=8,'row_1'=2,'chan'=8] {'chan'}, dimensions={1} | all-to-all | bytes 2097152 | tf_op jit(solution)/shard_map/all_to_all | solution.py:197
  376.6 2.7 copy.128
  379.3 35.9 %all_to_all.170 = bf16[128,32,128]{2,1,0:T(8,128)(2,1)S(1)} all-to-all(bf16[128,32,128]{2,1,0:T(8,128)(2,1)} %copy.128), channel_id=1, replica_groups=mesh['branch'=2,'row_0'=8,'row_1'=2,'chan'=8] {'branch','row_0','row_1'}, dimensions={0} | all-to-all | bytes 2097152 | tf_op jit(solution)/shard_map/all_to_all | solution.py:191
  416.1 29.4 %all_to_all.171 = bf16[4,1024,128]{2,0,1:T(4,128)(2,1)S(1)} all-to-all(bf16[4,1024,128]{2,0,1:T(4,128)(2,1)S(1)} %copy.130), channel_id=1, replica_groups=mesh['branch'=2,'row_0'=8,'row_1'=2,'chan'=8] {'chan'}, dimensions={1} | all-to-all | bytes 2097152 | tf_op jit(solution)/shard_map/all_to_all | solution.py:190
  446.7 41.8 %all-gather.9.cloned.1.call-done = bf16[4,1024,1024]{2,1,0:T(8,128)(2,1)} async-done(((bf16[4,128,1024]{2,1,0:T(8,128)(2,1)}), bf16[4,1024,1024]{2,1,0:T(8,128)(2,1)}) %all-gather.9.cloned.1.call-update) | async-done | bytes 8388624 | tf_op jit(solution)/shard_map/all_gather | solution.py:208
  488.4 7.6 %convolution_convert_fusion.2 = bf16[4,128,1024]{2,1,0:T(8,128)(2,1)} fusion(bf16[4,1024,1024]{2,1,0:T(8,128)(2,1)} %all-gather.9.cloned.1.call-done, bf16[4,8,16,8,128]{4,3,2,1,0:T(8,128)(2,1)} %bitcast.174), kind=kOutput, calls=%fused_computation.55 | convolution fusion | flops 1074266112 | bytes 10485760 | tf_op jit(solution)/shard_map/cik,cjk->cij/dot_general | solution.py:205
  496.0 2.4 copy.138
  498.4 19.4 %all_to_all.172 = bf16[4,128,1024]{1,0,2:T(4,128)(2,1)S(1)} all-to-all(bf16[4,128,1024]{1,0,2:T(4,128)(2,1)} %copy.138), channel_id=1, replica_groups=mesh['branch'=2,'row_0'=8,'row_1'=2,'chan'=8] {'chan'}, dimensions={2} | all-to-all | bytes 2097152 | tf_op jit(solution)/shard_map/all_to_all | solution.py:211
  518.9 2.3 copy.140
  522.6 4.6 all_to_all.173
  528.2 9.6 %all-to-all-start.13 = ((bf16[16,2,4,32,128]{4,3,2,1,0:T(8,128)(2,1)}), bf16[16,2,4,32,128]{4,3,2,1,0:T(8,128)(2,1)}, u32[]{:S(2)}, u32[]{:S(2)}) async-start(bf16[16,2,4,32,128]{4,3,2,1,0:T(8,128)(2,1)} %copy.142), calls=%async_computation.13 | async-start | bytes 2097152 | tf_op jit(solution)/shard_map/all_to_all | solution.py:49
  537.8 3.3 fusion.10
  541.1 24.7 %all-to-all-done.13 = bf16[16,2,4,32,128]{4,3,2,1,0:T(8,128)(2,1)} async-done(((bf16[16,2,4,32,128]{4,3,2,1,0:T(8,128)(2,1)}), bf16[16,2,4,32,128]{4,3,2,1,0:T(8,128)(2,1)}, u32[]{:S(2)}, u32[]{:S(2)}) %all-to-all-start.13) | async-done | bytes 1048608 | tf_op jit(solution)/shard_map/all_to_all | solution.py:49
  (132 shorter events, 53.3 us)
Async XLA Ops:
  7.2 18.9 %copy-start = (bf16[256,1024]{1,0:T(8,128)(2,1)S(1)}, bf16[256,1024]{1,0:T(8,128)(2,1)}, u32[]{:S(2)}) copy-start(bf16[256,1024]{1,0:T(8,128)(2,1)} %param.18) | copy-start | bytes 1572868
  7.2 4.2 copy-start.4
  7.2 4.2 copy-start.15
  7.2 17.8 %copy-start.2 = (bf16[8,128,256]{2,1,0:T(8,128)(2,1)S(1)}, bf16[8,128,256]{2,1,0:T(8,128)(2,1)}, u32[]{:S(2)}) copy-start(bf16[8,128,256]{2,1,0:T(8,128)(2,1)} %param.14) | copy-start | bytes 1572868
  7.2 97.5 %all-gather.5.cloned.1.call-start = ((), (), s32[]{:S(2)}) async-start(), calls=%async_computation.14 | async-start | bytes 2162688 | tf_op jit(solution)/shard_map/all_gather | solution.py:110
  29.7 3.8 copy-start.10
  29.7 28.5 %all-to-all-start = ((bf16[8,128,1024]{1,0,2:T(8,128)(2,1)}), bf16[8,128,1024]{1,0,2:T(8,128)(2,1)S(1)}, u32[]{:S(2)}, u32[]{:S(2)}) async-start(bf16[8,128,1024]{1,0,2:T(8,128)(2,1)} %copy.112), calls=%async_computation | async-start | bytes 4194304 | tf_op jit(solution)/shard_map/all_to_all | solution.py:99
  152.1 7.2 %copy-start.11 = (s32[8,128]{1,0:T(8,128)S(1)}, s32[8,128]{1,0:T(8,128)}, u32[]{:S(2)}) copy-start(s32[8,128]{1,0:T(8,128)} %param.17) | copy-start | bytes 12292
  154.8 14.1 %all-to-all-start.2 = ((bf16[8,2,16384]{2,1,0:T(2,128)(2,1)}), bf16[8,2,16384]{2,1,0:T(2,128)(2,1)S(1)}, u32[]{:S(2)}, u32[]{:S(2)}) async-start(bf16[8,2,16384]{2,1,0:T(2,128)(2,1)} %reshape.222), calls=%async_computation.2 | async-start | bytes 1048576 | tf_op jit(solution)/shard_map/all_to_all | solution.py:133
  159.1 94.3 %all-gather.7.cloned.1.call-start = ((), (), s32[]{:S(2)}) async-start(), calls=%async_computation.15 | async-start | bytes 2230272 | tf_op jit(solution)/shard_map/all_gather | solution.py:20
  159.4 12.1 %copy-start.8 = (bf16[256,256]{1,0:T(8,128)(2,1)S(1)}, bf16[256,256]{1,0:T(8,128)(2,1)}, u32[]{:S(2)}) copy-start(bf16[256,256]{1,0:T(8,128)(2,1)} %param.20) | copy-start | bytes 393220
  169.9 2.8 copy-start.13
  171.9 0.8 copy-start.6
  214.7 14.8 %all-to-all-start.6 = ((bf16[16,2,256]{2,1,0:T(2,128)(2,1)}), bf16[16,2,256]{2,1,0:T(2,128)(2,1)S(1)}, u32[]{:S(2)}, u32[]{:S(2)}) async-start(bf16[16,2,256]{2,1,0:T(2,128)(2,1)} %reshape.226), calls=%async_computation.6 | async-start | bytes 32768 | tf_op jit(solution)/shard_map/all_to_all | solution.py:49
  229.4 22.2 %all-to-all-start.4 = ((bf16[16,2,8,1024]{3,2,1,0:T(8,128)(2,1)}), bf16[16,2,8,1024]{3,2,1,0:T(8,128)(2,1)S(1)}, u32[]{:S(2)}, u32[]{:S(2)}) async-start(bf16[16,2,8,1024]{3,2,1,0:T(8,128)(2,1)} %copy.123), calls=%async_computation.4 | async-start | bytes 1048576 | tf_op jit(solution)/shard_map/all_to_all | solution.py:49
  234.2 254.3 %all-gather.9.cloned.1.call-start = ((), (), s32[]{:S(2)}) async-start(), calls=%async_computation.16 | async-start | bytes 9437184 | tf_op jit(solution)/shard_map/all_gather | solution.py:208
  260.6 33.9 %copy-start.12 = (bf16[1024,128]{1,0:T(8,128)(2,1)S(1)}, bf16[1024,128]{1,0:T(8,128)(2,1)}, u32[]{:S(2)}) copy-start(bf16[1024,128]{1,0:T(8,128)(2,1)} %param.22) | copy-start | bytes 786436
  310.3 2.3 copy-start.7
  311.6 1.0 copy-start.3
  527.1 10.6 %copy-start.14 = (bf16[128,128]{1,0:T(8,128)(2,1)S(1)}, bf16[128,128]{1,0:T(8,128)(2,1)}, u32[]{:S(2)}) copy-start(bf16[128,128]{1,0:T(8,128)(2,1)} %param.24) | copy-start | bytes 98308
  528.2 37.6 %all-to-all-start.13 = ((bf16[16,2,4,32,128]{4,3,2,1,0:T(8,128)(2,1)}), bf16[16,2,4,32,128]{4,3,2,1,0:T(8,128)(2,1)}, u32[]{:S(2)}, u32[]{:S(2)}) async-start(bf16[16,2,4,32,128]{4,3,2,1,0:T(8,128)(2,1)} %copy.142), calls=%async_computation.13 | async-start | bytes 2097152 | tf_op jit(solution)/shard_map/all_to_all | solution.py:49
  541.0 29.4 %copy-start.9 = (bf16[128,128]{1,0:T(8,128)(2,1)S(1)}, bf16[128,128]{1,0:T(8,128)(2,1)}, u32[]{:S(2)}) copy-start(bf16[128,128]{1,0:T(8,128)(2,1)} %param.25) | copy-start | bytes 98308
  565.7 4.7 copy-start.5
  570.4 1.9 copy-start.1
Sparse Core Ops, SparseCore 0:
  25.2 79.4 all-gather.4
  174.5 78.8 all-gather.6
  376.7 111.7 all-gather.8
where the time goes:
time: 581 us; the launch traced here: 579 us
  blocking collectives  194 us (33%)
  waiting for transfers between devices  168 us (29%)
  local copies, waits for them, and re-layouts  77.4 us (13%)
  matrix products  75.3 us (13%)
  starting transfers between devices  28.7 us (5%)
  other arithmetic  20.5 us (4%)
  between operations  14.3 us (2%)
    all_to_all x3, waiting for transfers between devices, exchange_in_order(): filled = lax.all_to_all(filled, axes[k], k, k, tiled=True)  49.6 us
    all_gather x1, waiting for transfers between devices, shards(): lax.all_gather(right_spread, 'chan', axis=1, tiled=True)  41.8 us
    all_gather x1, waiting for transfers between devices, shards(): pair_bias = lax.all_gather(pair_bias, BRANCH_ROW, axis=1, tiled=True)  40.9 us
    all_to_all x1, blocking collectives, shards(): lax.all_to_all(right_tri, BRANCH_ROW, split_axis=0, concat_axis=1, tiled=...  36.6 us
    all_to_all x1, blocking collectives, shards(): lax.all_to_all(left_tri, BRANCH_ROW, split_axis=0, concat_axis=1, tiled=T...  35.9 us
    reshape x1, local copies, waits for them, and re-layouts, shards(): outer_sum.astype(jnp.bfloat16)  32.9 us
    all_gather x1, blocking collectives, one_gather(): lines, at, gathered = (lax.all_gather(ravelled, axis), 0, [])  29.9 us
    all_to_all x1, blocking collectives, shards(): lax.all_to_all(lax.all_to_all(left_tri, BRANCH_ROW, split_axis=0, concat_...  29.4 us
  transfers between devices with their start and end apart: 8, of which 8 were waited for; matrix products, arithmetic and copies ran while one was open for 4% of the time, Pallas kernels for 0%

commit v1 on v0

v1 whole, which is shorter than its diff:
```python
import functools

import jax
import jax.numpy as jnp
from jax import lax
from jax.experimental import pallas as pl
from jax.experimental.pallas import tpu as pltpu
from jax.sharding import Mesh
from jax.sharding import PartitionSpec as P

BRANCH_ROW = ("branch", "row_0", "row_1")
PLANES = ("branch", "row_0")
CHIPS = ("branch", "row_0", "chan")
SWAP = ((0, 1), (1, 0))
EPSILON = 1e-05
MASKED = 1000000000.0
LOG2E = 1.4426950408889634
BF16 = jnp.bfloat16
F32 = jnp.float32
VMEM_LIMIT = 60 * 1024 * 1024


def params(*semantics):
    return pltpu.CompilerParams(
        dimension_semantics=semantics or ("arbitrary",), vmem_limit_bytes=VMEM_LIMIT
    )


def dot(a, b, dims):
    return lax.dot_general(a, b, ((dims[:1], dims[1:]), ((), ())), preferred_element_type=F32)


def standardize(values, axis):
    values = values.astype(F32)
    centered = values - jnp.mean(values, axis=axis, keepdims=True)
    spread = jnp.mean(centered * centered, axis=axis, keepdims=True)
    return centered * lax.rsqrt(spread + EPSILON)


def sigmoid(x):
    return 1.0 / (1.0 + jnp.exp(-x))


def whole(shape):
    return pl.BlockSpec(shape, lambda *_: (0,) * len(shape))


def project_kernel(heads, width, x_ref, w_ref, qkv_ref, gate_ref):
    normed = standardize(x_ref[0], -1).astype(BF16)
    packed = dot(w_ref[...], normed, (1, 1))
    for h in range(heads):
        base = h * 4 * width
        qkv_ref[h, 0] = packed[base : base + 3 * width].astype(BF16)
        gate_ref[0, h * width : (h + 1) * width] = packed[
            base + 3 * width : base + 4 * width
        ].astype(BF16)


def project_msa(stack, weights, heads):
    entries, residues, features = stack.shape
    width = features // heads
    return pl.pallas_call(
        functools.partial(project_kernel, heads, width),
        grid=(entries,),
        in_specs=[
            pl.BlockSpec((1, residues, features), lambda s: (s, 0, 0)),
            whole((4 * features, features)),
        ],
        out_specs=[
            pl.BlockSpec((heads, 1, 3 * width, residues), lambda s: (0, s, 0, 0)),
            pl.BlockSpec((1, features, residues), lambda s: (s, 0, 0)),
        ],
        out_shape=[
            jax.ShapeDtypeStruct((heads, entries, 3 * width, residues), BF16),
            jax.ShapeDtypeStruct((entries, features, residues), BF16),
        ],
        compiler_params=params(),
        name="project_msa",
    )(stack, weights.T)


def attend_kernel(width, me_ref, qkv_ref, mine_ref, other_ref, pen_ref, out_ref, bias_ref):
    block = pl.program_id(0)
    columns, entries = qkv_ref.shape[0], qkv_ref.shape[1]
    lanes = qkv_ref.shape[3]
    tile = mine_ref.shape[2]
    first = me_ref[0] == 0
    for plane in range(mine_ref.shape[0]):
        for j in range(columns):
            a = mine_ref[plane, j].astype(F32)
            b = other_ref[plane, j].astype(F32)
            pen = pen_ref[:, j * lanes : (j + 1) * lanes]
            row = plane * 2 * tile
            at = slice(j * lanes, (j + 1) * lanes)
            bias_ref[row : row + tile, at] = (jnp.where(first, a, b) + pen) * LOG2E
            bias_ref[row + tile : row + 2 * tile, at] = (jnp.where(first, b, a) + pen) * LOG2E
    scale = width ** (-0.5) * LOG2E
    ones = jnp.ones((8, columns * lanes), BF16)
    for s in range(entries):
        query = qkv_ref[block, s, 0:width]
        keys = jnp.concatenate([qkv_ref[j, s, width : 2 * width] for j in range(columns)], axis=1)
        values = jnp.concatenate(
            [qkv_ref[j, s, 2 * width : 3 * width] for j in range(columns)], axis=1
        )
        logits = dot(query, keys, (0, 0)) * scale + bias_ref[...]
        top = jnp.max(logits, axis=1, keepdims=True)
        weights = jnp.exp2(logits - top).astype(BF16)
        blended = dot(jnp.concatenate([values, ones], axis=0), weights, (1, 1))
        out_ref[0, s] = (blended[:width] * (1.0 / blended[width : width + 1])).astype(BF16)


def attend(me, qkv, mine, other, pen, width):
    columns, entries, _, lanes = qkv.shape
    planes, _, tile, _ = mine.shape
    per = lanes // (2 * tile)
    bias_spec = pl.BlockSpec((per, columns, tile, lanes), lambda b, me: (b, 0, 0, 0))
    return pl.pallas_call(
        functools.partial(attend_kernel, width),
        grid_spec=pltpu.PrefetchScalarGridSpec(
            num_scalar_prefetch=1,
            grid=(columns,),
            in_specs=[whole(qkv.shape), bias_spec, bias_spec, whole(pen.shape)],
            out_specs=pl.BlockSpec((1, entries, width, lanes), lambda b, me: (b, 0, 0, 0)),
            scratch_shapes=[pltpu.VMEM((lanes, columns * lanes), F32)],
        ),
        out_shape=jax.ShapeDtypeStruct((columns, entries, width, lanes), BF16),
        compiler_params=params(),
        name="attend",
    )(me, qkv, mine, other, pen)


def sides_kernel(
    side, att_ref, gate_ref, stack_ref, mask_ref, wo_ref, wl_ref, wr_ref, out_ref, left_ref, right_ref, hold_ref
):
    s = pl.program_id(0)
    residues = stack_ref.shape[1]
    attended = att_ref[...].astype(F32).reshape(-1, residues)
    gated = (attended * sigmoid(gate_ref[0].astype(F32))).astype(BF16)
    updated = (stack_ref[0].astype(F32) + dot(gated, wo_ref[...], (0, 0))).astype(BF16)
    out_ref[0] = updated
    normed = standardize(updated, -1).astype(BF16)
    mask = mask_ref[0]
    right = dot(wr_ref[...], normed, (1, 1)) * mask
    hold_ref[pl.ds(s, side, stride=8), :] = right
    hold_ref[pl.ds(side * 8 + s, 1), :] = mask
    group = 128 // side
    spread = dot(normed, wl_ref[...], (1, 0))
    rows = lax.broadcasted_iota(jnp.int32, spread.shape, 0)
    lanes = lax.broadcasted_iota(jnp.int32, spread.shape, 1)
    spread = jnp.where(rows % group == lanes // side, spread, 0.0).astype(BF16)
    to = lax.broadcasted_iota(jnp.int32, (residues // group, residues), 0)
    of = lax.broadcasted_iota(jnp.int32, (residues // group, residues), 1)
    gather = (jnp.where(of // group == to, 1.0, 0.0) * mask).astype(BF16)
    left_ref[0, 0 : residues // group] = dot(gather, spread, (1, 0)).astype(BF16)
    tail = lax.broadcasted_iota(jnp.int32, (16, residues), 0)
    left_ref[0, residues // group :] = jnp.where(tail == 0, mask, 0.0).astype(BF16)

    @pl.when(s == pl.num_programs(0) - 1)
    def _():
        right_ref[...] = hold_ref[...].astype(BF16)


def sides(attended, gate, stack, mask, w_out, w_sides):
    entries, residues, features = stack.shape
    heads, _, width, _ = attended.shape
    side = w_sides.shape[1] // 2
    group = 128 // side
    rows = residues // group + 16
    return pl.pallas_call(
        functools.partial(sides_kernel, side),
        grid=(entries,),
        in_specs=[
            pl.BlockSpec((heads, 1, width, residues), lambda s: (0, s, 0, 0)),
            pl.BlockSpec((1, features, residues), lambda s: (s, 0, 0)),
            pl.BlockSpec((1, residues, features), lambda s: (s, 0, 0)),
            pl.BlockSpec((1, 1, residues), lambda s: (s, 0, 0)),
            whole(w_out.shape),
            whole((features, 128)),
            whole((side, features)),
        ],
        out_specs=[
            pl.BlockSpec((1, residues, features), lambda s: (s, 0, 0)),
            pl.BlockSpec((1, rows, 128), lambda s: (s, 0, 0)),
            whole(((side + 1) * 8, residues)),
        ],
        out_shape=[
            jax.ShapeDtypeStruct(stack.shape, BF16),
            jax.ShapeDtypeStruct((entries, rows, 128), BF16),
            jax.ShapeDtypeStruct(((side + 1) * 8, residues), BF16),
        ],
        scratch_shapes=[pltpu.VMEM(((side + 1) * 8, residues), F32)],
        compiler_params=params(),
        name="sides",
    )(
        attended,
        gate,
        stack,
        mask[:, None, :].astype(F32),
        w_out,
        jnp.tile(w_sides[:, :side], (1, group)),
        w_sides[:, side:].T,
    )


def outer_kernel(
    side, at_ref, left_ref, lmask_ref, right_ref, rmask_ref, couple_ref, live_ref, we_ref, wt_ref,
    mid_ref, l_ref, r_ref, x_ref, count_ref,
):
    step = pl.program_id(0)
    rows, lanes = couple_ref.shape[0], couple_ref.shape[1]
    channels = couple_ref.shape[2]

    @pl.when(step == 0)
    def _():
        count_ref[...] = 1.0 / (dot(lmask_ref[...], rmask_ref[...], (0, 0)) + 1.0)

    wide = 8 * lanes
    for chunk in range(side * lanes // wide):
        outer = dot(
            left_ref[0], right_ref[:, chunk * wide : (chunk + 1) * wide], (0, 0)
        ).astype(BF16)
        for k in range(8):
            d = chunk * 8 + k
            for i in range(rows):
                x_ref[d * side : (d + 1) * side, i * lanes : (i + 1) * lanes] = outer[
                    i * side : (i + 1) * side, k * lanes : (k + 1) * lanes
                ]
    update = dot(we_ref[...], x_ref[...], (1, 0))
    normed = []
    for i in range(rows):
        over = count_ref[pl.ds(at_ref[0] * 32 + step * rows + i, 1), :]
        mid = couple_ref[i].astype(F32).T + update[:, i * lanes : (i + 1) * lanes] * over
        mid_ref[i] = mid
        normed.append(standardize(mid, 0).astype(BF16))
    normed = jnp.concatenate(normed, axis=1)
    for part, ref in ((0, l_ref), (2, r_ref)):
        gate = dot(wt_ref[part * channels : (part + 1) * channels], normed, (1, 0))
        value = dot(wt_ref[(part + 1) * channels : (part + 2) * channels], normed, (1, 0))
        both = sigmoid(gate) * value
        for i in range(rows):
            live = live_ref[pl.ds(step * rows + i, 1), :]
            ref[i] = (both[:, i * lanes : (i + 1) * lanes] * live).astype(BF16)


def outer(at, left, lmask, right, rmask, couple, live, w_exit, w_tri):
    steps, entries, _ = left.shape
    pair_rows, lanes, channels = couple.shape
    rows = pair_rows // steps
    side = right.shape[1] // lanes
    tile = pl.BlockSpec((rows, channels, lanes), lambda t, at: (t, 0, 0))
    w_exit = w_exit.reshape(side, side, channels).transpose(2, 1, 0).reshape(channels, side * side)
    return pl.pallas_call(
        functools.partial(outer_kernel, side),
        grid_spec=pltpu.PrefetchScalarGridSpec(
            num_scalar_prefetch=1,
            grid=(steps,),
            in_specs=[
                pl.BlockSpec((1, entries, 128), lambda t, at: (t, 0, 0)),
                whole(lmask.shape),
                whole(right.shape),
                whole(rmask.shape),
                pl.BlockSpec((rows, lanes, channels), lambda t, at: (t, 0, 0)),
                whole(live.shape),
                whole(w_exit.shape),
                whole((4 * channels, channels)),
            ],
            out_specs=[tile, tile, tile],
            scratch_shapes=[
                pltpu.VMEM((side * side, rows * lanes), BF16),
                pltpu.VMEM((128, lanes), F32),
            ],
        ),
        out_shape=[
            jax.ShapeDtypeStruct((pair_rows, channels, lanes), F32),
            jax.ShapeDtypeStruct((pair_rows, channels, lanes), BF16),
            jax.ShapeDtypeStruct((pair_rows, channels, lanes), BF16),
        ],
        compiler_params=params(),
        name="outer",
    )(at, left, lmask, right, rmask, couple, live, w_exit, w_tri.T)


def triangle_kernel(me_ref, l_ref, mine_ref, other_ref, out_ref):
    planes, columns, tile, lanes = l_ref.shape
    first = me_ref[0] == 0
    joined = lambda ref, p: jnp.concatenate([ref[p, k] for k in range(columns)], axis=1)
    rights = []
    for p in range(mine_ref.shape[0]):
        a, b = joined(mine_ref, p), joined(other_ref, p)
        rights += [jnp.where(first, a, b), jnp.where(first, b, a)]
    right = jnp.concatenate(rights, axis=0)
    per = lanes // (2 * tile)
    for p in range(0, planes, 4):
        left = jnp.concatenate([joined(l_ref, p + q) for q in range(4)], axis=0)
        product = dot(left, right, (1, 1)).astype(BF16)
        for q in range(4):
            for n in range(mine_ref.shape[0] // per):
                out_ref[p + q, n] = product[
                    q * tile : (q + 1) * tile, n * lanes : (n + 1) * lanes
                ]


def triangle(me, left, mine, other):
    planes, columns, tile, lanes = left.shape
    per = lanes // (2 * tile)
    take = 2
    spec = pl.BlockSpec((per * take, columns, tile, lanes), lambda n, me: (n, 0, 0, 0))
    return pl.pallas_call(
        triangle_kernel,
        grid_spec=pltpu.PrefetchScalarGridSpec(
            num_scalar_prefetch=1,
            grid=(columns // take,),
            in_specs=[whole(left.shape), spec, spec],
            out_specs=pl.BlockSpec((planes, take, tile, lanes), lambda n, me: (0, n, 0, 0)),
        ),
        out_shape=jax.ShapeDtypeStruct(left.shape, BF16),
        compiler_params=params(),
        name="triangle",
    )(me, left, mine, other)


def finish_kernel(prod_ref, mid_ref, wo_ref, ws_ref, out_ref, mixed_ref):
    step = pl.program_id(0)
    channels, pair_rows, lanes = prod_ref.shape
    rows = mid_ref.shape[0]

    @pl.when(step == 0)
    def _():
        total = jnp.zeros((pair_rows, lanes), F32)
        for c in range(channels):
            total = total + prod_ref[c].astype(F32)
        mean = total / channels
        spread = jnp.zeros((pair_rows, lanes), F32)
        for c in range(channels):
            centered = prod_ref[c].astype(F32) - mean
            spread = spread + centered * centered
        inverse = lax.rsqrt(spread / channels + EPSILON)
        for c in range(channels):
            mixed_ref[c * pair_rows : (c + 1) * pair_rows, :] = (
                prod_ref[c].astype(F32) - mean
            ) * inverse

    mixed, normed = [], []
    for i in range(rows):
        mixed.append(
            mixed_ref[pl.ds(step * rows + i, channels, stride=pair_rows), :].astype(BF16)
        )
        normed.append(standardize(mid_ref[i], 0).astype(BF16))
    update = dot(wo_ref[...], jnp.concatenate(mixed, axis=1), (1, 0))
    gate = sigmoid(dot(ws_ref[...], jnp.concatenate(normed, axis=1), (1, 0)))
    update = update * gate
    for i in range(rows):
        result = mid_ref[i] + update[:, i * lanes : (i + 1) * lanes]
        out_ref[i] = result.T.astype(BF16)


def finish(product, mid, w_out, w_switch):
    channels, pair_rows, lanes = product.shape
    rows = 4
    return pl.pallas_call(
        finish_kernel,
        grid=(pair_rows // rows,),
        in_specs=[
            whole(product.shape),
            pl.BlockSpec((rows, channels, lanes), lambda t: (t, 0, 0)),
            whole(w_out.shape),
            whole(w_switch.shape),
        ],
        out_specs=pl.BlockSpec((rows, lanes, channels), lambda t: (t, 0, 0)),
        out_shape=jax.ShapeDtypeStruct((pair_rows, lanes, channels), BF16),
        scratch_shapes=[pltpu.VMEM((channels * pair_rows, lanes), F32)],
        compiler_params=params(),
        name="finish",
    )(product, mid, w_out.T, w_switch.T)


def swap(x):
    return lax.ppermute(x, "row_1", SWAP)


def exchange(x, axes):
    return lax.all_to_all(x, axes, 0, 0, tiled=True)


def repeated(x, n):
    return jnp.broadcast_to(x[None], (n, *x.shape))


def shards(
    homolog_stack,
    couple_tensor,
    amino_occupancy,
    homolog_occupancy,
    focus_entry_coefficients,
    couple_offset_coefficients,
    focus_exit_coefficients,
    tensor_entry_coefficients,
    tensor_exit_coefficients,
    trio_entry_coefficients,
    trio_exit_switch,
    trio_exit_coefficients,
):
    entries, residues, features = homolog_stack.shape
    pair_rows, pair_cols, pair_width = couple_tensor.shape
    heads = couple_offset_coefficients.shape[1]
    width = features // heads
    side = tensor_entry_coefficients.shape[1] // 2
    planes = lax.axis_size("branch") * lax.axis_size("row_0")
    chan = lax.axis_size("chan")
    core = lax.axis_index("row_1").astype(jnp.int32)
    row = lax.axis_index(BRANCH_ROW).astype(jnp.int32)
    me = core.reshape(1)
    live = amino_occupancy.astype(F32)
    live_rows = lax.dynamic_slice_in_dim(live, row * pair_rows, pair_rows)
    live_cols = lax.dynamic_slice_in_dim(live, lax.axis_index("chan") * pair_cols, pair_cols)
    penalty = ((live - 1.0) * MASKED)[None, :]

    pair_norm = standardize(couple_tensor, -1).astype(BF16)
    bias = jnp.einsum(
        "ijc,ch->hij", pair_norm, couple_offset_coefficients, preferred_element_type=F32
    ).astype(BF16)
    bias = exchange(bias, "chan")
    bias = exchange(repeated(bias, planes), PLANES)
    bias_other = swap(bias)

    qkv, gate = project_msa(homolog_stack, focus_entry_coefficients, heads)
    qkv = exchange(qkv, "chan")
    attended = attend(me, qkv, bias, bias_other, penalty, width)
    attended = exchange(attended, "chan")

    homolog_after_update, left, right = sides(
        attended,
        gate,
        homolog_stack,
        homolog_occupancy,
        focus_exit_coefficients,
        tensor_entry_coefficients,
    )
    left = exchange(left, "chan")
    packed_rows = residues * side // 128
    per_plane = left.shape[0] * packed_rows // planes
    parts = jnp.concatenate(
        [
            repeated(right, planes),
            left[:, :packed_rows].reshape(planes, per_plane, 128),
            jnp.repeat(left[:, packed_rows : packed_rows + 8], planes // chan, axis=0),
        ],
        axis=1,
    )
    mine = exchange(parts, PLANES)
    other = swap(mine)
    both = jnp.stack([mine, other]).reshape(2 * planes, *mine.shape[1:])
    sources = 2 * planes
    wide = side * 8
    right_all = both[:, :wide].reshape(sources, side, 8, pair_cols)
    right_all = right_all.transpose(0, 2, 1, 3).reshape(sources * 8, side * pair_cols)
    right_mask = both[:, wide : wide + 8].reshape(sources * 8, pair_cols)
    tail = both[:, wide + 8 :]
    mine_left = lax.dynamic_slice_in_dim(tail, core * (per_plane // 2), per_plane // 2, 1)
    left = jnp.concatenate([mine_left, tail[:, per_plane : per_plane + 1]], axis=1)
    left = exchange(repeated(left.transpose(1, 0, 2), chan), "chan")
    left = left.transpose(1, 2, 0, 3).reshape(left.shape[1], sources * chan, 128)
    steps = per_plane // 2
    mid, left_tri, right_tri = outer(
        (row % 4).reshape(1),
        left[:steps],
        left[steps],
        right_all,
        right_mask,
        couple_tensor,
        live_rows[:, None] * live_cols[None, :],
        tensor_exit_coefficients,
        trio_entry_coefficients,
    )
    operands = jnp.stack([left_tri, right_tri]).transpose(2, 0, 1, 3)
    operands = exchange(operands, CHIPS)
    grid = (planes, chan, pair_rows, pair_cols)
    left_tri, right_tri = operands[:, 0].reshape(grid), operands[:, 1].reshape(grid)
    product = triangle(me, left_tri, right_tri, swap(right_tri))
    product = exchange(product.reshape(pair_width, pair_rows, pair_cols), CHIPS)
    pair_result = finish(product, mid, trio_exit_coefficients, trio_exit_switch)
    return (homolog_after_update, pair_result)


def solution(mesh):
    torus = Mesh(
        mesh.devices.reshape(mesh.shape["branch"], 8, 2, mesh.shape["chan"]),
        ("branch", "row_0", "row_1", "chan"),
    )
    return jax.shard_map(
        shards,
        mesh=torus,
        in_specs=(
            P(BRANCH_ROW, "chan", None),
            P(BRANCH_ROW, "chan", None),
            P(),
            P(BRANCH_ROW, "chan"),
            *(P() for _ in range(8)),
        ),
        out_specs=(P(BRANCH_ROW, "chan", None), P(BRANCH_ROW, "chan", None)),
        check_vma=False,
    )
```

time: 581 us -> 329 us (0.57)
  waiting for transfers between devices: 168 us -> 84.1 us
  blocking collectives: 194 us -> 120 us
  matrix products: 75.3 us -> 1.46 us
  Pallas kernels: 0 us -> 61.1 us
  local copies, waits for them, and re-layouts: 77.4 us -> 20.6 us
  between operations: 14.3 us -> 0.91 us
  other arithmetic: 20.5 us -> 9.19 us
    all_gather x3 -> x0, waiting for transfers between devices: 84.5 us -> none  [the longest x1 41.8 us: shards(): lax.all_gather(right_spread, 'chan', axis=1, tiled=True)]
    dot_general x26 -> x0, matrix products: 73.8 us -> none  [the longest x8 24.1 us: row_attention(): jnp.einsum('ihd,jhd->hij', query_rows, key_rows, preferred_element_type=j...]
    pallas_call x0 -> x6, Pallas kernels: none -> 61.1 us  [the longest x1 20.5 us: attend(): pl.pallas_call(functools.partial(attend_kernel, width), grid_spec=pltpu.P...]
    all_to_all x9 -> x4, blocking collectives: 164 us -> 120 us  [exchange(): return lax.all_to_all(x, axes, 0, 0, tiled=True)]
    reshape x8 -> x3, local copies, waits for them, and re-layouts: 40.8 us -> 3.07 us  [the longest x1 1.58 us: shards(): right_all.transpose(0, 2, 1, 3).reshape(sources * 8, side * pair_cols)]
    all_gather x1 -> x0, blocking collectives: 29.9 us -> none  [one_gather(): lines, at, gathered = (lax.all_gather(ravelled, axis), 0, [])]
    all_to_all x15 -> x0, local copies, waits for them, and re-layouts: 14.5 us -> none  [the longest x2 3.4 us: shards(): lax.all_to_all(product.astype(jnp.bfloat16), 'chan', split_axis=2, concat...]
    reduce_sum x16 -> x2, other arithmetic: 14.4 us -> 3.99 us  [the longest x1 2.33 us: standardize(): spread = jnp.mean(centered * centered, axis=axis, keepdims=True)]
  transfers between devices with their start and end apart: 8 -> 8, of which waited for: 8 -> 7; matrix products, arithmetic and copies ran while one was open for 4% -> 3% of each run, Pallas kernels for 0% -> 2%
where the time goes in v1:
time: 329 us; the launch traced here: 326 us
  blocking collectives  120 us (36%)
  waiting for transfers between devices  84.1 us (26%)
  Pallas kernels  61.1 us (19%)
  starting transfers between devices  28.7 us (9%)
  local copies, waits for them, and re-layouts  20.6 us (6%)
  other arithmetic  9.19 us (3%)
    all_to_all x4, blocking collectives, exchange(): return lax.all_to_all(x, axes, 0, 0, tiled=True)  120 us
    all_to_all x5, waiting for transfers between devices, exchange(): return lax.all_to_all(x, axes, 0, 0, tiled=True)  81.2 us
    all_to_all x5, starting transfers between devices, exchange(): return lax.all_to_all(x, axes, 0, 0, tiled=True)  28.6 us
    pallas_call x1, Pallas kernels, attend(): pl.pallas_call(functools.partial(attend_kernel, width), grid_spec=pltpu.P...  20.5 us
    pallas_call x1, Pallas kernels, outer(): pl.pallas_call(functools.partial(outer_kernel, side), grid_spec=pltpu.Pre...  11.1 us
    pallas_call x1, Pallas kernels, finish(): pl.pallas_call(finish_kernel, grid=(pair_rows // rows,), in_specs=[whole(...  8.55 us
    unnamed x38, local copies, waits for them, and re-layouts  8.21 us
    pallas_call x1, Pallas kernels, sides(): pl.pallas_call(functools.partial(sides_kernel, side), grid=(entries,), in...  8.05 us
  transfers between devices with their start and end apart: 8, of which 7 were waited for; matrix products, arithmetic and copies ran while one was open for 3% of the time, Pallas kernels for 2%

profile of v1, /device:TPU:32, one launch (start us, length us, event | category | flops | bytes accessed | tf_op | source)
XLA Modules:
  0.0 326.4 jit_solution(6680932538883181274)
XLA Ops:
  0.7 1.7 convert_reduce_fusion
  2.3 2.3 fusion.2
  4.7 1.5 fusion.4
  6.2 11.7 %all_to_all.45 = bf16[8,32,128]{2,1,0:T(8,128)(2,1)S(1)} all-to-all(bf16[8,32,128]{2,1,0:T(8,128)(2,1)S(1)} %copy.46), channel_id=1, replica_groups=mesh['branch'=2,'row_0'=8,'row_1'=2,'chan'=8] {'chan'}, dimensions={0} | all-to-all | bytes 131072 | tf_op jit(solution)/shard_map/all_to_all | solution.py:382
  17.9 1.2 broadcast_in_dim.10
  19.0 10.8 %all-to-all-start.2 = ((bf16[16,8,32,128]{3,2,1,0:T(8,128)(2,1)}), bf16[16,8,32,128]{3,2,1,0:T(8,128)(2,1)S(1)}, u32[]{:S(2)}, u32[]{:S(2)}) async-start(bf16[16,8,32,128]{3,2,1,0:T(8,128)(2,1)} %broadcast_in_dim.10), calls=%async_computation.2 | async-start | bytes 2097152 | tf_op jit(solution)/shard_map/all_to_all | solution.py:382
  29.8 1.0 copy.45
  30.8 7.2 %project_msa.1 = (bf16[8,8,96,128]{3,2,1,0:T(8,128)(2,1)}, bf16[8,256,128]{2,1,0:T(8,128)(2,1)}) custom-call(bf16[8,128,256]{2,1,0:T(8,128)(2,1)} %stack_ref.1, bf16[1024,256]{1,0:T(8,128)(2,1)} %bitcast.61), custom_call_target="tpu_custom_call" | custom-call | tf_op jit(solution)/shard_map/project_msa/pallas_call | solution.py:62
  38.0 18.3 %all-to-all-done.2.mine_ref = bf16[16,8,32,128]{3,2,1,0:T(8,128)(2,1)S(1)} async-done(((bf16[16,8,32,128]{3,2,1,0:T(8,128)(2,1)}), bf16[16,8,32,128]{3,2,1,0:T(8,128)(2,1)S(1)}, u32[]{:S(2)}, u32[]{:S(2)}) %all-to-all-start.2) | async-done | bytes 1048608 | tf_op jit(solution)/shard_map/all_to_all | solution.py:382
  56.2 3.6 %all-to-all-start = ((bf16[8,8,96,128]{3,2,1,0:T(8,128)(2,1)}), bf16[8,8,96,128]{3,2,1,0:T(8,128)(2,1)S(1)}, u32[]{:S(2)}, u32[]{:S(2)}) async-start(bf16[8,8,96,128]{3,2,1,0:T(8,128)(2,1)} %get-tuple-element.10), calls=%async_computation | async-start | bytes 3145728 | tf_op jit(solution)/shard_map/all_to_all | solution.py:382
  60.5 16.4 %all-to-all-done.qkv_ref = bf16[8,8,96,128]{3,2,1,0:T(8,128)(2,1)S(1)} async-done(((bf16[8,8,96,128]{3,2,1,0:T(8,128)(2,1)}), bf16[8,8,96,128]{3,2,1,0:T(8,128)(2,1)S(1)}, u32[]{:S(2)}, u32[]{:S(2)}) %all-to-all-start) | async-done | bytes 1572896 | tf_op jit(solution)/shard_map/all_to_all | solution.py:382
  76.9 1.2 copy-done.2
  78.1 20.5 %attend.1 = bf16[8,8,32,128]{3,2,1,0:T(8,128)(2,1)} custom-call(s32[1]{0:T(128)} %bitcast.me_ref, bf16[8,8,96,128]{3,2,1,0:T(8,128)(2,1)} %copy-done.2, bf16[16,8,32,128]{3,2,1,0:T(8,128)(2,1)} %copy-done.3, bf16[16,8,32,128]{3,2,1,0:T(8,128)(2,1)} %collective-permute-done.other_ref, f32[1,1024]{1,0:T(1,128)} %bitcast.75), custom_call_target="tpu_custom_call" | custom-call | tf_op jit(solution)/shard_map/attend/pallas_call | solution.py:117
  98.6 3.6 %all-to-all-start.3 = ((bf16[8,8,32,128]{3,2,1,0:T(8,128)(2,1)}), bf16[8,8,32,128]{3,2,1,0:T(8,128)(2,1)S(1)}, u32[]{:S(2)}, u32[]{:S(2)}) async-start(bf16[8,8,32,128]{3,2,1,0:T(8,128)(2,1)} %attend.1), calls=%async_computation.3 | async-start | bytes 1048576 | tf_op jit(solution)/shard_map/all_to_all | solution.py:382
  102.8 0.6 slice_bitcast_fusion.2
  103.4 0.7 copy.47.wl_ref
  104.1 7.6 %all-to-all-done.3.att_ref = bf16[8,8,32,128]{3,2,1,0:T(8,128)(2,1)S(1)} async-done(((bf16[8,8,32,128]{3,2,1,0:T(8,128)(2,1)}), bf16[8,8,32,128]{3,2,1,0:T(8,128)(2,1)S(1)}, u32[]{:S(2)}, u32[]{:S(2)}) %all-to-all-start.3) | async-done | bytes 524320 | tf_op jit(solution)/shard_map/all_to_all | solution.py:382
  111.7 0.8 copy-done.6
  112.5 8.0 %sides.1 = (bf16[8,128,256]{2,1,0:T(8,128)(2,1)}, bf16[8,48,128]{2,1,0:T(8,128)(2,1)}, bf16[264,128]{1,0:T(8,128)(2,1)}) custom-call(bf16[8,8,32,128]{3,2,1,0:T(8,128)(2,1)} %copy-done.6, bf16[8,256,128]{2,1,0:T(8,128)(2,1)} %get-tuple-element.11.gate_ref, bf16[8,128,256]{2,1,0:T(8,128)(2,1)} %stack_ref.1, f32[8,1,128]{2,1,0:T(1,128)} %bitcast.74, ...), custom_call_target="tpu_custom_call" | custom-call | tf_op jit(solution)/shard_map/sides/pallas_call | solution.py:169
  120.5 9.7 %all_to_all.46 = bf16[8,48,128]{2,1,0:T(8,128)(2,1)S(1)} all-to-all(bf16[8,48,128]{2,1,0:T(8,128)(2,1)} %get-tuple-element.14), channel_id=1, replica_groups=mesh['branch'=2,'row_0'=8,'row_1'=2,'chan'=8] {'chan'}, dimensions={0} | all-to-all | bytes 196608 | tf_op jit(solution)/shard_map/all_to_all | solution.py:382
  130.3 1.0 broadcast_in_dim.12
  131.4 38.8 %all_to_all.47 = bf16[16,288,128]{2,1,0:T(8,128)(2,1)S(1)} all-to-all(bf16[16,288,128]{2,1,0:T(8,128)(2,1)S(1)} %pad_maximum_fusion.1), channel_id=1, replica_groups=mesh['branch'=2,'row_0'=8,'row_1'=2,'chan'=8] {'branch','row_0'}, dimensions={0} | all-to-all | bytes 2359296 | tf_op jit(solution)/shard_map/all_to_all | solution.py:382
  170.5 0.9 copy.53.we_ref
  171.3 0.7 copy.52
  172.1 0.7 broadcast_multiply_fusion.live_ref
  173.0 1.0 copy-done.7
  174.1 1.5 pad_maximum_fusion
  175.7 0.9 broadcast_in_dim.14
  176.6 3.5 %all-to-all-start.6 = ((bf16[8,9,32,128]{3,2,1,0:T(8,128)(2,1)}), bf16[8,9,32,128]{3,2,1,0:T(8,128)(2,1)S(1)}, u32[]{:S(2)}, u32[]{:S(2)}) async-start(bf16[8,9,32,128]{3,2,1,0:T(8,128)(2,1)} %broadcast_in_dim.14), calls=%async_computation.6 | async-start | bytes 1179648 | tf_op jit(solution)/shard_map/all_to_all | solution.py:382
  180.1 1.6 slice_bitcast_fusion.right_ref
  181.7 0.6 slice_bitcast_fusion.1.rmask_ref
  182.4 8.4 %all-to-all-done.6 = bf16[8,9,32,128]{3,2,1,0:T(8,128)(2,1)S(1)} async-done(((bf16[8,9,32,128]{3,2,1,0:T(8,128)(2,1)}), bf16[8,9,32,128]{3,2,1,0:T(8,128)(2,1)S(1)}, u32[]{:S(2)}, u32[]{:S(2)}) %all-to-all-start.6) | async-done | bytes 589856 | tf_op jit(solution)/shard_map/all_to_all | solution.py:382
  190.8 1.1 copy.59
  191.9 0.6 copy.60
  192.6 11.1 %outer.1 = (f32[32,128,128]{2,1,0:T(8,128)}, bf16[32,128,128]{2,1,0:T(8,128)(2,1)}, bf16[32,128,128]{2,1,0:T(8,128)(2,1)}) custom-call(s32[1]{0:T(128)} %bitcast.8.at_ref, bf16[8,256,128]{2,1,0:T(8,128)(2,1)} %bitcast.60, bf16[256,128]{1,0:T(8,128)(2,1)} %bitcast.67, bf16[256,4096]{1,0:T(8,128)(2,1)} %slice_bitcast_fusion.right_ref, ...), custom_call_target="tpu_custom_call" | custom-call | tf_op jit(solution)/shard_map/outer/pallas_call | solution.py:252
  203.7 1.7 maximum_bitcast_fusion
  205.4 1.4 copy.54
  206.8 60.2 %all_to_all.48 = bf16[128,2,32,128]{3,2,1,0:T(8,128)(2,1)S(1)} all-to-all(bf16[128,2,32,128]{3,2,1,0:T(8,128)(2,1)S(1)} %copy.54), channel_id=1, replica_groups=mesh['branch'=2,'row_0'=8,'row_1'=2,'chan'=8] {'branch','row_0','chan'}, dimensions={0} | all-to-all | bytes 4194304 | tf_op jit(solution)/shard_map/all_to_all | solution.py:382
  267.0 1.3 fusion.9
  268.3 2.7 collective-permute-done.2.other_ref
  271.0 1.0 copy-done.8
  272.0 5.8 %triangle.1 = bf16[16,8,32,128]{3,2,1,0:T(8,128)(2,1)} custom-call(s32[1]{0:T(128)} %bitcast.me_ref, bf16[16,8,32,128]{3,2,1,0:T(8,128)(2,1)} %bitcast.57, bf16[16,8,32,128]{3,2,1,0:T(8,128)(2,1)} %bitcast.56, bf16[16,8,32,128]{3,2,1,0:T(8,128)(2,1)} %copy-done.8), custom_call_target="tpu_custom_call" | custom-call | tf_op jit(solution)/shard_map/triangle/pallas_call | solution.py:308
  277.8 7.1 %all-to-all-start.8 = ((bf16[128,32,128]{2,1,0:T(8,128)(2,1)}), bf16[128,32,128]{2,1,0:T(8,128)(2,1)S(1)}, u32[]{:S(2)}, u32[]{:S(2)}) async-start(bf16[128,32,128]{2,1,0:T(8,128)(2,1)} %bitcast.54), calls=%async_computation.8 | async-start | bytes 2097152 | tf_op jit(solution)/shard_map/all_to_all | solution.py:382
  284.9 0.7 copy.55
  285.6 0.7 copy.56
  286.3 30.6 %all-to-all-done.8.prod_ref = bf16[128,32,128]{2,1,0:T(8,128)(2,1)S(1)} async-done(((bf16[128,32,128]{2,1,0:T(8,128)(2,1)}), bf16[128,32,128]{2,1,0:T(8,128)(2,1)S(1)}, u32[]{:S(2)}, u32[]{:S(2)}) %all-to-all-start.8) | async-done | bytes 1048608 | tf_op jit(solution)/shard_map/all_to_all | solution.py:382
  316.9 1.0 copy-done.5
  317.9 8.5 %finish.1 = bf16[32,128,128]{2,1,0:T(8,128)(2,1)} custom-call(bf16[128,32,128]{2,1,0:T(8,128)(2,1)} %copy-done.5, f32[32,128,128]{2,1,0:T(8,128)} %get-tuple-element.17.mid_ref, bf16[128,128]{1,0:T(8,128)(2,1)} %bitcast.71, bf16[128,128]{1,0:T(8,128)(2,1)} %bitcast.72), custom_call_target="tpu_custom_call" | custom-call | tf_op jit(solution)/shard_map/finish/pallas_call | solution.py:360
  (55 shorter events, 2.2 us)
Async XLA Ops:
  0.6 4.1 %copy-start = (bf16[128,8]{0,1:T(8,128)(2,1)S(1)}, bf16[128,8]{0,1:T(8,128)(2,1)}, u32[]{:S(2)}) copy-start(bf16[128,8]{0,1:T(8,128)(2,1)} %param.17) | copy-start | bytes 6148
  0.6 4.1 %copy-start.1 = (bf16[32,128,128]{2,1,0:T(8,128)(2,1)S(1)}, bf16[32,128,128]{2,1,0:T(8,128)(2,1)}, u32[]{:S(2)}) copy-start(bf16[32,128,128]{2,1,0:T(8,128)(2,1)} %couple_ref.1) | copy-start | bytes 3145732
  6.2 23.6 %copy-start.9 = (bf16[256,1024]{1,0:T(8,128)(2,1)S(1)}, bf16[256,1024]{1,0:T(8,128)(2,1)}, u32[]{:S(2)}) copy-start(bf16[256,1024]{1,0:T(8,128)(2,1)} %param.16) | copy-start | bytes 1572868
  19.0 37.2 %all-to-all-start.2 = ((bf16[16,8,32,128]{3,2,1,0:T(8,128)(2,1)}), bf16[16,8,32,128]{3,2,1,0:T(8,128)(2,1)S(1)}, u32[]{:S(2)}, u32[]{:S(2)}) async-start(bf16[16,8,32,128]{3,2,1,0:T(8,128)(2,1)} %broadcast_in_dim.10), calls=%async_computation.2 | async-start | bytes 2097152 | tf_op jit(solution)/shard_map/all_to_all | solution.py:382
  30.8 29.1 %copy-start.15 = (s32[1024]{0:T(1024)S(1)}, s32[1024]{0:T(1024)}, u32[]{:S(2)}) copy-start(s32[1024]{0:T(1024)} %param.14) | copy-start | bytes 12292
  56.2 20.7 %copy-start.3 = (bf16[16,8,32,128]{3,2,1,0:T(8,128)(2,1)}, bf16[16,8,32,128]{3,2,1,0:T(8,128)(2,1)S(1)}, u32[]{:S(2)}) copy-start(bf16[16,8,32,128]{3,2,1,0:T(8,128)(2,1)S(1)} %all-to-all-done.2.mine_ref) | copy-start | bytes 3145732
  56.2 20.7 %all-to-all-start = ((bf16[8,8,96,128]{3,2,1,0:T(8,128)(2,1)}), bf16[8,8,96,128]{3,2,1,0:T(8,128)(2,1)S(1)}, u32[]{:S(2)}, u32[]{:S(2)}) async-start(bf16[8,8,96,128]{3,2,1,0:T(8,128)(2,1)} %get-tuple-element.10), calls=%async_computation | async-start | bytes 3145728 | tf_op jit(solution)/shard_map/all_to_all | solution.py:382
  59.8 17.1 %collective-permute-start = (bf16[16,8,32,128]{3,2,1,0:T(8,128)(2,1)S(1)}, bf16[16,8,32,128]{3,2,1,0:T(8,128)(2,1)}, u32[]{:S(2)}, u32[]{:S(2)}) collective-permute-start(bf16[16,8,32,128]{3,2,1,0:T(8,128)(2,1)S(1)} %all-to-all-done.2.mine_ref), channel_id=1, source_target_pairs={{0,8},{8,0},{1,9},{9,1},{2,10},{10,2},{3,11},{11,3},{4,12},{12,4},... | collective-permute-start | bytes 3145736 | tf_op jit(solution)/shard_map/ppermute | solution.py:378
  76.9 1.2 copy-start.2
  78.1 24.1 %copy-start.16 = (s32[8,128]{1,0:T(8,128)S(1)}, s32[8,128]{1,0:T(8,128)}, u32[]{:S(2)}) copy-start(s32[8,128]{1,0:T(8,128)} %param.15) | copy-start | bytes 12292
  78.1 24.7 %copy-start.12 = (bf16[256,64]{0,1:T(8,128)(2,1)S(1)}, bf16[256,64]{0,1:T(8,128)(2,1)}, u32[]{:S(2)}) copy-start(bf16[256,64]{0,1:T(8,128)(2,1)} %param.19) | copy-start | bytes 98308
  98.6 13.1 %all-to-all-start.3 = ((bf16[8,8,32,128]{3,2,1,0:T(8,128)(2,1)}), bf16[8,8,32,128]{3,2,1,0:T(8,128)(2,1)S(1)}, u32[]{:S(2)}, u32[]{:S(2)}) async-start(bf16[8,8,32,128]{3,2,1,0:T(8,128)(2,1)} %attend.1), calls=%async_computation.3 | async-start | bytes 1048576 | tf_op jit(solution)/shard_map/all_to_all | solution.py:382
  111.7 0.8 copy-start.6
  131.3 39.0 %copy-start.10 = (bf16[1024,128]{1,0:T(8,128)(2,1)S(1)}, bf16[1024,128]{1,0:T(8,128)(2,1)}, u32[]{:S(2)}) copy-start(bf16[1024,128]{1,0:T(8,128)(2,1)} %param.20) | copy-start | bytes 786436
  131.4 39.9 %copy-start.11 = (bf16[128,512]{1,0:T(8,128)(2,1)S(1)}, bf16[128,512]{1,0:T(8,128)(2,1)}, u32[]{:S(2)}) copy-start(bf16[128,512]{1,0:T(8,128)(2,1)} %param.21) | copy-start | bytes 393220
  170.2 2.8 collective-permute-start.1
  173.0 1.0 copy-start.7
  176.6 14.1 %all-to-all-start.6 = ((bf16[8,9,32,128]{3,2,1,0:T(8,128)(2,1)}), bf16[8,9,32,128]{3,2,1,0:T(8,128)(2,1)S(1)}, u32[]{:S(2)}, u32[]{:S(2)}) async-start(bf16[8,9,32,128]{3,2,1,0:T(8,128)(2,1)} %broadcast_in_dim.14), calls=%async_computation.6 | async-start | bytes 1179648 | tf_op jit(solution)/shard_map/all_to_all | solution.py:382
  268.3 2.7 copy-start.4
  268.3 2.7 collective-permute-start.2
  271.0 1.0 copy-start.8
  277.8 7.1 %copy-start.13 = (bf16[128,128]{1,0:T(8,128)(2,1)S(1)}, bf16[128,128]{1,0:T(8,128)(2,1)}, u32[]{:S(2)}) copy-start(bf16[128,128]{1,0:T(8,128)(2,1)} %param.23) | copy-start | bytes 98308
  277.8 7.8 %copy-start.14 = (bf16[128,128]{1,0:T(8,128)(2,1)S(1)}, bf16[128,128]{1,0:T(8,128)(2,1)}, u32[]{:S(2)}) copy-start(bf16[128,128]{1,0:T(8,128)(2,1)} %param.22) | copy-start | bytes 98308
  277.8 39.1 %all-to-all-start.8 = ((bf16[128,32,128]{2,1,0:T(8,128)(2,1)}), bf16[128,32,128]{2,1,0:T(8,128)(2,1)S(1)}, u32[]{:S(2)}, u32[]{:S(2)}) async-start(bf16[128,32,128]{2,1,0:T(8,128)(2,1)} %bitcast.54), calls=%async_computation.8 | async-start | bytes 2097152 | tf_op jit(solution)/shard_map/all_to_all | solution.py:382
  316.9 1.0 copy-start.5

commit v2 on v1

--- a/solution.py
+++ b/solution.py
@@ -8,8 +8,8 @@
 from jax.sharding import Mesh
 from jax.sharding import PartitionSpec as P
 
+
 BRANCH_ROW = ("branch", "row_0", "row_1")
-PLANES = ("branch", "row_0")
 CHIPS = ("branch", "row_0", "chan")
 SWAP = ((0, 1), (1, 0))
 EPSILON = 1e-05
@@ -79,18 +79,21 @@
     )(stack, weights.T)
 
 
-def attend_kernel(width, me_ref, qkv_ref, mine_ref, other_ref, pen_ref, out_ref, bias_ref):
+def attend_kernel(width, at_ref, qkv_ref, mine_ref, other_ref, pen_ref, out_ref, bias_ref):
     block = pl.program_id(0)
     columns, entries = qkv_ref.shape[0], qkv_ref.shape[1]
     lanes = qkv_ref.shape[3]
-    tile = mine_ref.shape[2]
-    first = me_ref[0] == 0
-    for plane in range(mine_ref.shape[0]):
+    length, _, _, tile, _ = mine_ref.shape
+    first = at_ref[0] == 0
+    for q in range(lanes // (2 * tile)):
+        plane = block * (lanes // (2 * tile)) + q
+        place = ring_place((plane + 2 * length - at_ref[2]) % length, length)
+        side = jnp.bitwise_xor(plane // length, at_ref[1])
         for j in range(columns):
-            a = mine_ref[plane, j].astype(F32)
-            b = other_ref[plane, j].astype(F32)
+            a = mine_ref[place, side, j].astype(F32)
+            b = other_ref[place, side, j].astype(F32)
             pen = pen_ref[:, j * lanes : (j + 1) * lanes]
-            row = plane * 2 * tile
+            row = q * 2 * tile
             at = slice(j * lanes, (j + 1) * lanes)
             bias_ref[row : row + tile, at] = (jnp.where(first, a, b) + pen) * LOG2E
             bias_ref[row + tile : row + 2 * tile, at] = (jnp.where(first, b, a) + pen) * LOG2E
@@ -109,24 +112,21 @@
         out_ref[0, s] = (blended[:width] * (1.0 / blended[width : width + 1])).astype(BF16)
 
 
-def attend(me, qkv, mine, other, pen, width):
+def attend(at, qkv, mine, other, pen, width):
     columns, entries, _, lanes = qkv.shape
-    planes, _, tile, _ = mine.shape
-    per = lanes // (2 * tile)
-    bias_spec = pl.BlockSpec((per, columns, tile, lanes), lambda b, me: (b, 0, 0, 0))
     return pl.pallas_call(
         functools.partial(attend_kernel, width),
         grid_spec=pltpu.PrefetchScalarGridSpec(
             num_scalar_prefetch=1,
             grid=(columns,),
-            in_specs=[whole(qkv.shape), bias_spec, bias_spec, whole(pen.shape)],
-            out_specs=pl.BlockSpec((1, entries, width, lanes), lambda b, me: (b, 0, 0, 0)),
+            in_specs=[whole(qkv.shape), whole(mine.shape), whole(other.shape), whole(pen.shape)],
+            out_specs=pl.BlockSpec((1, entries, width, lanes), lambda b, at: (b, 0, 0, 0)),
             scratch_shapes=[pltpu.VMEM((lanes, columns * lanes), F32)],
         ),
         out_shape=jax.ShapeDtypeStruct((columns, entries, width, lanes), BF16),
         compiler_params=params(),
         name="attend",
-    )(me, qkv, mine, other, pen)
+    )(at, qkv, mine, other, pen)
 
 
 def sides_kernel(
@@ -203,8 +203,8 @@
 
 
 def outer_kernel(
-    side, at_ref, left_ref, lmask_ref, right_ref, rmask_ref, couple_ref, live_ref, we_ref, wt_ref,
-    mid_ref, l_ref, r_ref, x_ref, count_ref,
+    side, at_ref, left_ref, lmask_ref, mine_ref, other_ref, couple_ref, live_ref, we_ref, wt_ref,
+    mid_ref, l_ref, r_ref, right_ref, rmask_ref, x_ref, count_ref,
 ):
     step = pl.program_id(0)
     rows, lanes = couple_ref.shape[0], couple_ref.shape[1]
@@ -212,6 +212,19 @@
 
     @pl.when(step == 0)
     def _():
+        length, branches = mine_ref.shape[0], mine_ref.shape[1]
+        for branch in range(branches):
+            for z in range(length):
+                place = ring_place((z + length - at_ref[2]) % length, length)
+                which = jnp.bitwise_xor(branch, at_ref[1])
+                row = (branch * length + z) * 16
+                for d in range(side + 1):
+                    pair = [ref[place, which, d * 8 : (d + 1) * 8] for ref in (mine_ref, other_ref)]
+                    pair = jnp.concatenate(pair, axis=0)
+                    if d < side:
+                        right_ref[row : row + 16, d * lanes : (d + 1) * lanes] = pair
+                    else:
+                        rmask_ref[row : row + 16, :] = pair
         count_ref[...] = 1.0 / (dot(lmask_ref[...], rmask_ref[...], (0, 0)) + 1.0)
 
     wide = 8 * lanes
@@ -228,7 +241,7 @@
     update = dot(we_ref[...], x_ref[...], (1, 0))
     normed = []
     for i in range(rows):
-        over = count_ref[pl.ds(at_ref[0] * 32 + step * rows + i, 1), :]
+        over = count_ref[pl.ds(at_ref[3] * 32 + step * rows + i, 1), :]
         mid = couple_ref[i].astype(F32).T + update[:, i * lanes : (i + 1) * lanes] * over
         mid_ref[i] = mid
         normed.append(standardize(mid, 0).astype(BF16))
@@ -242,11 +255,11 @@
             ref[i] = (both[:, i * lanes : (i + 1) * lanes] * live).astype(BF16)
 
 
-def outer(at, left, lmask, right, rmask, couple, live, w_exit, w_tri):
+def outer(at, left, lmask, mine, other, couple, live, w_exit, w_tri):
     steps, entries, _ = left.shape
     pair_rows, lanes, channels = couple.shape
     rows = pair_rows // steps
-    side = right.shape[1] // lanes
+    side = mine.shape[2] // 8 - 1
     tile = pl.BlockSpec((rows, channels, lanes), lambda t, at: (t, 0, 0))
     w_exit = w_exit.reshape(side, side, channels).transpose(2, 1, 0).reshape(channels, side * side)
     return pl.pallas_call(
@@ -257,8 +270,8 @@
             in_specs=[
                 pl.BlockSpec((1, entries, 128), lambda t, at: (t, 0, 0)),
                 whole(lmask.shape),
-                whole(right.shape),
-                whole(rmask.shape),
+                whole(mine.shape),
+                whole(other.shape),
                 pl.BlockSpec((rows, lanes, channels), lambda t, at: (t, 0, 0)),
                 whole(live.shape),
                 whole(w_exit.shape),
@@ -266,6 +279,8 @@
             ],
             out_specs=[tile, tile, tile],
             scratch_shapes=[
+                pltpu.VMEM((entries, side * lanes), BF16),
+                pltpu.VMEM((entries, lanes), BF16),
                 pltpu.VMEM((side * side, rows * lanes), BF16),
                 pltpu.VMEM((128, lanes), F32),
             ],
@@ -277,7 +292,7 @@
         ],
         compiler_params=params(),
         name="outer",
-    )(at, left, lmask, right, rmask, couple, live, w_exit, w_tri.T)
+    )(at, left, lmask, mine, other, couple, live, w_exit, w_tri.T)
 
 
 def triangle_kernel(me_ref, l_ref, mine_ref, other_ref, out_ref):
@@ -382,6 +397,25 @@
     return lax.all_to_all(x, axes, 0, 0, tiled=True)
 
 
+def ring_gather(x):
+    n = lax.axis_size("row_0")
+    up = tuple((k, (k + 1) % n) for k in range(n))
+    down = tuple((k, (k - 1) % n) for k in range(n))
+    pair = jnp.stack([x, lax.ppermute(x, "branch", SWAP)])
+    places, above, below = [pair], pair, pair
+    for _ in range(n // 2 - 1):
+        above = lax.ppermute(above, "row_0", up)
+        below = lax.ppermute(below, "row_0", down)
+        places += [above, below]
+    last = [lax.ppermute(above[:1], "row_0", up), lax.ppermute(below[1:], "row_0", down)]
+    places.append(jnp.concatenate(last))
+    return jnp.stack(places)
+
+
+def ring_place(ahead, n):
+    return jnp.where(ahead <= n // 2, jnp.maximum(2 * ahead - (ahead == n // 2), 0), 2 * (n - ahead) - 1)
+
+
 def repeated(x, n):
     return jnp.broadcast_to(x[None], (n, *x.shape))
 
@@ -400,7 +434,7 @@
     trio_exit_switch,
     trio_exit_coefficients,
 ):
-    entries, residues, features = homolog_stack.shape
+    _, residues, features = homolog_stack.shape
     pair_rows, pair_cols, pair_width = couple_tensor.shape
     heads = couple_offset_coefficients.shape[1]
     width = features // heads
@@ -409,6 +443,8 @@
     chan = lax.axis_size("chan")
     core = lax.axis_index("row_1").astype(jnp.int32)
     row = lax.axis_index(BRANCH_ROW).astype(jnp.int32)
+    place = [core, lax.axis_index("branch"), lax.axis_index("row_0"), row % 4]
+    at = jnp.stack([p.astype(jnp.int32) for p in place])
     me = core.reshape(1)
     live = amino_occupancy.astype(F32)
     live_rows = lax.dynamic_slice_in_dim(live, row * pair_rows, pair_rows)
@@ -420,12 +456,12 @@
         "ijc,ch->hij", pair_norm, couple_offset_coefficients, preferred_element_type=F32
     ).astype(BF16)
     bias = exchange(bias, "chan")
-    bias = exchange(repeated(bias, planes), PLANES)
+    bias = ring_gather(bias)
     bias_other = swap(bias)
 
     qkv, gate = project_msa(homolog_stack, focus_entry_coefficients, heads)
     qkv = exchange(qkv, "chan")
-    attended = attend(me, qkv, bias, bias_other, penalty, width)
+    attended = attend(at, qkv, bias, bias_other, penalty, width)
     attended = exchange(attended, "chan")
 
     homolog_after_update, left, right = sides(
@@ -436,37 +472,30 @@
         focus_exit_coefficients,
         tensor_entry_coefficients,
     )
+    right = ring_gather(right)
+    right_other = swap(right)
     left = exchange(left, "chan")
+    members = 2 * planes
     packed_rows = residues * side // 128
-    per_plane = left.shape[0] * packed_rows // planes
-    parts = jnp.concatenate(
+    steps = chan * packed_rows // members
+    left = jnp.concatenate(
         [
-            repeated(right, planes),
-            left[:, :packed_rows].reshape(planes, per_plane, 128),
-            jnp.repeat(left[:, packed_rows : packed_rows + 8], planes // chan, axis=0),
+            left[:, :packed_rows].reshape(members, steps, 128),
+            jnp.repeat(left[:, packed_rows : packed_rows + 8], members // chan, axis=0),
         ],
         axis=1,
     )
-    mine = exchange(parts, PLANES)
-    other = swap(mine)
-    both = jnp.stack([mine, other]).reshape(2 * planes, *mine.shape[1:])
-    sources = 2 * planes
-    wide = side * 8
-    right_all = both[:, :wide].reshape(sources, side, 8, pair_cols)
-    right_all = right_all.transpose(0, 2, 1, 3).reshape(sources * 8, side * pair_cols)
-    right_mask = both[:, wide : wide + 8].reshape(sources * 8, pair_cols)
-    tail = both[:, wide + 8 :]
-    mine_left = lax.dynamic_slice_in_dim(tail, core * (per_plane // 2), per_plane // 2, 1)
-    left = jnp.concatenate([mine_left, tail[:, per_plane : per_plane + 1]], axis=1)
+    left = exchange(left, BRANCH_ROW)
+    left = left[:, : steps + 1].reshape(planes, 2, steps + 1, 128)
+    left = jnp.where(core == 0, left, left[:, ::-1]).reshape(members, steps + 1, 128)
     left = exchange(repeated(left.transpose(1, 0, 2), chan), "chan")
-    left = left.transpose(1, 2, 0, 3).reshape(left.shape[1], sources * chan, 128)
-    steps = per_plane // 2
+    left = left.transpose(1, 2, 0, 3).reshape(steps + 1, members * chan, 128)
     mid, left_tri, right_tri = outer(
-        (row % 4).reshape(1),
+        at,
         left[:steps],
         left[steps],
-        right_all,
-        right_mask,
+        right,
+        right_other,
         couple_tensor,
         live_rows[:, None] * live_cols[None, :],
         tensor_exit_coefficients,
@@ -487,6 +516,7 @@
         mesh.devices.reshape(mesh.shape["branch"], 8, 2, mesh.shape["chan"]),
         ("branch", "row_0", "row_1", "chan"),
     )
+
     return jax.shard_map(
         shards,
         mesh=torus,

time: 329 us -> 330 us (level)
  blocking collectives: 120 us -> 72.1 us
  starting transfers between devices: 28.7 us -> 67.9 us
  waiting for transfers between devices: 84.1 us -> 96.5 us
  local copies, waits for them, and re-layouts: 20.6 us -> 15.2 us
    all_to_all x4 -> x2, blocking collectives: 120 us -> 72.1 us  [exchange(): return lax.all_to_all(x, axes, 0, 0, tiled=True)]
    ppermute x0 -> x18, waiting for transfers between devices: none -> 33.2 us  [the longest x6 17.2 us: ring_gather(): below = lax.ppermute(below, 'row_0', down)]
    ppermute x0 -> x18, starting transfers between devices: none -> 31.3 us  [the longest x6 14.2 us: ring_gather(): above = lax.ppermute(above, 'row_0', up)]
    all_to_all x5 -> x6, waiting for transfers between devices: 81.2 us -> 59.3 us  [exchange(): return lax.all_to_all(x, axes, 0, 0, tiled=True)]
    all_to_all x5 -> x6, starting transfers between devices: 28.6 us -> 36.5 us  [exchange(): return lax.all_to_all(x, axes, 0, 0, tiled=True)]
    unnamed x38 -> x52, local copies, waits for them, and re-layouts: 8.21 us -> 7.23 us
  transfers between devices with their start and end apart: 8 -> 27, of which waited for: 7 -> 20; matrix products, arithmetic and copies ran while one was open for 3% -> 4% of each run, Pallas kernels for 2% -> 2%
where the time goes in v2:
time: 330 us; the launch traced here: 328 us
  waiting for transfers between devices  96.5 us (29%)
  blocking collectives  72.1 us (22%)
  starting transfers between devices  67.9 us (21%)
  Pallas kernels  63.4 us (19%)
  local copies, waits for them, and re-layouts  15.2 us (5%)
  other arithmetic  10.1 us (3%)
    all_to_all x2, blocking collectives, exchange(): return lax.all_to_all(x, axes, 0, 0, tiled=True)  72.1 us
    all_to_all x6, waiting for transfers between devices, exchange(): return lax.all_to_all(x, axes, 0, 0, tiled=True)  59.3 us
    all_to_all x6, starting transfers between devices, exchange(): return lax.all_to_all(x, axes, 0, 0, tiled=True)  36.5 us
    pallas_call x1, Pallas kernels, attend(): pl.pallas_call(functools.partial(attend_kernel, width), grid_spec=pltpu.P...  21.8 us
    ppermute x6, waiting for transfers between devices, ring_gather(): below = lax.ppermute(below, 'row_0', down)  17.2 us
    ppermute x6, starting transfers between devices, ring_gather(): above = lax.ppermute(above, 'row_0', up)  14.2 us
    pallas_call x1, Pallas kernels, outer(): pl.pallas_call(functools.partial(outer_kernel, side), grid_spec=pltpu.Pre...  12.2 us
    pallas_call x1, Pallas kernels, finish(): pl.pallas_call(finish_kernel, grid=(pair_rows // rows,), in_specs=[whole(...  8.55 us
  transfers between devices with their start and end apart: 27, of which 20 were waited for; matrix products, arithmetic and copies ran while one was open for 4% of the time, Pallas kernels for 2%

profile of v2, /device:TPU:32, one launch (start us, length us, event | category | flops | bytes accessed | tf_op | source)
XLA Modules:
  0.0 327.7 jit_solution(17681862402881770134)
XLA Ops:
  0.7 1.7 convert_reduce_fusion
  3.7 1.5 fusion.4
  5.2 11.5 %all_to_all.40 = bf16[8,32,128]{2,1,0:T(8,128)(2,1)S(1)} all-to-all(bf16[8,32,128]{2,1,0:T(8,128)(2,1)S(1)} %bitcast.107), channel_id=1, replica_groups=mesh['branch'=2,'row_0'=8,'row_1'=2,'chan'=8] {'chan'}, dimensions={0} | all-to-all | bytes 131072 | tf_op jit(solution)/shard_map/all_to_all | solution.py:397
  16.7 2.7 collective-permute-start
  19.4 3.0 collective-permute-done
  22.5 2.0 collective-permute-start.1
  25.5 7.2 %project_msa.1 = (bf16[8,8,96,128]{3,2,1,0:T(8,128)(2,1)}, bf16[8,256,128]{2,1,0:T(8,128)(2,1)}) custom-call(bf16[8,128,256]{2,1,0:T(8,128)(2,1)} %stack_ref.1, bf16[1024,256]{1,0:T(8,128)(2,1)} %bitcast.91), custom_call_target="tpu_custom_call" | custom-call | tf_op jit(solution)/shard_map/project_msa/pallas_call | solution.py:62
  32.7 3.6 %all-to-all-start = ((bf16[8,8,96,128]{3,2,1,0:T(8,128)(2,1)}), bf16[8,8,96,128]{3,2,1,0:T(8,128)(2,1)S(1)}, u32[]{:S(2)}, u32[]{:S(2)}) async-start(bf16[8,8,96,128]{3,2,1,0:T(8,128)(2,1)} %get-tuple-element.10), calls=%async_computation | async-start | bytes 3145728 | tf_op jit(solution)/shard_map/all_to_all | solution.py:397
  36.5 2.0 collective-permute-start.3
  38.5 2.8 collective-permute-done.2
  41.3 1.7 collective-permute-start.4
  44.6 3.5 %collective-permute-done.4 = bf16[2,8,32,128]{3,2,1,0:T(8,128)(2,1)S(1)} collective-permute-done((bf16[2,8,32,128]{3,2,1,0:T(8,128)(2,1)S(1)}, bf16[2,8,32,128]{3,2,1,0:T(8,128)(2,1)S(1)}, u32[]{:S(2)}, u32[]{:S(2)}) %collective-permute-start.4) | collective-permute-done | bytes 131104 | tf_op jit(solution)/shard_map/ppermute | solution.py:408
  48.0 2.1 collective-permute-start.6
  50.1 5.2 %collective-permute-done.6 = bf16[2,8,32,128]{3,2,1,0:T(8,128)(2,1)S(1)} collective-permute-done((bf16[2,8,32,128]{3,2,1,0:T(8,128)(2,1)S(1)}, bf16[2,8,32,128]{3,2,1,0:T(8,128)(2,1)S(1)}, u32[]{:S(2)}, u32[]{:S(2)}) %collective-permute-start.6) | collective-permute-done | bytes 131104 | tf_op jit(solution)/shard_map/ppermute | solution.py:408
  56.6 2.1 collective-permute-start.7
  58.8 2.1 collective-permute-done.8
  60.9 1.8 collective-permute-done.7
  64.2 1.4 collective-permute-done.9.other_ref
  65.6 21.8 %attend.1 = bf16[8,8,32,128]{3,2,1,0:T(8,128)(2,1)} custom-call(s32[4]{0:T(128)} %pad_add_fusion.at_ref, bf16[8,8,96,128]{3,2,1,0:T(8,128)(2,1)} %copy-done.2, bf16[8,2,8,32,128]{4,3,2,1,0:T(8,128)(2,1)} %copy-done.7, bf16[8,2,8,32,128]{4,3,2,1,0:T(8,128)(2,1)} %collective-permute-done.9.other_ref, f32[1,1024]{1,0:T(1,128)} %bitcast.115), custom_call_target="tpu_custom_call" | custom-call | tf_op jit(solution)/shard_map/attend/pallas_call | solution.py:117
  87.3 5.8 %all-to-all-start.2 = ((bf16[8,8,32,128]{3,2,1,0:T(8,128)(2,1)}), bf16[8,8,32,128]{3,2,1,0:T(8,128)(2,1)S(1)}, u32[]{:S(2)}, u32[]{:S(2)}) async-start(bf16[8,8,32,128]{3,2,1,0:T(8,128)(2,1)} %attend.1), calls=%async_computation.2 | async-start | bytes 1048576 | tf_op jit(solution)/shard_map/all_to_all | solution.py:397
  95.1 7.8 %all-to-all-done.2.att_ref = bf16[8,8,32,128]{3,2,1,0:T(8,128)(2,1)S(1)} async-done(((bf16[8,8,32,128]{3,2,1,0:T(8,128)(2,1)}), bf16[8,8,32,128]{3,2,1,0:T(8,128)(2,1)S(1)}, u32[]{:S(2)}, u32[]{:S(2)}) %all-to-all-start.2) | async-done | bytes 524320 | tf_op jit(solution)/shard_map/all_to_all | solution.py:397
  103.7 8.1 %sides.1 = (bf16[8,128,256]{2,1,0:T(8,128)(2,1)}, bf16[8,48,128]{2,1,0:T(8,128)(2,1)}, bf16[264,128]{1,0:T(8,128)(2,1)}) custom-call(bf16[8,8,32,128]{3,2,1,0:T(8,128)(2,1)} %copy-done.5, bf16[8,256,128]{2,1,0:T(8,128)(2,1)} %get-tuple-element.11.gate_ref, bf16[8,128,256]{2,1,0:T(8,128)(2,1)} %stack_ref.1, f32[8,1,128]{2,1,0:T(1,128)} %bitcast.114, ...), custom_call_target="tpu_custom_call" | custom-call | tf_op jit(solution)/shard_map/sides/pallas_call | solution.py:169
  111.7 2.8 collective-permute-start.10
  114.5 3.3 %collective-permute-done.10 = bf16[264,128]{1,0:T(8,128)(2,1)S(1)} collective-permute-done((bf16[264,128]{1,0:T(8,128)(2,1)}, bf16[264,128]{1,0:T(8,128)(2,1)S(1)}, u32[]{:S(2)}, u32[]{:S(2)}) %collective-permute-start.10) | collective-permute-done | bytes 67616 | tf_op jit(solution)/shard_map/ppermute | solution.py:404
  118.7 1.3 collective-permute-start.11
  120.0 3.4 %all-to-all-start.3 = ((bf16[8,48,128]{2,1,0:T(8,128)(2,1)}), bf16[8,48,128]{2,1,0:T(8,128)(2,1)S(1)}, u32[]{:S(2)}, u32[]{:S(2)}) async-start(bf16[8,48,128]{2,1,0:T(8,128)(2,1)} %get-tuple-element.13), calls=%async_computation.3 | async-start | bytes 196608 | tf_op jit(solution)/shard_map/all_to_all | solution.py:397
  123.4 2.1 collective-permute-start.12
  126.4 3.5 %all-to-all-done.3 = bf16[8,48,128]{2,1,0:T(8,128)(2,1)S(1)} async-done(((bf16[8,48,128]{2,1,0:T(8,128)(2,1)}), bf16[8,48,128]{2,1,0:T(8,128)(2,1)S(1)}, u32[]{:S(2)}, u32[]{:S(2)}) %all-to-all-start.3) | async-done | bytes 98336 | tf_op jit(solution)/shard_map/all_to_all | solution.py:397
  129.9 3.3 %collective-permute-start.13 = (bf16[2,264,128]{2,1,0:T(8,128)(2,1)S(1)}, bf16[2,264,128]{2,1,0:T(8,128)(2,1)S(1)}, u32[]{:S(2)}, u32[]{:S(2)}) collective-permute-start(bf16[2,264,128]{2,1,0:T(8,128)(2,1)S(1)} %collective-permute-done.11), channel_id=1, source_target_pairs={{0,16},{16,32},{32,48},{48,64},{64,80},{80,96},{96,112},{112,0},{1... | collective-permute-start | bytes 405512 | tf_op jit(solution)/shard_map/ppermute | solution.py:407
  133.3 2.6 collective-permute-done.13
  136.0 4.5 %collective-permute-start.15 = (bf16[2,264,128]{2,1,0:T(8,128)(2,1)S(1)}, bf16[2,264,128]{2,1,0:T(8,128)(2,1)S(1)}, u32[]{:S(2)}, u32[]{:S(2)}) collective-permute-start(bf16[2,264,128]{2,1,0:T(8,128)(2,1)S(1)} %collective-permute-done.13), channel_id=1, source_target_pairs={{0,16},{16,32},{32,48},{48,64},{64,80},{80,96},{96,112},{112,0},{1... | collective-permute-start | bytes 405512 | tf_op jit(solution)/shard_map/ppermute | solution.py:407
  140.8 5.4 %collective-permute-done.16 = bf16[2,264,128]{2,1,0:T(8,128)(2,1)S(1)} collective-permute-done((bf16[2,264,128]{2,1,0:T(8,128)(2,1)S(1)}, bf16[2,264,128]{2,1,0:T(8,128)(2,1)S(1)}, u32[]{:S(2)}, u32[]{:S(2)}) %collective-permute-start.16) | collective-permute-done | bytes 135200 | tf_op jit(solution)/shard_map/ppermute | solution.py:408
  146.3 2.0 collective-permute-start.17
  148.3 2.1 collective-permute-done.18
  152.0 11.7 %all-to-all-start.4 = ((bf16[32,16,128]{2,1,0:T(8,128)(2,1)}), bf16[32,16,128]{2,1,0:T(8,128)(2,1)S(1)}, u32[]{:S(2)}, u32[]{:S(2)}) async-start(bf16[32,16,128]{2,1,0:T(8,128)(2,1)} %pad_maximum_fusion.2), calls=%async_computation.4 | async-start | bytes 262144 | tf_op jit(solution)/shard_map/all_to_all | solution.py:397
  163.7 10.8 %all-to-all-done.4 = bf16[32,16,128]{2,1,0:T(8,128)(2,1)S(1)} async-done(((bf16[32,16,128]{2,1,0:T(8,128)(2,1)}), bf16[32,16,128]{2,1,0:T(8,128)(2,1)S(1)}, u32[]{:S(2)}, u32[]{:S(2)}) %all-to-all-start.4) | async-done | bytes 131104 | tf_op jit(solution)/shard_map/all_to_all | solution.py:397
  175.6 4.9 %all-to-all-start.5 = ((bf16[8,9,32,128]{3,2,1,0:T(8,128)(2,1)}), bf16[8,9,32,128]{3,2,1,0:T(8,128)(2,1)S(1)}, u32[]{:S(2)}, u32[]{:S(2)}) async-start(bf16[8,9,32,128]{3,2,1,0:T(8,128)(2,1)} %broadcast_in_dim.8), calls=%async_computation.5 | async-start | bytes 1179648 | tf_op jit(solution)/shard_map/all_to_all | solution.py:397
  183.0 6.7 %all-to-all-done.5 = bf16[8,9,32,128]{3,2,1,0:T(8,128)(2,1)S(1)} async-done(((bf16[8,9,32,128]{3,2,1,0:T(8,128)(2,1)}), bf16[8,9,32,128]{3,2,1,0:T(8,128)(2,1)S(1)}, u32[]{:S(2)}, u32[]{:S(2)}) %all-to-all-start.5) | async-done | bytes 589856 | tf_op jit(solution)/shard_map/all_to_all | solution.py:397
  192.6 12.2 %outer.1 = (f32[32,128,128]{2,1,0:T(8,128)}, bf16[32,128,128]{2,1,0:T(8,128)(2,1)}, bf16[32,128,128]{2,1,0:T(8,128)(2,1)}) custom-call(s32[4]{0:T(128)} %pad_add_fusion.at_ref, bf16[8,256,128]{2,1,0:T(8,128)(2,1)} %bitcast.90, bf16[256,128]{1,0:T(8,128)(2,1)} %bitcast.104, bf16[8,2,264,128]{3,2,1,0:T(8,128)(2,1)} %copy-done.6, ...), custom_call_target="tpu_custom_call" | custom-call | tf_op jit(solution)/shard_map/outer/pallas_call | solution.py:265
  204.7 1.7 maximum_bitcast_fusion
  206.5 1.4 copy.54
  207.8 60.5 %all_to_all.41 = bf16[128,2,32,128]{3,2,1,0:T(8,128)(2,1)S(1)} all-to-all(bf16[128,2,32,128]{3,2,1,0:T(8,128)(2,1)S(1)} %copy.54), channel_id=1, replica_groups=mesh['branch'=2,'row_0'=8,'row_1'=2,'chan'=8] {'branch','row_0','chan'}, dimensions={0} | all-to-all | bytes 4194304 | tf_op jit(solution)/shard_map/all_to_all | solution.py:397
  268.4 1.3 fusion.12
  269.7 2.7 collective-permute-done.20.other_ref
  273.4 5.7 %triangle.1 = bf16[16,8,32,128]{3,2,1,0:T(8,128)(2,1)} custom-call(s32[1]{0:T(128)} %bitcast.me_ref, bf16[16,8,32,128]{3,2,1,0:T(8,128)(2,1)} %bitcast.87, bf16[16,8,32,128]{3,2,1,0:T(8,128)(2,1)} %bitcast.86, bf16[16,8,32,128]{3,2,1,0:T(8,128)(2,1)} %copy-done.9), custom_call_target="tpu_custom_call" | custom-call | tf_op jit(solution)/shard_map/triangle/pallas_call | solution.py:323
  279.1 7.1 %all-to-all-start.7 = ((bf16[128,32,128]{2,1,0:T(8,128)(2,1)}), bf16[128,32,128]{2,1,0:T(8,128)(2,1)S(1)}, u32[]{:S(2)}, u32[]{:S(2)}) async-start(bf16[128,32,128]{2,1,0:T(8,128)(2,1)} %bitcast.84), calls=%async_computation.7 | async-start | bytes 2097152 | tf_op jit(solution)/shard_map/all_to_all | solution.py:397
  287.7 30.5 %all-to-all-done.7.prod_ref = bf16[128,32,128]{2,1,0:T(8,128)(2,1)S(1)} async-done(((bf16[128,32,128]{2,1,0:T(8,128)(2,1)}), bf16[128,32,128]{2,1,0:T(8,128)(2,1)S(1)}, u32[]{:S(2)}, u32[]{:S(2)}) %all-to-all-start.7) | async-done | bytes 1048608 | tf_op jit(solution)/shard_map/all_to_all | solution.py:397
  319.2 8.5 %finish.1 = bf16[32,128,128]{2,1,0:T(8,128)(2,1)} custom-call(bf16[128,32,128]{2,1,0:T(8,128)(2,1)} %copy-done.4, f32[32,128,128]{2,1,0:T(8,128)} %get-tuple-element.17.mid_ref, bf16[128,128]{1,0:T(8,128)(2,1)} %bitcast.112, bf16[128,128]{1,0:T(8,128)(2,1)} %bitcast.113), custom_call_target="tpu_custom_call" | custom-call | tf_op jit(solution)/shard_map/finish/pallas_call | solution.py:375
  (108 shorter events, 23.4 us)
Async XLA Ops:
  0.6 3.0 copy-start
  0.6 1.7 copy-start.1
  3.7 20.8 %copy-start.10 = (bf16[256,1024]{1,0:T(8,128)(2,1)S(1)}, bf16[256,1024]{1,0:T(8,128)(2,1)}, u32[]{:S(2)}) copy-start(bf16[256,1024]{1,0:T(8,128)(2,1)} %param.16) | copy-start | bytes 1572868
  16.7 5.8 %collective-permute-start = (bf16[8,32,128]{2,1,0:T(8,128)(2,1)S(1)}, bf16[8,32,128]{2,1,0:T(8,128)(2,1)S(1)}, u32[]{:S(2)}, u32[]{:S(2)}) collective-permute-start(bf16[8,32,128]{2,1,0:T(8,128)(2,1)S(1)} %all_to_all.40), channel_id=1, source_target_pairs={{0,128},{128,0},{1,129},{129,1},{2,130},{130,2},{3,131},{131,3},{4... | collective-permute-start | bytes 196616 | tf_op jit(solution)/shard_map/ppermute | solution.py:404
  22.5 14.0 %collective-permute-start.1 = (bf16[2,8,32,128]{3,2,1,0:T(8,128)(2,1)S(1)}, bf16[2,8,32,128]{3,2,1,0:T(8,128)(2,1)S(1)}, u32[]{:S(2)}, u32[]{:S(2)}) collective-permute-start(bf16[2,8,32,128]{3,2,1,0:T(8,128)(2,1)S(1)} %pad_maximum_fusion.1), channel_id=1, source_target_pairs={{0,16},{16,32},{32,48},{48,64},{64,80},{80,96},{96,112},{112,0},{1... | collective-permute-start | bytes 393224 | tf_op jit(solution)/shard_map/ppermute | solution.py:407
  32.7 31.5 %all-to-all-start = ((bf16[8,8,96,128]{3,2,1,0:T(8,128)(2,1)}), bf16[8,8,96,128]{3,2,1,0:T(8,128)(2,1)S(1)}, u32[]{:S(2)}, u32[]{:S(2)}) async-start(bf16[8,8,96,128]{3,2,1,0:T(8,128)(2,1)} %get-tuple-element.10), calls=%async_computation | async-start | bytes 3145728 | tf_op jit(solution)/shard_map/all_to_all | solution.py:397
  36.2 5.0 %collective-permute-start.2 = (bf16[2,8,32,128]{3,2,1,0:T(8,128)(2,1)S(1)}, bf16[2,8,32,128]{3,2,1,0:T(8,128)(2,1)S(1)}, u32[]{:S(2)}, u32[]{:S(2)}) collective-permute-start(bf16[2,8,32,128]{3,2,1,0:T(8,128)(2,1)S(1)} %pad_maximum_fusion.1), channel_id=1, source_target_pairs={{0,112},{16,0},{32,16},{48,32},{64,48},{80,64},{96,80},{112,96},{1... | collective-permute-start | bytes 393224 | tf_op jit(solution)/shard_map/ppermute | solution.py:408
  36.5 27.1 %copy-start.16 = (s32[1024]{0:T(1024)S(1)}, s32[1024]{0:T(1024)}, u32[]{:S(2)}) copy-start(s32[1024]{0:T(1024)} %param.14) | copy-start | bytes 12292
  36.5 7.0 %collective-permute-start.3 = (bf16[2,8,32,128]{3,2,1,0:T(8,128)(2,1)S(1)}, bf16[2,8,32,128]{3,2,1,0:T(8,128)(2,1)S(1)}, u32[]{:S(2)}, u32[]{:S(2)}) collective-permute-start(bf16[2,8,32,128]{3,2,1,0:T(8,128)(2,1)S(1)} %collective-permute-done.1), channel_id=1, source_target_pairs={{0,16},{16,32},{32,48},{48,64},{64,80},{80,96},{96,112},{112,0},{1... | collective-permute-start | bytes 393224 | tf_op jit(solution)/shard_map/ppermute | solution.py:407
  41.3 6.8 %collective-permute-start.4 = (bf16[2,8,32,128]{3,2,1,0:T(8,128)(2,1)S(1)}, bf16[2,8,32,128]{3,2,1,0:T(8,128)(2,1)S(1)}, u32[]{:S(2)}, u32[]{:S(2)}) collective-permute-start(bf16[2,8,32,128]{3,2,1,0:T(8,128)(2,1)S(1)} %collective-permute-done.2), channel_id=1, source_target_pairs={{0,112},{16,0},{32,16},{48,32},{64,48},{80,64},{96,80},{112,96},{1... | collective-permute-start | bytes 393224 | tf_op jit(solution)/shard_map/ppermute | solution.py:408
  43.5 13.1 %collective-permute-start.5 = (bf16[2,8,32,128]{3,2,1,0:T(8,128)(2,1)S(1)}, bf16[2,8,32,128]{3,2,1,0:T(8,128)(2,1)S(1)}, u32[]{:S(2)}, u32[]{:S(2)}) collective-permute-start(bf16[2,8,32,128]{3,2,1,0:T(8,128)(2,1)S(1)} %collective-permute-done.3), channel_id=1, source_target_pairs={{0,16},{16,32},{32,48},{48,64},{64,80},{80,96},{96,112},{112,0},{1... | collective-permute-start | bytes 393224 | tf_op jit(solution)/shard_map/ppermute | solution.py:407
  48.0 7.3 %collective-permute-start.6 = (bf16[2,8,32,128]{3,2,1,0:T(8,128)(2,1)S(1)}, bf16[2,8,32,128]{3,2,1,0:T(8,128)(2,1)S(1)}, u32[]{:S(2)}, u32[]{:S(2)}) collective-permute-start(bf16[2,8,32,128]{3,2,1,0:T(8,128)(2,1)S(1)} %collective-permute-done.4), channel_id=1, source_target_pairs={{0,112},{16,0},{32,16},{48,32},{64,48},{80,64},{96,80},{112,96},{1... | collective-permute-start | bytes 393224 | tf_op jit(solution)/shard_map/ppermute | solution.py:408
  55.4 5.5 %collective-permute-start.8 = (bf16[1,8,32,128]{3,2,1,0:T(8,128)(2,1)S(1)}, bf16[1,8,32,128]{3,2,1,0:T(8,128)(2,1)S(1)}, u32[]{:S(2)}, u32[]{:S(2)}) collective-permute-start(bf16[1,8,32,128]{3,2,1,0:T(8,128)(2,1)S(1)} %slice.58), channel_id=1, source_target_pairs={{0,112},{16,0},{32,16},{48,32},{64,48},{80,64},{96,80},{112,96},{1... | collective-permute-start | bytes 196616 | tf_op jit(solution)/shard_map/ppermute | solution.py:410
  56.6 6.0 %collective-permute-start.7 = (bf16[1,8,32,128]{3,2,1,0:T(8,128)(2,1)S(1)}, bf16[1,8,32,128]{3,2,1,0:T(8,128)(2,1)S(1)}, u32[]{:S(2)}, u32[]{:S(2)}) collective-permute-start(bf16[1,8,32,128]{3,2,1,0:T(8,128)(2,1)S(1)} %slice.57), channel_id=1, source_target_pairs={{0,16},{16,32},{32,48},{48,64},{64,80},{80,96},{96,112},{112,0},{1... | collective-permute-start | bytes 196616 | tf_op jit(solution)/shard_map/ppermute | solution.py:410
  62.7 2.9 copy-start.7
  62.7 2.9 collective-permute-start.9
  64.2 1.4 copy-start.2
  65.6 27.6 %copy-start.17 = (s32[8,128]{1,0:T(8,128)S(1)}, s32[8,128]{1,0:T(8,128)}, u32[]{:S(2)}) copy-start(s32[8,128]{1,0:T(8,128)} %param.15) | copy-start | bytes 12292
  65.6 28.2 %copy-start.13 = (bf16[256,64]{0,1:T(8,128)(2,1)S(1)}, bf16[256,64]{0,1:T(8,128)(2,1)}, u32[]{:S(2)}) copy-start(bf16[256,64]{0,1:T(8,128)(2,1)} %param.19) | copy-start | bytes 98308
  87.3 15.6 %all-to-all-start.2 = ((bf16[8,8,32,128]{3,2,1,0:T(8,128)(2,1)}), bf16[8,8,32,128]{3,2,1,0:T(8,128)(2,1)S(1)}, u32[]{:S(2)}, u32[]{:S(2)}) async-start(bf16[8,8,32,128]{3,2,1,0:T(8,128)(2,1)} %attend.1), calls=%async_computation.2 | async-start | bytes 1048576 | tf_op jit(solution)/shard_map/all_to_all | solution.py:397
  102.9 0.8 copy-start.5
  111.7 6.1 %collective-permute-start.10 = (bf16[264,128]{1,0:T(8,128)(2,1)}, bf16[264,128]{1,0:T(8,128)(2,1)S(1)}, u32[]{:S(2)}, u32[]{:S(2)}) collective-permute-start(bf16[264,128]{1,0:T(8,128)(2,1)} %get-tuple-element.14), channel_id=1, source_target_pairs={{0,128},{128,0},{1,129},{129,1},{2,130},{130,2},{3,131},{131,3},{4... | collective-permute-start | bytes 202760 | tf_op jit(solution)/shard_map/ppermute | solution.py:404
  118.7 11.2 %collective-permute-start.11 = (bf16[2,264,128]{2,1,0:T(8,128)(2,1)S(1)}, bf16[2,264,128]{2,1,0:T(8,128)(2,1)S(1)}, u32[]{:S(2)}, u32[]{:S(2)}) collective-permute-start(bf16[2,264,128]{2,1,0:T(8,128)(2,1)S(1)} %pad_maximum_fusion), channel_id=1, source_target_pairs={{0,16},{16,32},{32,48},{48,64},{64,80},{80,96},{96,112},{112,0},{1... | collective-permute-start | bytes 405512 | tf_op jit(solution)/shard_map/ppermute | solution.py:407
  120.0 9.8 %all-to-all-start.3 = ((bf16[8,48,128]{2,1,0:T(8,128)(2,1)}), bf16[8,48,128]{2,1,0:T(8,128)(2,1)S(1)}, u32[]{:S(2)}, u32[]{:S(2)}) async-start(bf16[8,48,128]{2,1,0:T(8,128)(2,1)} %get-tuple-element.13), calls=%async_computation.3 | async-start | bytes 196608 | tf_op jit(solution)/shard_map/all_to_all | solution.py:397
  123.4 9.8 %collective-permute-start.12 = (bf16[2,264,128]{2,1,0:T(8,128)(2,1)S(1)}, bf16[2,264,128]{2,1,0:T(8,128)(2,1)S(1)}, u32[]{:S(2)}, u32[]{:S(2)}) collective-permute-start(bf16[2,264,128]{2,1,0:T(8,128)(2,1)S(1)} %pad_maximum_fusion), channel_id=1, source_target_pairs={{0,112},{16,0},{32,16},{48,32},{64,48},{80,64},{96,80},{112,96},{1... | collective-permute-start | bytes 405512 | tf_op jit(solution)/shard_map/ppermute | solution.py:408
  129.9 6.1 %collective-permute-start.13 = (bf16[2,264,128]{2,1,0:T(8,128)(2,1)S(1)}, bf16[2,264,128]{2,1,0:T(8,128)(2,1)S(1)}, u32[]{:S(2)}, u32[]{:S(2)}) collective-permute-start(bf16[2,264,128]{2,1,0:T(8,128)(2,1)S(1)} %collective-permute-done.11), channel_id=1, source_target_pairs={{0,16},{16,32},{32,48},{48,64},{64,80},{80,96},{96,112},{112,0},{1... | collective-permute-start | bytes 405512 | tf_op jit(solution)/shard_map/ppermute | solution.py:407
  133.2 7.5 %collective-permute-start.14 = (bf16[2,264,128]{2,1,0:T(8,128)(2,1)S(1)}, bf16[2,264,128]{2,1,0:T(8,128)(2,1)S(1)}, u32[]{:S(2)}, u32[]{:S(2)}) collective-permute-start(bf16[2,264,128]{2,1,0:T(8,128)(2,1)S(1)} %collective-permute-done.12), channel_id=1, source_target_pairs={{0,112},{16,0},{32,16},{48,32},{64,48},{80,64},{96,80},{112,96},{1... | collective-permute-start | bytes 405512 | tf_op jit(solution)/shard_map/ppermute | solution.py:408
  136.0 10.3 %collective-permute-start.15 = (bf16[2,264,128]{2,1,0:T(8,128)(2,1)S(1)}, bf16[2,264,128]{2,1,0:T(8,128)(2,1)S(1)}, u32[]{:S(2)}, u32[]{:S(2)}) collective-permute-start(bf16[2,264,128]{2,1,0:T(8,128)(2,1)S(1)} %collective-permute-done.13), channel_id=1, source_target_pairs={{0,16},{16,32},{32,48},{48,64},{64,80},{80,96},{96,112},{112,0},{1... | collective-permute-start | bytes 405512 | tf_op jit(solution)/shard_map/ppermute | solution.py:407
  140.7 5.4 %collective-permute-start.16 = (bf16[2,264,128]{2,1,0:T(8,128)(2,1)S(1)}, bf16[2,264,128]{2,1,0:T(8,128)(2,1)S(1)}, u32[]{:S(2)}, u32[]{:S(2)}) collective-permute-start(bf16[2,264,128]{2,1,0:T(8,128)(2,1)S(1)} %collective-permute-done.14), channel_id=1, source_target_pairs={{0,112},{16,0},{32,16},{48,32},{64,48},{80,64},{96,80},{112,96},{1... | collective-permute-start | bytes 405512 | tf_op jit(solution)/shard_map/ppermute | solution.py:408
  146.2 4.3 %collective-permute-start.18 = (bf16[1,264,128]{2,1,0:T(8,128)(2,1)S(1)}, bf16[1,264,128]{2,1,0:T(8,128)(2,1)S(1)}, u32[]{:S(2)}, u32[]{:S(2)}) collective-permute-start(bf16[1,264,128]{2,1,0:T(8,128)(2,1)S(1)} %slice.65), channel_id=1, source_target_pairs={{0,112},{16,0},{32,16},{48,32},{64,48},{80,64},{96,80},{112,96},{1... | collective-permute-start | bytes 202760 | tf_op jit(solution)/shard_map/ppermute | solution.py:410
  146.3 4.8 %collective-permute-start.17 = (bf16[1,264,128]{2,1,0:T(8,128)(2,1)S(1)}, bf16[1,264,128]{2,1,0:T(8,128)(2,1)S(1)}, u32[]{:S(2)}, u32[]{:S(2)}) collective-permute-start(bf16[1,264,128]{2,1,0:T(8,128)(2,1)S(1)} %slice.64), channel_id=1, source_target_pairs={{0,16},{16,32},{32,48},{48,64},{64,80},{80,96},{96,112},{112,0},{1... | collective-permute-start | bytes 202760 | tf_op jit(solution)/shard_map/ppermute | solution.py:410
  151.1 24.5 %copy-start.6 = (bf16[8,2,264,128]{3,2,1,0:T(8,128)(2,1)}, bf16[8,2,264,128]{3,2,1,0:T(8,128)(2,1)S(1)}, u32[]{:S(2)}) copy-start(bf16[8,2,264,128]{3,2,1,0:T(8,128)(2,1)S(1)} %fusion.8.mine_ref) | copy-start | bytes 3244036
  151.1 40.5 %collective-permute-start.19 = (bf16[8,2,264,128]{3,2,1,0:T(8,128)(2,1)S(1)}, bf16[8,2,264,128]{3,2,1,0:T(8,128)(2,1)S(1)}, u32[]{:S(2)}, u32[]{:S(2)}) collective-permute-start(bf16[8,2,264,128]{3,2,1,0:T(8,128)(2,1)S(1)} %fusion.8.mine_ref), channel_id=1, source_target_pairs={{0,8},{8,0},{1,9},{9,1},{2,10},{10,2},{3,11},{11,3},{4,12},{12,4},... | collective-permute-start | bytes 3244040 | tf_op jit(solution)/shard_map/ppermute | solution.py:393
  152.0 22.5 %all-to-all-start.4 = ((bf16[32,16,128]{2,1,0:T(8,128)(2,1)}), bf16[32,16,128]{2,1,0:T(8,128)(2,1)S(1)}, u32[]{:S(2)}, u32[]{:S(2)}) async-start(bf16[32,16,128]{2,1,0:T(8,128)(2,1)} %pad_maximum_fusion.2), calls=%async_computation.4 | async-start | bytes 262144 | tf_op jit(solution)/shard_map/all_to_all | solution.py:397
  174.6 6.0 %copy-start.11 = (bf16[1024,128]{1,0:T(8,128)(2,1)S(1)}, bf16[1024,128]{1,0:T(8,128)(2,1)}, u32[]{:S(2)}) copy-start(bf16[1024,128]{1,0:T(8,128)(2,1)} %param.20) | copy-start | bytes 786436
  175.6 6.1 %copy-start.12 = (bf16[128,512]{1,0:T(8,128)(2,1)S(1)}, bf16[128,512]{1,0:T(8,128)(2,1)}, u32[]{:S(2)}) copy-start(bf16[128,512]{1,0:T(8,128)(2,1)} %param.21) | copy-start | bytes 393220
  175.6 14.2 %all-to-all-start.5 = ((bf16[8,9,32,128]{3,2,1,0:T(8,128)(2,1)}), bf16[8,9,32,128]{3,2,1,0:T(8,128)(2,1)S(1)}, u32[]{:S(2)}, u32[]{:S(2)}) async-start(bf16[8,9,32,128]{3,2,1,0:T(8,128)(2,1)} %broadcast_in_dim.8), calls=%async_computation.5 | async-start | bytes 1179648 | tf_op jit(solution)/shard_map/all_to_all | solution.py:397
  191.6 1.0 copy-start.8
  269.7 2.7 copy-start.3
  269.7 2.7 collective-permute-start.20
  272.4 1.0 copy-start.9
  279.1 7.1 %copy-start.14 = (bf16[128,128]{1,0:T(8,128)(2,1)S(1)}, bf16[128,128]{1,0:T(8,128)(2,1)}, u32[]{:S(2)}) copy-start(bf16[128,128]{1,0:T(8,128)(2,1)} %param.23) | copy-start | bytes 98308
  279.1 7.8 %copy-start.15 = (bf16[128,128]{1,0:T(8,128)(2,1)S(1)}, bf16[128,128]{1,0:T(8,128)(2,1)}, u32[]{:S(2)}) copy-start(bf16[128,128]{1,0:T(8,128)(2,1)} %param.22) | copy-start | bytes 98308
  279.1 39.1 %all-to-all-start.7 = ((bf16[128,32,128]{2,1,0:T(8,128)(2,1)}), bf16[128,32,128]{2,1,0:T(8,128)(2,1)S(1)}, u32[]{:S(2)}, u32[]{:S(2)}) async-start(bf16[128,32,128]{2,1,0:T(8,128)(2,1)} %bitcast.84), calls=%async_computation.7 | async-start | bytes 2097152 | tf_op jit(solution)/shard_map/all_to_all | solution.py:397
  318.2 1.0 copy-start.4

commit v3 on v2

v3 whole, which is shorter than its diff:
```python
import functools

import jax
import jax.numpy as jnp
from jax import lax
from jax.experimental import pallas as pl
from jax.experimental.pallas import tpu as pltpu
from jax.sharding import Mesh
from jax.sharding import PartitionSpec as P


BRANCH_ROW = ("branch", "row_0", "row_1")
CHIPS = ("branch", "row_0", "chan")
SWAP = ((0, 1), (1, 0))
EPSILON = 1e-05
MASKED = 1000000000.0
LOG2E = 1.4426950408889634
BF16 = jnp.bfloat16
F32 = jnp.float32


def params(mebibytes):
    return pltpu.CompilerParams(
        dimension_semantics=("arbitrary",), vmem_limit_bytes=mebibytes * 1024 * 1024
    )


def dot(a, b, dims):
    return lax.dot_general(a, b, ((dims[:1], dims[1:]), ((), ())), preferred_element_type=F32)


def standardize(values, axis):
    values = values.astype(F32)
    centered = values - jnp.mean(values, axis=axis, keepdims=True)
    spread = jnp.mean(centered * centered, axis=axis, keepdims=True)
    return centered * lax.rsqrt(spread + EPSILON)


def sigmoid(x):
    return 1.0 / (1.0 + jnp.exp(-x))


def whole(shape):
    return pl.BlockSpec(shape, lambda *_: (0,) * len(shape))


def project_kernel(heads, width, x_ref, w_ref, qkv_ref, gate_ref):
    entries, residues, features = x_ref.shape
    normed = standardize(x_ref[...].reshape(entries * residues, features), -1).astype(BF16)
    packed = dot(w_ref[...], normed, (1, 1)).astype(BF16)
    for s in range(entries):
        at = slice(s * residues, (s + 1) * residues)
        for h in range(heads):
            base = h * 4 * width
            qkv_ref[h, s] = packed[base : base + 3 * width, at]
            gate_ref[s, h * width : (h + 1) * width] = packed[
                base + 3 * width : base + 4 * width, at
            ]


def project_msa(stack, weights, heads):
    entries, residues, features = stack.shape
    width = features // heads
    take = 2
    return pl.pallas_call(
        functools.partial(project_kernel, heads, width),
        grid=(entries // take,),
        in_specs=[
            pl.BlockSpec((take, residues, features), lambda s: (s, 0, 0)),
            whole((4 * features, features)),
        ],
        out_specs=[
            pl.BlockSpec((heads, take, 3 * width, residues), lambda s: (0, s, 0, 0)),
            pl.BlockSpec((take, features, residues), lambda s: (s, 0, 0)),
        ],
        out_shape=[
            jax.ShapeDtypeStruct((heads, entries, 3 * width, residues), BF16),
            jax.ShapeDtypeStruct((entries, features, residues), BF16),
        ],
        compiler_params=params(16),
        name="project_msa",
    )(stack, weights.T)


def attend_kernel(width, at_ref, qkv_ref, mine_ref, other_ref, pen_ref, out_ref, bias_ref, value_ref):
    block = pl.program_id(0)
    columns, entries = qkv_ref.shape[0], qkv_ref.shape[1]
    lanes = qkv_ref.shape[3]
    take = out_ref.shape[0]
    length, _, _, tile, _ = mine_ref.shape
    first = at_ref[0] == 0

    @pl.when(block == 0)
    def _():
        ones = jnp.ones((lanes - width, lanes), F32)

        @pl.loop(0, entries)
        def _(s):
            for j in range(columns):
                part = jnp.concatenate([qkv_ref[j, s, 2 * width :].astype(F32), ones], axis=0)
                value_ref[s, j * lanes : (j + 1) * lanes] = part.T.astype(BF16)

    planes = take * lanes // (2 * tile)

    @pl.loop(0, planes)
    def _(q):
        plane = block * planes + q
        place = ring_place((plane + 2 * length - at_ref[2]) % length, length)
        side = jnp.bitwise_xor(plane // length, at_ref[1])
        upper = pl.ds(pl.multiple_of(q * 2 * tile, tile), tile)
        lower = pl.ds(pl.multiple_of(q * 2 * tile + tile, tile), tile)
        for j in range(columns):
            a = mine_ref[place, side, j].astype(F32)
            b = other_ref[place, side, j].astype(F32)
            at = slice(j * lanes, (j + 1) * lanes)
            pen = pen_ref[:, at]
            bias_ref[upper, at] = (jnp.where(first, a, b) + pen) * LOG2E
            bias_ref[lower, at] = (jnp.where(first, b, a) + pen) * LOG2E

    scale = width ** (-0.5) * LOG2E
    for s in range(entries):
        query = jnp.concatenate([qkv_ref[block * take + t, s, 0:width] for t in range(take)], axis=1)
        query = (query.astype(F32) * scale).T.astype(BF16)
        keys = jnp.concatenate([qkv_ref[j, s, width : 2 * width] for j in range(columns)], axis=1)
        logits = dot(query, keys, (1, 0)) + bias_ref[...]
        top = jnp.max(logits, axis=1, keepdims=True)
        weights = jnp.exp2(logits - top).astype(BF16)
        blended = dot(weights, value_ref[s], (1, 0))
        for t in range(take):
            part = blended[t * lanes : (t + 1) * lanes].T
            out_ref[t, s] = (part[:width] * (1.0 / part[width : width + 1])).astype(BF16)


def attend(at, qkv, mine, other, pen, width):
    columns, entries, _, lanes = qkv.shape
    take = 2
    return pl.pallas_call(
        functools.partial(attend_kernel, width),
        grid_spec=pltpu.PrefetchScalarGridSpec(
            num_scalar_prefetch=1,
            grid=(columns // take,),
            in_specs=[whole(qkv.shape), whole(mine.shape), whole(other.shape), whole(pen.shape)],
            out_specs=pl.BlockSpec((take, entries, width, lanes), lambda b, at: (b, 0, 0, 0)),
            scratch_shapes=[
                pltpu.VMEM((take * lanes, columns * lanes), F32),
                pltpu.VMEM((entries, columns * lanes, lanes), BF16),
            ],
        ),
        out_shape=jax.ShapeDtypeStruct((columns, entries, width, lanes), BF16),
        compiler_params=params(32),
        name="attend",
    )(at, qkv, mine, other, pen)


def sides_kernel(
    side, att_ref, gate_ref, stack_ref, mask_ref, wo_ref, wl_ref, wr_ref, out_ref, left_ref, right_ref, hold_ref
):
    step = pl.program_id(0)
    take, residues, features = stack_ref.shape
    gated = jnp.concatenate(
        [
            (
                att_ref[:, s].astype(F32).reshape(-1, residues) * sigmoid(gate_ref[s].astype(F32))
            ).astype(BF16)
            for s in range(take)
        ],
        axis=1,
    )
    stack = stack_ref[...].astype(F32).reshape(take * residues, features)
    updated = (stack + dot(gated, wo_ref[...], (0, 0))).astype(BF16)
    out_ref[...] = updated.reshape(take, residues, features)
    normed = standardize(updated, -1).astype(BF16)
    right = dot(wr_ref[...], normed, (1, 1))
    group = 128 // side
    spread = dot(normed, wl_ref[...], (1, 0))
    rows = lax.broadcasted_iota(jnp.int32, spread.shape, 0)
    lanes = lax.broadcasted_iota(jnp.int32, spread.shape, 1)
    spread = jnp.where(rows % group == lanes // side, spread, 0.0).astype(BF16)
    to = lax.broadcasted_iota(jnp.int32, (residues // group, residues), 0)
    of = lax.broadcasted_iota(jnp.int32, (residues // group, residues), 1)
    gather = jnp.where(of // group == to, 1.0, 0.0)
    tail = lax.broadcasted_iota(jnp.int32, (16, residues), 0)
    for s in range(take):
        mask = mask_ref[s]
        at = slice(s * residues, (s + 1) * residues)
        hold_ref[pl.ds(step * take + s, side, stride=8), :] = right[:, at] * mask
        hold_ref[pl.ds(side * 8 + step * take + s, 1), :] = mask
        left = dot((gather * mask).astype(BF16), spread[at], (1, 0))
        left_ref[s, 0 : residues // group] = left.astype(BF16)
        left_ref[s, residues // group :] = jnp.where(tail == 0, mask, 0.0).astype(BF16)

    @pl.when(step == pl.num_programs(0) - 1)
    def _():
        right_ref[...] = hold_ref[...].astype(BF16)


def sides(attended, gate, stack, mask, w_out, w_sides):
    entries, residues, features = stack.shape
    heads, _, width, _ = attended.shape
    side = w_sides.shape[1] // 2
    group = 128 // side
    rows = residues // group + 16
    take = 4
    return pl.pallas_call(
        functools.partial(sides_kernel, side),
        grid=(entries // take,),
        in_specs=[
            pl.BlockSpec((heads, take, width, residues), lambda s: (0, s, 0, 0)),
            pl.BlockSpec((take, features, residues), lambda s: (s, 0, 0)),
            pl.BlockSpec((take, residues, features), lambda s: (s, 0, 0)),
            pl.BlockSpec((take, 1, residues), lambda s: (s, 0, 0)),
            whole(w_out.shape),
            whole((features, 128)),
            whole((side, features)),
        ],
        out_specs=[
            pl.BlockSpec((take, residues, features), lambda s: (s, 0, 0)),
            pl.BlockSpec((take, rows, 128), lambda s: (s, 0, 0)),
            whole(((side + 1) * 8, residues)),
        ],
        out_shape=[
            jax.ShapeDtypeStruct(stack.shape, BF16),
            jax.ShapeDtypeStruct((entries, rows, 128), BF16),
            jax.ShapeDtypeStruct(((side + 1) * 8, residues), BF16),
        ],
        scratch_shapes=[pltpu.VMEM(((side + 1) * 8, residues), F32)],
        compiler_params=params(16),
        name="sides",
    )(
        attended,
        gate,
        stack,
        mask[:, None, :].astype(F32),
        w_out,
        jnp.tile(w_sides[:, :side], (1, group)),
        w_sides[:, side:].T,
    )


OUTER_CHUNKS = 4


def outer_kernel(
    side, at_ref, left_ref, lmask_ref, mine_ref, other_ref, couple_ref, live_ref, we_ref, wt_ref,
    mid_ref, l_ref, r_ref, right_ref, rmask_ref, rows_ref, x_ref, update_ref, count_ref,
):
    step = pl.program_id(0)
    rows, lanes = couple_ref.shape[0], couple_ref.shape[1]
    channels = couple_ref.shape[2]
    pair_rows = live_ref.shape[0]

    @pl.when(step == 0)
    def _():
        length, branches = mine_ref.shape[0], mine_ref.shape[1]

        @pl.loop(0, branches * length)
        def _(plane):
            place = ring_place((plane + branches * length - at_ref[2]) % length, length)
            which = jnp.bitwise_xor(plane // length, at_ref[1])
            at = pl.ds(pl.multiple_of(plane * 16, 16), 16)
            for d in range(side + 1):
                pair = [ref[place, which, d * 8 : (d + 1) * 8] for ref in (mine_ref, other_ref)]
                pair = jnp.concatenate(pair, axis=0)
                if d < side:
                    right_ref[d // 2, at, d % 2 * lanes : (d % 2 + 1) * lanes] = pair
                else:
                    rmask_ref[at, :] = pair

        count_ref[...] = 1.0 / (dot(lmask_ref[...], rmask_ref[...], (0, 0)) + 1.0)
        for t in range(left_ref.shape[0]):
            rows_ref[t * 128 : (t + 1) * 128] = left_ref[t].T

    @pl.when(step < OUTER_CHUNKS)
    def _():
        part = side // OUTER_CHUNKS
        for k in range(0, part, 2):
            sums = dot(rows_ref[...], right_ref[step * (part // 2) + k // 2], (1, 0)).astype(BF16)
            for i in range(pair_rows):
                for e in range(2):
                    x_ref[(k + e) * side : (k + e + 1) * side, i * lanes : (i + 1) * lanes] = sums[
                        i * side : (i + 1) * side, e * lanes : (e + 1) * lanes
                    ]
        added = dot(we_ref[step], x_ref[...], (1, 0))

        @pl.when(step == 0)
        def _():
            update_ref[...] = added

        @pl.when(step > 0)
        def _():
            update_ref[...] += added

    @pl.when(step >= OUTER_CHUNKS)
    def _():
        first = (step - OUTER_CHUNKS) * rows
        normed = []
        for i in range(rows):
            over = count_ref[pl.ds(at_ref[3] * pair_rows + first + i, 1), :]
            update = update_ref[:, pl.ds(pl.multiple_of((first + i) * lanes, lanes), lanes)]
            mid = couple_ref[i].astype(F32).T + update * over
            mid_ref[i] = mid
            normed.append(standardize(mid, 0).astype(BF16))
        normed = jnp.concatenate(normed, axis=1)
        for part, ref in ((0, l_ref), (2, r_ref)):
            gate = dot(wt_ref[part * channels : (part + 1) * channels], normed, (1, 0))
            value = dot(wt_ref[(part + 1) * channels : (part + 2) * channels], normed, (1, 0))
            both = sigmoid(gate) * value
            for i in range(rows):
                live = live_ref[pl.ds(first + i, 1), :]
                ref[i] = (both[:, i * lanes : (i + 1) * lanes] * live).astype(BF16)


def outer(at, left, lmask, mine, other, couple, live, w_exit, w_tri):
    _, entries, _ = left.shape
    pair_rows, lanes, channels = couple.shape
    rows = 8
    side = mine.shape[2] // 8 - 1
    move = lambda t, at: (jnp.maximum(t - OUTER_CHUNKS, 0), 0, 0)
    tile = pl.BlockSpec((rows, channels, lanes), move)
    depth = side * side // OUTER_CHUNKS
    w_exit = w_exit.reshape(side, side, channels).transpose(1, 0, 2)
    w_exit = w_exit.reshape(OUTER_CHUNKS, depth, channels).transpose(0, 2, 1)
    return pl.pallas_call(
        functools.partial(outer_kernel, side),
        grid_spec=pltpu.PrefetchScalarGridSpec(
            num_scalar_prefetch=1,
            grid=(OUTER_CHUNKS + pair_rows // rows,),
            in_specs=[
                whole(left.shape),
                whole(lmask.shape),
                whole(mine.shape),
                whole(other.shape),
                pl.BlockSpec((rows, lanes, channels), move),
                whole(live.shape),
                whole(w_exit.shape),
                whole((4 * channels, channels)),
            ],
            out_specs=[tile, tile, tile],
            scratch_shapes=[
                pltpu.VMEM((side // 2, entries, 2 * lanes), BF16),
                pltpu.VMEM((entries, lanes), BF16),
                pltpu.VMEM((pair_rows * side, entries), BF16),
                pltpu.VMEM((depth, pair_rows * lanes), BF16),
                pltpu.VMEM((channels, pair_rows * lanes), F32),
                pltpu.VMEM((128, lanes), F32),
            ],
        ),
        out_shape=[
            jax.ShapeDtypeStruct((pair_rows, channels, lanes), F32),
            jax.ShapeDtypeStruct((pair_rows, channels, lanes), BF16),
            jax.ShapeDtypeStruct((pair_rows, channels, lanes), BF16),
        ],
        compiler_params=params(40),
        name="outer",
    )(at, left, lmask, mine, other, couple, live, w_exit, w_tri.T)


def triangle_kernel(me_ref, l_ref, mine_ref, other_ref, out_ref):
    planes, columns, tile, lanes = l_ref.shape
    first = me_ref[0] == 0
    joined = lambda ref, p: jnp.concatenate([ref[p, k] for k in range(columns)], axis=1)
    rights = []
    for p in range(mine_ref.shape[0]):
        a, b = joined(mine_ref, p), joined(other_ref, p)
        rights += [jnp.where(first, a, b), jnp.where(first, b, a)]
    right = jnp.concatenate(rights, axis=0)
    per = lanes // (2 * tile)
    for p in range(0, planes, 4):
        left = jnp.concatenate([joined(l_ref, p + q) for q in range(4)], axis=0)
        product = dot(left, right, (1, 1)).astype(BF16)
        for q in range(4):
            for n in range(mine_ref.shape[0] // per):
                out_ref[p + q, n] = product[
                    q * tile : (q + 1) * tile, n * lanes : (n + 1) * lanes
                ]


def triangle(me, left, mine, other):
    planes, columns, tile, lanes = left.shape
    per = lanes // (2 * tile)
    take = 2
    spec = pl.BlockSpec((per * take, columns, tile, lanes), lambda n, me: (n, 0, 0, 0))
    return pl.pallas_call(
        triangle_kernel,
        grid_spec=pltpu.PrefetchScalarGridSpec(
            num_scalar_prefetch=1,
            grid=(columns // take,),
            in_specs=[whole(left.shape), spec, spec],
            out_specs=pl.BlockSpec((planes, take, tile, lanes), lambda n, me: (0, n, 0, 0)),
        ),
        out_shape=jax.ShapeDtypeStruct(left.shape, BF16),
        compiler_params=params(20),
        name="triangle",
    )(me, left, mine, other)


def switch_kernel(mid_ref, ws_ref, gate_ref):
    rows, _, lanes = mid_ref.shape
    normed = [standardize(mid_ref[i], 0).astype(BF16) for i in range(rows)]
    gate = sigmoid(dot(ws_ref[...], jnp.concatenate(normed, axis=1), (1, 0)))
    for i in range(rows):
        gate_ref[i] = gate[:, i * lanes : (i + 1) * lanes]


def switch(mid, w_switch):
    pair_rows, channels, lanes = mid.shape
    tile = pl.BlockSpec((2, channels, lanes), lambda t: (t, 0, 0))
    return pl.pallas_call(
        switch_kernel,
        grid=(pair_rows // 2,),
        in_specs=[tile, whole(w_switch.shape)],
        out_specs=tile,
        out_shape=jax.ShapeDtypeStruct(mid.shape, F32),
        compiler_params=params(16),
        name="switch",
    )(mid, w_switch.T)


def finish_kernel(prod_ref, mid_ref, gate_ref, wo_ref, out_ref, mixed_ref):
    step = pl.program_id(0)
    channels, pair_rows, lanes = prod_ref.shape
    rows = mid_ref.shape[0]

    @pl.when(step == 0)
    def _():
        zero = jnp.zeros((pair_rows, lanes), F32)
        take = 16

        def add(k, total):
            for c in range(take):
                total = total + prod_ref[k * take + c].astype(F32)
            return total

        mean = lax.fori_loop(0, channels // take, add, zero) / channels

        def add_square(k, total):
            for c in range(take):
                centered = prod_ref[k * take + c].astype(F32) - mean
                total = total + centered * centered
            return total

        spread = lax.fori_loop(0, channels // take, add_square, zero) / channels
        inverse = lax.rsqrt(spread + EPSILON)

        @pl.loop(0, channels // take)
        def _(k):
            for c in range(take):
                row = pl.multiple_of((k * take + c) * pair_rows, pair_rows)
                mixed_ref[pl.ds(row, pair_rows), :] = (
                    prod_ref[k * take + c].astype(F32) - mean
                ) * inverse

    mixed = [
        mixed_ref[pl.ds(step * rows + i, channels, stride=pair_rows), :].astype(BF16)
        for i in range(rows)
    ]
    update = dot(wo_ref[...], jnp.concatenate(mixed, axis=1), (1, 0))
    for i in range(rows):
        result = mid_ref[i] + update[:, i * lanes : (i + 1) * lanes] * gate_ref[i]
        out_ref[i] = result.T.astype(BF16)


def finish(product, mid, gate, w_out):
    channels, pair_rows, lanes = product.shape
    rows = 8
    tile = pl.BlockSpec((rows, channels, lanes), lambda t: (t, 0, 0))
    return pl.pallas_call(
        finish_kernel,
        grid=(pair_rows // rows,),
        in_specs=[whole(product.shape), tile, tile, whole(w_out.shape)],
        out_specs=pl.BlockSpec((rows, lanes, channels), lambda t: (t, 0, 0)),
        out_shape=jax.ShapeDtypeStruct((pair_rows, lanes, channels), BF16),
        scratch_shapes=[pltpu.VMEM((channels * pair_rows, lanes), F32)],
        compiler_params=params(24),
        name="finish",
    )(product, mid, gate, w_out.T)


def swap(x):
    return lax.ppermute(x, "row_1", SWAP)


def exchange(x, axes):
    return lax.all_to_all(x, axes, 0, 0, tiled=True)


def ring_gather(x):
    n = lax.axis_size("row_0")

    def shift(y, by):
        return lax.ppermute(y, "row_0", tuple((k, (k + by) % n) for k in range(n)))

    pair = jnp.stack([x, lax.ppermute(x, "branch", SWAP)])
    above, below, above_2, below_2 = (shift(pair, by) for by in (1, -1, 2, -2))
    above_3, below_3 = shift(above_2, 1), shift(below_2, -1)
    last = [shift(above_2[:1], 2), shift(below_2[1:], -2)]
    return jnp.stack([pair, above, below, above_2, below_2, above_3, below_3, jnp.concatenate(last)])


def ring_place(ahead, n):
    return jnp.where(ahead <= n // 2, jnp.maximum(2 * ahead - (ahead == n // 2), 0), 2 * (n - ahead) - 1)


def repeated(x, n):
    return jnp.broadcast_to(x[None], (n, *x.shape))


def shards(
    homolog_stack,
    couple_tensor,
    amino_occupancy,
    homolog_occupancy,
    focus_entry_coefficients,
    couple_offset_coefficients,
    focus_exit_coefficients,
    tensor_entry_coefficients,
    tensor_exit_coefficients,
    trio_entry_coefficients,
    trio_exit_switch,
    trio_exit_coefficients,
):
    _, residues, features = homolog_stack.shape
    pair_rows, pair_cols, pair_width = couple_tensor.shape
    heads = couple_offset_coefficients.shape[1]
    width = features // heads
    side = tensor_entry_coefficients.shape[1] // 2
    planes = lax.axis_size("branch") * lax.axis_size("row_0")
    chan = lax.axis_size("chan")
    core = lax.axis_index("row_1").astype(jnp.int32)
    row = lax.axis_index(BRANCH_ROW).astype(jnp.int32)
    place = [core, lax.axis_index("branch"), lax.axis_index("row_0"), row % 4]
    at = jnp.stack([p.astype(jnp.int32) for p in place])
    me = core.reshape(1)
    live = amino_occupancy.astype(F32)
    live_rows = lax.dynamic_slice_in_dim(live, row * pair_rows, pair_rows)
    live_cols = lax.dynamic_slice_in_dim(live, lax.axis_index("chan") * pair_cols, pair_cols)
    penalty = ((live - 1.0) * MASKED)[None, :]

    pair_norm = standardize(couple_tensor, -1).astype(BF16)
    bias = jnp.einsum(
        "ijc,ch->hij", pair_norm, couple_offset_coefficients, preferred_element_type=F32
    ).astype(BF16)
    bias = exchange(bias, "chan")
    bias = ring_gather(bias)
    bias_other = swap(bias)

    qkv, gate = project_msa(homolog_stack, focus_entry_coefficients, heads)
    qkv = exchange(qkv, "chan")
    attended = attend(at, qkv, bias, bias_other, penalty, width)
    attended = exchange(attended, "chan")

    homolog_after_update, left, right = sides(
        attended,
        gate,
        homolog_stack,
        homolog_occupancy,
        focus_exit_coefficients,
        tensor_entry_coefficients,
    )
    right = ring_gather(right)
    right_other = swap(right)
    members = 2 * planes
    packed_rows = residues * side // 128
    steps = chan * packed_rows // members
    left = exchange(left, "chan")
    left = jnp.concatenate(
        [
            left[:, :packed_rows].reshape(members, steps, 128),
            jnp.repeat(left[:, packed_rows : packed_rows + 8], members // chan, axis=0),
        ],
        axis=1,
    )
    left = exchange(left, BRANCH_ROW)
    left = left[:, : steps + 1].reshape(planes, 2, steps + 1, 128)
    left = jnp.where(core == 0, left, left[:, ::-1]).reshape(members, steps + 1, 128)
    left = repeated(left.transpose(1, 0, 2), chan)
    left = exchange(left, "chan")
    left = left.transpose(1, 2, 0, 3).reshape(steps + 1, members * chan, 128)
    mid, left_tri, right_tri = outer(
        at,
        left[:steps],
        left[steps],
        right,
        right_other,
        couple_tensor,
        live_rows[:, None] * live_cols[None, :],
        tensor_exit_coefficients,
        trio_entry_coefficients,
    )
    operands = jnp.stack([left_tri, right_tri]).transpose(2, 0, 1, 3)
    operands = exchange(operands, CHIPS)
    grid = (planes, chan, pair_rows, pair_cols)
    left_tri, right_tri = operands[:, 0].reshape(grid), operands[:, 1].reshape(grid)
    product = triangle(me, left_tri, right_tri, swap(right_tri))
    product = exchange(product.reshape(pair_width, pair_rows, pair_cols), CHIPS)
    gate = switch(mid, trio_exit_switch)
    pair_result = finish(product, mid, gate, trio_exit_coefficients)
    return (homolog_after_update, pair_result)


def solution(mesh):
    torus = Mesh(
        mesh.devices.reshape(mesh.shape["branch"], 8, 2, mesh.shape["chan"]),
        ("branch", "row_0", "row_1", "chan"),
    )

    return jax.shard_map(
        shards,
        mesh=torus,
        in_specs=(
            P(BRANCH_ROW, "chan", None),
            P(BRANCH_ROW, "chan", None),
            P(),
            P(BRANCH_ROW, "chan"),
            *(P() for _ in range(8)),
        ),
        out_specs=(P(BRANCH_ROW, "chan", None), P(BRANCH_ROW, "chan", None)),
        check_vma=False,
    )
```

time: 330 us -> 290 us (0.88)
  waiting for transfers between devices: 96.5 us -> 75.2 us
  Pallas kernels: 63.4 us -> 46.1 us
  local copies, waits for them, and re-layouts: 15.2 us -> 22.4 us
  starting transfers between devices: 67.9 us -> 63.7 us
  other arithmetic: 10.1 us -> 6.12 us
    ppermute x16, waiting for transfers between devices: 26.8 us -> 4.96 us  [shift(): lax.ppermute(y, 'row_0', tuple(((k, (k + by) % n) for k in range(n))))]
    unnamed x52 -> x60, local copies, waits for them, and re-layouts: 7.23 us -> 15.1 us
    all_to_all x6, starting transfers between devices: 36.5 us -> 30.2 us  [exchange(): return lax.all_to_all(x, axes, 0, 0, tiled=True)]
    pallas_call x1, Pallas kernels: 7.15 us -> 2.24 us  [project_msa(): pl.pallas_call(functools.partial(project_kernel, heads, width), grid=(ent...]
    pallas_call x1, Pallas kernels: 8.55 us -> 3.72 us  [finish(): pl.pallas_call(finish_kernel, grid=(pair_rows // rows,), in_specs=[whole(...]
    pallas_call x1 -> x2, Pallas kernels: 8.06 us -> 6.51 us  [the longest x1 3.93 us: switch(): pl.pallas_call(switch_kernel, grid=(pair_rows // 2,), in_specs=[tile, who...]
  transfers between devices with their start and end apart: 27 -> 27, of which waited for: 20 -> 12; matrix products, arithmetic and copies ran while one was open for 4% -> 5% of each run, Pallas kernels for 2% -> 2%
where the time goes in v3:
time: 290 us; the launch traced here: 288 us
  waiting for transfers between devices  75.2 us (26%)
  blocking collectives  72.2 us (25%)
  starting transfers between devices  63.7 us (22%)
  Pallas kernels  46.1 us (16%)
  local copies, waits for them, and re-layouts  22.4 us (8%)
  other arithmetic  6.12 us (2%)
    all_to_all x2, blocking collectives, exchange(): return lax.all_to_all(x, axes, 0, 0, tiled=True)  72.2 us
    all_to_all x6, waiting for transfers between devices, exchange(): return lax.all_to_all(x, axes, 0, 0, tiled=True)  61.5 us
    all_to_all x6, starting transfers between devices, exchange(): return lax.all_to_all(x, axes, 0, 0, tiled=True)  30.2 us
    ppermute x16, starting transfers between devices, shift(): lax.ppermute(y, 'row_0', tuple(((k, (k + by) % n) for k in range(n))))  27.7 us
    pallas_call x1, Pallas kernels, attend(): pl.pallas_call(functools.partial(attend_kernel, width), grid_spec=pltpu.P...  20 us
    unnamed x60, local copies, waits for them, and re-layouts  15.1 us
    pallas_call x1, Pallas kernels, outer(): pl.pallas_call(functools.partial(outer_kernel, side), grid_spec=pltpu.Pre...  9.69 us
    ppermute x2, waiting for transfers between devices, ring_gather(): pair = jnp.stack([x, lax.ppermute(x, 'branch', SWAP)])  6.1 us
  transfers between devices with their start and end apart: 27, of which 12 were waited for; matrix products, arithmetic and copies ran while one was open for 5% of the time, Pallas kernels for 2%

profile of v3, /device:TPU:32, one launch (start us, length us, event | category | flops | bytes accessed | tf_op | source)
XLA Modules:
  0.0 288.3 jit_solution(2297300516072598398)
XLA Ops:
  0.7 1.7 convert_reduce_fusion
  2.3 1.3 fusion.2
  3.7 1.5 fusion.4
  5.2 11.7 %all_to_all.40 = bf16[8,32,128]{2,1,0:T(8,128)(2,1)S(1)} all-to-all(bf16[8,32,128]{2,1,0:T(8,128)(2,1)S(1)} %bitcast.110), channel_id=1, replica_groups=mesh['branch'=2,'row_0'=8,'row_1'=2,'chan'=8] {'chan'}, dimensions={0} | all-to-all | bytes 131072 | tf_op jit(solution)/shard_map/all_to_all | solution.py:484
  16.9 2.7 collective-permute-start
  19.6 3.0 %collective-permute-done = bf16[8,32,128]{2,1,0:T(8,128)(2,1)S(1)} collective-permute-done((bf16[8,32,128]{2,1,0:T(8,128)(2,1)S(1)}, bf16[8,32,128]{2,1,0:T(8,128)(2,1)S(1)}, u32[]{:S(2)}, u32[]{:S(2)}) %collective-permute-start) | collective-permute-done | bytes 65568 | tf_op jit(solution)/shard_map/ppermute | solution.py:493
  23.3 5.4 %collective-permute-start.4 = (bf16[2,8,32,128]{3,2,1,0:T(8,128)(2,1)}, bf16[2,8,32,128]{3,2,1,0:T(8,128)(2,1)S(1)}, u32[]{:S(2)}, u32[]{:S(2)}) collective-permute-start(bf16[2,8,32,128]{3,2,1,0:T(8,128)(2,1)} %pad_maximum_fusion.1), channel_id=1, source_target_pairs={{0,96},{16,112},{32,0},{48,16},{64,32},{80,48},{96,64},{112,80},{1... | collective-permute-start | bytes 393224 | tf_op jit(solution)/shard_map/ppermute | solution.py:491
  29.9 2.2 project_msa.1
  32.2 1.2 copy-done.6
  34.1 3.6 %all-to-all-start = ((bf16[8,8,96,128]{3,2,1,0:T(8,128)(2,1)}), bf16[8,8,96,128]{3,2,1,0:T(8,128)(2,1)S(1)}, u32[]{:S(2)}, u32[]{:S(2)}) async-start(bf16[8,8,96,128]{3,2,1,0:T(8,128)(2,1)} %copy-done.6), calls=%async_computation | async-start | bytes 3145728 | tf_op jit(solution)/shard_map/all_to_all | solution.py:484
  37.7 1.1 collective-permute-start.2
  39.5 4.2 %collective-permute-start.8 = (bf16[1,8,32,128]{3,2,1,0:T(8,128)(2,1)S(1)}, bf16[1,8,32,128]{3,2,1,0:T(8,128)(2,1)S(1)}, u32[]{:S(2)}, u32[]{:S(2)}) collective-permute-start(bf16[1,8,32,128]{3,2,1,0:T(8,128)(2,1)S(1)} %slice.58), channel_id=1, source_target_pairs={{0,96},{16,112},{32,0},{48,16},{64,32},{80,48},{96,64},{112,80},{1... | collective-permute-start | bytes 196616 | tf_op jit(solution)/shard_map/ppermute | solution.py:491
  44.8 1.1 collective-permute-start.6
  45.9 1.6 bitcast_dynamic-update-slice_fusion.12
  51.6 3.6 %all-to-all-done.qkv_ref = bf16[8,8,96,128]{3,2,1,0:T(8,128)(2,1)S(1)} async-done(((bf16[8,8,96,128]{3,2,1,0:T(8,128)(2,1)}), bf16[8,8,96,128]{3,2,1,0:T(8,128)(2,1)S(1)}, u32[]{:S(2)}, u32[]{:S(2)}) %all-to-all-start) | async-done | bytes 1572896 | tf_op jit(solution)/shard_map/all_to_all | solution.py:484
  55.2 20.0 %attend.1 = bf16[8,8,32,128]{3,2,1,0:T(8,128)(2,1)S(1)} custom-call(s32[4]{0:T(128)S(1)} %pad_add_fusion.at_ref, bf16[8,8,96,128]{3,2,1,0:T(8,128)(2,1)S(1)} %all-to-all-done.qkv_ref, bf16[8,2,8,32,128]{4,3,2,1,0:T(8,128)(2,1)} %fusion.9.mine_ref, bf16[8,2,8,32,128]{4,3,2,1,0:T(8,128)(2,1)} %collective-permute-done.9.other_ref, f32[1,1024]{1,0:T(1,128)S(1)} %bitcast.100), custom_call_target="tpu_custom_call" | custom-call | tf_op jit(solution)/shard_map/attend/pallas_call | solution.py:137
  76.0 5.0 %all-to-all-start.2 = ((bf16[8,8,32,128]{3,2,1,0:T(8,128)(2,1)}), bf16[8,8,32,128]{3,2,1,0:T(8,128)(2,1)S(1)}, u32[]{:S(2)}, u32[]{:S(2)}) async-start(bf16[8,8,32,128]{3,2,1,0:T(8,128)(2,1)} %copy-done.5), calls=%async_computation.2 | async-start | bytes 1048576 | tf_op jit(solution)/shard_map/all_to_all | solution.py:484
  81.2 9.6 %all-to-all-done.2.att_ref = bf16[8,8,32,128]{3,2,1,0:T(8,128)(2,1)S(1)} async-done(((bf16[8,8,32,128]{3,2,1,0:T(8,128)(2,1)}), bf16[8,8,32,128]{3,2,1,0:T(8,128)(2,1)S(1)}, u32[]{:S(2)}, u32[]{:S(2)}) %all-to-all-start.2) | async-done | bytes 524320 | tf_op jit(solution)/shard_map/all_to_all | solution.py:484
  90.8 2.6 sides.1
  93.4 2.7 collective-permute-start.10
  96.1 3.1 %collective-permute-done.10 = bf16[264,128]{1,0:T(8,128)(2,1)S(1)} collective-permute-done((bf16[264,128]{1,0:T(8,128)(2,1)S(1)}, bf16[264,128]{1,0:T(8,128)(2,1)S(1)}, u32[]{:S(2)}, u32[]{:S(2)}) %collective-permute-start.10) | collective-permute-done | bytes 67616 | tf_op jit(solution)/shard_map/ppermute | solution.py:493
  99.2 4.1 %collective-permute-start.14 = (bf16[2,264,128]{2,1,0:T(8,128)(2,1)S(1)}, bf16[2,264,128]{2,1,0:T(8,128)(2,1)S(1)}, u32[]{:S(2)}, u32[]{:S(2)}) collective-permute-start(bf16[2,264,128]{2,1,0:T(8,128)(2,1)S(1)} %pad_maximum_fusion), channel_id=1, source_target_pairs={{0,96},{16,112},{32,0},{48,16},{64,32},{80,48},{96,64},{112,80},{1... | collective-permute-start | bytes 405512 | tf_op jit(solution)/shard_map/ppermute | solution.py:491
  103.2 1.3 collective-permute-start.11
  104.5 3.4 %all-to-all-start.3 = ((bf16[8,48,128]{2,1,0:T(8,128)(2,1)}), bf16[8,48,128]{2,1,0:T(8,128)(2,1)S(1)}, u32[]{:S(2)}, u32[]{:S(2)}) async-start(bf16[8,48,128]{2,1,0:T(8,128)(2,1)} %get-tuple-element.13), calls=%async_computation.3 | async-start | bytes 196608 | tf_op jit(solution)/shard_map/all_to_all | solution.py:484
  109.0 5.4 %all-to-all-done.3 = bf16[8,48,128]{2,1,0:T(8,128)(2,1)S(1)} async-done(((bf16[8,48,128]{2,1,0:T(8,128)(2,1)}), bf16[8,48,128]{2,1,0:T(8,128)(2,1)S(1)}, u32[]{:S(2)}, u32[]{:S(2)}) %all-to-all-start.3) | async-done | bytes 98336 | tf_op jit(solution)/shard_map/all_to_all | solution.py:484
  114.4 3.7 %collective-permute-start.18 = (bf16[1,264,128]{2,1,0:T(8,128)(2,1)S(1)}, bf16[1,264,128]{2,1,0:T(8,128)(2,1)S(1)}, u32[]{:S(2)}, u32[]{:S(2)}) collective-permute-start(bf16[1,264,128]{2,1,0:T(8,128)(2,1)S(1)} %slice.65), channel_id=1, source_target_pairs={{0,96},{16,112},{32,0},{48,16},{64,32},{80,48},{96,64},{112,80},{1... | collective-permute-start | bytes 202760 | tf_op jit(solution)/shard_map/ppermute | solution.py:491
  118.2 3.6 %collective-permute-start.15 = (bf16[2,264,128]{2,1,0:T(8,128)(2,1)S(1)}, bf16[2,264,128]{2,1,0:T(8,128)(2,1)S(1)}, u32[]{:S(2)}, u32[]{:S(2)}) collective-permute-start(bf16[2,264,128]{2,1,0:T(8,128)(2,1)S(1)} %collective-permute-done.13), channel_id=1, source_target_pairs={{0,16},{16,32},{32,48},{48,64},{64,80},{80,96},{96,112},{112,0},{1... | collective-permute-start | bytes 405512 | tf_op jit(solution)/shard_map/ppermute | solution.py:491
  121.9 2.4 collective-permute-done.15
  124.4 2.4 collective-permute-done.16
  128.0 6.9 %all-to-all-start.4 = ((bf16[32,16,128]{2,1,0:T(8,128)(2,1)}), bf16[32,16,128]{2,1,0:T(8,128)(2,1)S(1)}, u32[]{:S(2)}, u32[]{:S(2)}) async-start(bf16[32,16,128]{2,1,0:T(8,128)(2,1)} %pad_maximum_fusion.2), calls=%async_computation.4 | async-start | bytes 262144 | tf_op jit(solution)/shard_map/all_to_all | solution.py:484
  134.9 10.8 %all-to-all-done.4 = bf16[32,16,128]{2,1,0:T(8,128)(2,1)S(1)} async-done(((bf16[32,16,128]{2,1,0:T(8,128)(2,1)}), bf16[32,16,128]{2,1,0:T(8,128)(2,1)S(1)}, u32[]{:S(2)}, u32[]{:S(2)}) %all-to-all-start.4) | async-done | bytes 131104 | tf_op jit(solution)/shard_map/all_to_all | solution.py:484
  146.7 4.2 %all-to-all-start.5 = ((bf16[8,9,32,128]{3,2,1,0:T(8,128)(2,1)}), bf16[8,9,32,128]{3,2,1,0:T(8,128)(2,1)}, u32[]{:S(2)}, u32[]{:S(2)}) async-start(bf16[8,9,32,128]{3,2,1,0:T(8,128)(2,1)} %broadcast_in_dim.8), calls=%async_computation.5 | async-start | bytes 1179648 | tf_op jit(solution)/shard_map/all_to_all | solution.py:484
  151.8 1.1 copy.51
  152.9 1.7 copy.52
  154.7 5.7 %all-to-all-done.5 = bf16[8,9,32,128]{3,2,1,0:T(8,128)(2,1)} async-done(((bf16[8,9,32,128]{3,2,1,0:T(8,128)(2,1)}), bf16[8,9,32,128]{3,2,1,0:T(8,128)(2,1)}, u32[]{:S(2)}, u32[]{:S(2)}) %all-to-all-start.5) | async-done | bytes 589856 | tf_op jit(solution)/shard_map/all_to_all | solution.py:484
  160.4 1.2 slice.62
  163.8 1.2 copy-done.10
  165.1 9.7 %outer.1 = (f32[32,128,128]{2,1,0:T(8,128)S(1)}, bf16[32,128,128]{2,1,0:T(8,128)(2,1)S(1)}, bf16[32,128,128]{2,1,0:T(8,128)(2,1)S(1)}) custom-call(s32[4]{0:T(128)S(1)} %pad_add_fusion.at_ref, bf16[8,256,128]{2,1,0:T(8,128)(2,1)S(1)} %bitcast.88, bf16[256,128]{1,0:T(8,128)(2,1)S(1)} %bitcast.96, bf16[8,2,264,128]{3,2,1,0:T(8,128)(2,1)S(1)} %copy-done.8, ...), custom_call_target="tpu_custom_call" | custom-call | tf_op jit(solution)/shard_map/outer/pallas_call | solution.py:323
  175.0 1.4 copy.53
  176.3 60.5 %all_to_all.41 = bf16[128,2,32,128]{3,2,1,0:T(8,128)(2,1)S(1)} all-to-all(bf16[128,2,32,128]{3,2,1,0:T(8,128)(2,1)S(1)} %copy.53), channel_id=1, replica_groups=mesh['branch'=2,'row_0'=8,'row_1'=2,'chan'=8] {'branch','row_0','chan'}, dimensions={0} | all-to-all | bytes 4194304 | tf_op jit(solution)/shard_map/all_to_all | solution.py:484
  237.3 2.6 collective-permute-done.20.other_ref
  240.0 4.0 %triangle.1 = bf16[16,8,32,128]{3,2,1,0:T(8,128)(2,1)} custom-call(s32[1]{0:T(128)} %bitcast.me_ref, bf16[16,8,32,128]{3,2,1,0:T(8,128)(2,1)S(1)} %bitcast.87, bf16[16,8,32,128]{3,2,1,0:T(8,128)(2,1)S(1)} %bitcast.86, bf16[16,8,32,128]{3,2,1,0:T(8,128)(2,1)S(1)} %collective-permute-done.20.other_ref), custom_call_target="tpu_custom_call" | custom-call | tf_op jit(solution)/shard_map/triangle/pallas_call | solution.py:383
  243.9 7.1 %all-to-all-start.7 = ((bf16[128,32,128]{2,1,0:T(8,128)(2,1)}), bf16[128,32,128]{2,1,0:T(8,128)(2,1)S(1)}, u32[]{:S(2)}, u32[]{:S(2)}) async-start(bf16[128,32,128]{2,1,0:T(8,128)(2,1)} %bitcast.49), calls=%async_computation.7 | async-start | bytes 2097152 | tf_op jit(solution)/shard_map/all_to_all | solution.py:484
  251.3 3.9 %switch.1.gate_ref = f32[32,128,128]{2,1,0:T(8,128)S(1)} custom-call(f32[32,128,128]{2,1,0:T(8,128)S(1)} %get-tuple-element.17.mid_ref, bf16[128,128]{1,0:T(8,128)(2,1)S(1)} %bitcast.98), custom_call_target="tpu_custom_call" | custom-call | tf_op jit(solution)/shard_map/switch/pallas_call | solution.py:408
  255.2 1.3 copy-done.2
  256.6 26.5 %all-to-all-done.7.prod_ref = bf16[128,32,128]{2,1,0:T(8,128)(2,1)S(1)} async-done(((bf16[128,32,128]{2,1,0:T(8,128)(2,1)}), bf16[128,32,128]{2,1,0:T(8,128)(2,1)S(1)}, u32[]{:S(2)}, u32[]{:S(2)}) %all-to-all-start.7) | async-done | bytes 1048608 | tf_op jit(solution)/shard_map/all_to_all | solution.py:484
  283.0 1.6 copy-done.3
  284.6 3.7 %finish.1 = bf16[32,128,128]{2,1,0:T(8,128)(2,1)} custom-call(bf16[128,32,128]{2,1,0:T(8,128)(2,1)S(1)} %all-to-all-done.7.prod_ref, f32[32,128,128]{2,1,0:T(8,128)S(1)} %get-tuple-element.17.mid_ref, f32[32,128,128]{2,1,0:T(8,128)S(1)} %copy-done.3, bf16[128,128]{1,0:T(8,128)(2,1)S(1)} %bitcast.97), custom_call_target="tpu_custom_call" | custom-call | tf_op jit(solution)/shard_map/finish/pallas_call | solution.py:467
  (117 shorter events, 17.1 us)
Async XLA Ops:
  0.6 3.0 %copy-start = (bf16[128,8]{0,1:T(8,128)(2,1)S(1)}, bf16[128,8]{0,1:T(8,128)(2,1)}, u32[]{:S(2)}) copy-start(bf16[128,8]{0,1:T(8,128)(2,1)} %param.17) | copy-start | bytes 6148
  0.6 1.7 copy-start.1
  3.7 26.0 %copy-start.15 = (bf16[256,1024]{1,0:T(8,128)(2,1)S(1)}, bf16[256,1024]{1,0:T(8,128)(2,1)}, u32[]{:S(2)}) copy-start(bf16[256,1024]{1,0:T(8,128)(2,1)} %param.16) | copy-start | bytes 1572868
  5.2 24.8 %copy-start.4 = (bf16[8,128,256]{2,1,0:T(8,128)(2,1)S(1)}, bf16[8,128,256]{2,1,0:T(8,128)(2,1)}, u32[]{:S(2)}) copy-start(bf16[8,128,256]{2,1,0:T(8,128)(2,1)} %stack_ref.1) | copy-start | bytes 1572868
  16.9 5.8 %collective-permute-start = (bf16[8,32,128]{2,1,0:T(8,128)(2,1)S(1)}, bf16[8,32,128]{2,1,0:T(8,128)(2,1)S(1)}, u32[]{:S(2)}, u32[]{:S(2)}) collective-permute-start(bf16[8,32,128]{2,1,0:T(8,128)(2,1)S(1)} %all_to_all.40), channel_id=1, source_target_pairs={{0,128},{128,0},{1,129},{129,1},{2,130},{130,2},{3,131},{131,3},{4... | collective-permute-start | bytes 196616 | tf_op jit(solution)/shard_map/ppermute | solution.py:493
  23.3 16.2 %collective-permute-start.4 = (bf16[2,8,32,128]{3,2,1,0:T(8,128)(2,1)}, bf16[2,8,32,128]{3,2,1,0:T(8,128)(2,1)S(1)}, u32[]{:S(2)}, u32[]{:S(2)}) collective-permute-start(bf16[2,8,32,128]{3,2,1,0:T(8,128)(2,1)} %pad_maximum_fusion.1), channel_id=1, source_target_pairs={{0,96},{16,112},{32,0},{48,16},{64,32},{80,48},{96,64},{112,80},{1... | collective-permute-start | bytes 393224 | tf_op jit(solution)/shard_map/ppermute | solution.py:491
  28.7 15.0 %collective-permute-start.3 = (bf16[2,8,32,128]{3,2,1,0:T(8,128)(2,1)}, bf16[2,8,32,128]{3,2,1,0:T(8,128)(2,1)S(1)}, u32[]{:S(2)}, u32[]{:S(2)}) collective-permute-start(bf16[2,8,32,128]{3,2,1,0:T(8,128)(2,1)} %pad_maximum_fusion.1), channel_id=1, source_target_pairs={{0,32},{16,48},{32,64},{48,80},{64,96},{80,112},{96,0},{112,16},{1... | collective-permute-start | bytes 393224 | tf_op jit(solution)/shard_map/ppermute | solution.py:491
  28.7 16.1 %collective-permute-start.1 = (bf16[2,8,32,128]{3,2,1,0:T(8,128)(2,1)}, bf16[2,8,32,128]{3,2,1,0:T(8,128)(2,1)}, u32[]{:S(2)}, u32[]{:S(2)}) collective-permute-start(bf16[2,8,32,128]{3,2,1,0:T(8,128)(2,1)} %pad_maximum_fusion.1), channel_id=1, source_target_pairs={{0,16},{16,32},{32,48},{48,64},{64,80},{80,96},{96,112},{112,0},{1... | collective-permute-start | bytes 393224 | tf_op jit(solution)/shard_map/ppermute | solution.py:491
  32.2 1.2 copy-start.6
  34.1 21.1 %all-to-all-start = ((bf16[8,8,96,128]{3,2,1,0:T(8,128)(2,1)}), bf16[8,8,96,128]{3,2,1,0:T(8,128)(2,1)S(1)}, u32[]{:S(2)}, u32[]{:S(2)}) async-start(bf16[8,8,96,128]{3,2,1,0:T(8,128)(2,1)} %copy-done.6), calls=%async_computation | async-start | bytes 3145728 | tf_op jit(solution)/shard_map/all_to_all | solution.py:484
  37.7 9.8 %collective-permute-start.2 = (bf16[2,8,32,128]{3,2,1,0:T(8,128)(2,1)}, bf16[2,8,32,128]{3,2,1,0:T(8,128)(2,1)S(1)}, u32[]{:S(2)}, u32[]{:S(2)}) collective-permute-start(bf16[2,8,32,128]{3,2,1,0:T(8,128)(2,1)} %pad_maximum_fusion.1), channel_id=1, source_target_pairs={{0,112},{16,0},{32,16},{48,32},{64,48},{80,64},{96,80},{112,96},{1... | collective-permute-start | bytes 393224 | tf_op jit(solution)/shard_map/ppermute | solution.py:491
  39.5 12.2 %copy-start.20 = (s32[1024]{0:T(1024)S(1)}, s32[1024]{0:T(1024)}, u32[]{:S(2)}) copy-start(s32[1024]{0:T(1024)} %param.14) | copy-start | bytes 12292
  39.5 11.3 %collective-permute-start.8 = (bf16[1,8,32,128]{3,2,1,0:T(8,128)(2,1)S(1)}, bf16[1,8,32,128]{3,2,1,0:T(8,128)(2,1)S(1)}, u32[]{:S(2)}, u32[]{:S(2)}) collective-permute-start(bf16[1,8,32,128]{3,2,1,0:T(8,128)(2,1)S(1)} %slice.58), channel_id=1, source_target_pairs={{0,96},{16,112},{32,0},{48,16},{64,32},{80,48},{96,64},{112,80},{1... | collective-permute-start | bytes 196616 | tf_op jit(solution)/shard_map/ppermute | solution.py:491
  43.7 7.2 %collective-permute-start.7 = (bf16[1,8,32,128]{3,2,1,0:T(8,128)(2,1)S(1)}, bf16[1,8,32,128]{3,2,1,0:T(8,128)(2,1)S(1)}, u32[]{:S(2)}, u32[]{:S(2)}) collective-permute-start(bf16[1,8,32,128]{3,2,1,0:T(8,128)(2,1)S(1)} %slice.57), channel_id=1, source_target_pairs={{0,32},{16,48},{32,64},{48,80},{64,96},{80,112},{96,0},{112,16},{1... | collective-permute-start | bytes 196616 | tf_op jit(solution)/shard_map/ppermute | solution.py:491
  43.8 5.7 %collective-permute-start.5 = (bf16[2,8,32,128]{3,2,1,0:T(8,128)(2,1)S(1)}, bf16[2,8,32,128]{3,2,1,0:T(8,128)(2,1)S(1)}, u32[]{:S(2)}, u32[]{:S(2)}) collective-permute-start(bf16[2,8,32,128]{3,2,1,0:T(8,128)(2,1)S(1)} %collective-permute-done.3), channel_id=1, source_target_pairs={{0,16},{16,32},{32,48},{48,64},{64,80},{80,96},{96,112},{112,0},{1... | collective-permute-start | bytes 393224 | tf_op jit(solution)/shard_map/ppermute | solution.py:491
  44.8 5.3 %collective-permute-start.6 = (bf16[2,8,32,128]{3,2,1,0:T(8,128)(2,1)S(1)}, bf16[2,8,32,128]{3,2,1,0:T(8,128)(2,1)S(1)}, u32[]{:S(2)}, u32[]{:S(2)}) collective-permute-start(bf16[2,8,32,128]{3,2,1,0:T(8,128)(2,1)S(1)} %collective-permute-done.4), channel_id=1, source_target_pairs={{0,112},{16,0},{32,16},{48,32},{64,48},{80,64},{96,80},{112,96},{1... | collective-permute-start | bytes 393224 | tf_op jit(solution)/shard_map/ppermute | solution.py:491
  51.5 3.6 %collective-permute-start.9 = (bf16[8,2,8,32,128]{4,3,2,1,0:T(8,128)(2,1)}, bf16[8,2,8,32,128]{4,3,2,1,0:T(8,128)(2,1)}, u32[]{:S(2)}, u32[]{:S(2)}) collective-permute-start(bf16[8,2,8,32,128]{4,3,2,1,0:T(8,128)(2,1)} %fusion.9.mine_ref), channel_id=1, source_target_pairs={{0,8},{8,0},{1,9},{9,1},{2,10},{10,2},{3,11},{11,3},{4,12},{12,4},... | collective-permute-start | bytes 3145736 | tf_op jit(solution)/shard_map/ppermute | solution.py:480
  55.2 25.9 %copy-start.21 = (s32[8,128]{1,0:T(8,128)S(1)}, s32[8,128]{1,0:T(8,128)}, u32[]{:S(2)}) copy-start(s32[8,128]{1,0:T(8,128)} %param.15) | copy-start | bytes 12292
  55.2 25.9 %copy-start.17 = (bf16[256,64]{0,1:T(8,128)(2,1)S(1)}, bf16[256,64]{0,1:T(8,128)(2,1)}, u32[]{:S(2)}) copy-start(bf16[256,64]{0,1:T(8,128)(2,1)} %param.19) | copy-start | bytes 98308
  75.2 0.8 copy-start.5
  76.0 14.8 %copy-start.12 = (bf16[8,256,128]{2,1,0:T(8,128)(2,1)S(1)}, bf16[8,256,128]{2,1,0:T(8,128)(2,1)}, u32[]{:S(2)}) copy-start(bf16[8,256,128]{2,1,0:T(8,128)(2,1)} %copy-done.11) | copy-start | bytes 1572868
  76.0 14.8 %copy-start.14 = (bf16[256,256]{1,0:T(8,128)(2,1)S(1)}, bf16[256,256]{1,0:T(8,128)(2,1)}, u32[]{:S(2)}) copy-start(bf16[256,256]{1,0:T(8,128)(2,1)} %wo_ref.1) | copy-start | bytes 393220
  76.0 14.8 %all-to-all-start.2 = ((bf16[8,8,32,128]{3,2,1,0:T(8,128)(2,1)}), bf16[8,8,32,128]{3,2,1,0:T(8,128)(2,1)S(1)}, u32[]{:S(2)}, u32[]{:S(2)}) async-start(bf16[8,8,32,128]{3,2,1,0:T(8,128)(2,1)} %copy-done.5), calls=%async_computation.2 | async-start | bytes 1048576 | tf_op jit(solution)/shard_map/all_to_all | solution.py:484
  93.4 5.8 %collective-permute-start.10 = (bf16[264,128]{1,0:T(8,128)(2,1)S(1)}, bf16[264,128]{1,0:T(8,128)(2,1)S(1)}, u32[]{:S(2)}, u32[]{:S(2)}) collective-permute-start(bf16[264,128]{1,0:T(8,128)(2,1)S(1)} %get-tuple-element.14), channel_id=1, source_target_pairs={{0,128},{128,0},{1,129},{129,1},{2,130},{130,2},{3,131},{131,3},{4... | collective-permute-start | bytes 202760 | tf_op jit(solution)/shard_map/ppermute | solution.py:493
  99.2 15.2 %collective-permute-start.14 = (bf16[2,264,128]{2,1,0:T(8,128)(2,1)S(1)}, bf16[2,264,128]{2,1,0:T(8,128)(2,1)S(1)}, u32[]{:S(2)}, u32[]{:S(2)}) collective-permute-start(bf16[2,264,128]{2,1,0:T(8,128)(2,1)S(1)} %pad_maximum_fusion), channel_id=1, source_target_pairs={{0,96},{16,112},{32,0},{48,16},{64,32},{80,48},{96,64},{112,80},{1... | collective-permute-start | bytes 405512 | tf_op jit(solution)/shard_map/ppermute | solution.py:491
  103.2 14.9 %collective-permute-start.13 = (bf16[2,264,128]{2,1,0:T(8,128)(2,1)S(1)}, bf16[2,264,128]{2,1,0:T(8,128)(2,1)S(1)}, u32[]{:S(2)}, u32[]{:S(2)}) collective-permute-start(bf16[2,264,128]{2,1,0:T(8,128)(2,1)S(1)} %pad_maximum_fusion), channel_id=1, source_target_pairs={{0,32},{16,48},{32,64},{48,80},{64,96},{80,112},{96,0},{112,16},{1... | collective-permute-start | bytes 405512 | tf_op jit(solution)/shard_map/ppermute | solution.py:491
  103.2 18.6 %collective-permute-start.11 = (bf16[2,264,128]{2,1,0:T(8,128)(2,1)S(1)}, bf16[2,264,128]{2,1,0:T(8,128)(2,1)S(1)}, u32[]{:S(2)}, u32[]{:S(2)}) collective-permute-start(bf16[2,264,128]{2,1,0:T(8,128)(2,1)S(1)} %pad_maximum_fusion), channel_id=1, source_target_pairs={{0,16},{16,32},{32,48},{48,64},{64,80},{80,96},{96,112},{112,0},{1... | collective-permute-start | bytes 405512 | tf_op jit(solution)/shard_map/ppermute | solution.py:491
  104.5 9.8 %all-to-all-start.3 = ((bf16[8,48,128]{2,1,0:T(8,128)(2,1)}), bf16[8,48,128]{2,1,0:T(8,128)(2,1)S(1)}, u32[]{:S(2)}, u32[]{:S(2)}) async-start(bf16[8,48,128]{2,1,0:T(8,128)(2,1)} %get-tuple-element.13), calls=%async_computation.3 | async-start | bytes 196608 | tf_op jit(solution)/shard_map/all_to_all | solution.py:484
  107.9 13.9 %collective-permute-start.12 = (bf16[2,264,128]{2,1,0:T(8,128)(2,1)S(1)}, bf16[2,264,128]{2,1,0:T(8,128)(2,1)S(1)}, u32[]{:S(2)}, u32[]{:S(2)}) collective-permute-start(bf16[2,264,128]{2,1,0:T(8,128)(2,1)S(1)} %pad_maximum_fusion), channel_id=1, source_target_pairs={{0,112},{16,0},{32,16},{48,32},{64,48},{80,64},{96,80},{112,96},{1... | collective-permute-start | bytes 405512 | tf_op jit(solution)/shard_map/ppermute | solution.py:491
  114.4 12.5 %collective-permute-start.18 = (bf16[1,264,128]{2,1,0:T(8,128)(2,1)S(1)}, bf16[1,264,128]{2,1,0:T(8,128)(2,1)S(1)}, u32[]{:S(2)}, u32[]{:S(2)}) collective-permute-start(bf16[1,264,128]{2,1,0:T(8,128)(2,1)S(1)} %slice.65), channel_id=1, source_target_pairs={{0,96},{16,112},{32,0},{48,16},{64,32},{80,48},{96,64},{112,80},{1... | collective-permute-start | bytes 202760 | tf_op jit(solution)/shard_map/ppermute | solution.py:491
  118.1 8.7 %collective-permute-start.17 = (bf16[1,264,128]{2,1,0:T(8,128)(2,1)S(1)}, bf16[1,264,128]{2,1,0:T(8,128)(2,1)S(1)}, u32[]{:S(2)}, u32[]{:S(2)}) collective-permute-start(bf16[1,264,128]{2,1,0:T(8,128)(2,1)S(1)} %slice.64), channel_id=1, source_target_pairs={{0,32},{16,48},{32,64},{48,80},{64,96},{80,112},{96,0},{112,16},{1... | collective-permute-start | bytes 202760 | tf_op jit(solution)/shard_map/ppermute | solution.py:491
  118.2 6.2 %collective-permute-start.15 = (bf16[2,264,128]{2,1,0:T(8,128)(2,1)S(1)}, bf16[2,264,128]{2,1,0:T(8,128)(2,1)S(1)}, u32[]{:S(2)}, u32[]{:S(2)}) collective-permute-start(bf16[2,264,128]{2,1,0:T(8,128)(2,1)S(1)} %collective-permute-done.13), channel_id=1, source_target_pairs={{0,16},{16,32},{32,48},{48,64},{64,80},{80,96},{96,112},{112,0},{1... | collective-permute-start | bytes 405512 | tf_op jit(solution)/shard_map/ppermute | solution.py:491
  121.8 5.0 %collective-permute-start.16 = (bf16[2,264,128]{2,1,0:T(8,128)(2,1)S(1)}, bf16[2,264,128]{2,1,0:T(8,128)(2,1)S(1)}, u32[]{:S(2)}, u32[]{:S(2)}) collective-permute-start(bf16[2,264,128]{2,1,0:T(8,128)(2,1)S(1)} %collective-permute-done.14), channel_id=1, source_target_pairs={{0,112},{16,0},{32,16},{48,32},{64,48},{80,64},{96,80},{112,96},{1... | collective-permute-start | bytes 405512 | tf_op jit(solution)/shard_map/ppermute | solution.py:491
  126.9 19.8 %copy-start.7 = (bf16[8,2,264,128]{3,2,1,0:T(8,128)(2,1)}, bf16[8,2,264,128]{3,2,1,0:T(8,128)(2,1)S(1)}, u32[]{:S(2)}) copy-start(bf16[8,2,264,128]{3,2,1,0:T(8,128)(2,1)S(1)} %fusion.8.mine_ref) | copy-start | bytes 3244036
  126.9 35.9 %collective-permute-start.19 = (bf16[8,2,264,128]{3,2,1,0:T(8,128)(2,1)S(1)}, bf16[8,2,264,128]{3,2,1,0:T(8,128)(2,1)S(1)}, u32[]{:S(2)}, u32[]{:S(2)}) collective-permute-start(bf16[8,2,264,128]{3,2,1,0:T(8,128)(2,1)S(1)} %fusion.8.mine_ref), channel_id=1, source_target_pairs={{0,8},{8,0},{1,9},{9,1},{2,10},{10,2},{3,11},{11,3},{4,12},{12,4},... | collective-permute-start | bytes 3244040 | tf_op jit(solution)/shard_map/ppermute | solution.py:480
  128.0 17.7 %all-to-all-start.4 = ((bf16[32,16,128]{2,1,0:T(8,128)(2,1)}), bf16[32,16,128]{2,1,0:T(8,128)(2,1)S(1)}, u32[]{:S(2)}, u32[]{:S(2)}) async-start(bf16[32,16,128]{2,1,0:T(8,128)(2,1)} %pad_maximum_fusion.2), calls=%async_computation.4 | async-start | bytes 262144 | tf_op jit(solution)/shard_map/all_to_all | solution.py:484
  145.7 5.3 %copy-start.16 = (bf16[1024,128]{1,0:T(8,128)(2,1)S(1)}, bf16[1024,128]{1,0:T(8,128)(2,1)}, u32[]{:S(2)}) copy-start(bf16[1024,128]{1,0:T(8,128)(2,1)} %param.20) | copy-start | bytes 786436
  146.7 13.7 %all-to-all-start.5 = ((bf16[8,9,32,128]{3,2,1,0:T(8,128)(2,1)}), bf16[8,9,32,128]{3,2,1,0:T(8,128)(2,1)}, u32[]{:S(2)}, u32[]{:S(2)}) async-start(bf16[8,9,32,128]{3,2,1,0:T(8,128)(2,1)} %broadcast_in_dim.8), calls=%async_computation.5 | async-start | bytes 1179648 | tf_op jit(solution)/shard_map/all_to_all | solution.py:484
  160.4 3.4 %copy-start.8 = (bf16[8,2,264,128]{3,2,1,0:T(8,128)(2,1)S(1)}, bf16[8,2,264,128]{3,2,1,0:T(8,128)(2,1)}, u32[]{:S(2)}) copy-start(bf16[8,2,264,128]{3,2,1,0:T(8,128)(2,1)} %copy-done.7) | copy-start | bytes 3244036
  160.4 3.4 %copy-start.13 = (bf16[128,512]{0,1:T(8,128)(2,1)S(1)}, bf16[128,512]{0,1:T(8,128)(2,1)}, u32[]{:S(2)}) copy-start(bf16[128,512]{0,1:T(8,128)(2,1)} %copy.52) | copy-start | bytes 393220
  162.8 1.0 copy-start.9
  163.8 1.2 copy-start.10
  237.2 2.7 collective-permute-start.20
  243.9 7.1 %copy-start.18 = (bf16[128,128]{1,0:T(8,128)(2,1)S(1)}, bf16[128,128]{1,0:T(8,128)(2,1)}, u32[]{:S(2)}) copy-start(bf16[128,128]{1,0:T(8,128)(2,1)} %param.22) | copy-start | bytes 98308
  243.9 7.2 %copy-start.19 = (bf16[128,128]{1,0:T(8,128)(2,1)S(1)}, bf16[128,128]{1,0:T(8,128)(2,1)}, u32[]{:S(2)}) copy-start(bf16[128,128]{1,0:T(8,128)(2,1)} %param.23) | copy-start | bytes 98308
  243.9 39.1 %all-to-all-start.7 = ((bf16[128,32,128]{2,1,0:T(8,128)(2,1)}), bf16[128,32,128]{2,1,0:T(8,128)(2,1)S(1)}, u32[]{:S(2)}, u32[]{:S(2)}) async-start(bf16[128,32,128]{2,1,0:T(8,128)(2,1)} %bitcast.49), calls=%async_computation.7 | async-start | bytes 2097152 | tf_op jit(solution)/shard_map/all_to_all | solution.py:484
  255.2 1.3 copy-start.2
  283.0 1.6 copy-start.3
  (1 other events, 0.8 us)

commit v4 on v3

--- a/solution.py
+++ b/solution.py
@@ -42,6 +42,41 @@
 
 def whole(shape):
     return pl.BlockSpec(shape, lambda *_: (0,) * len(shape))
+
+
+def bias_kernel(x_ref, w_ref, out_ref, hold_ref):
+    step = pl.program_id(0)
+    rows, lanes, channels = x_ref.shape
+    heads, pair_rows, _ = out_ref.shape
+    normed = standardize(x_ref[...].reshape(rows * lanes, channels), -1).astype(BF16)
+    bias = dot(w_ref[...], normed, (1, 1))
+    for i in range(rows):
+        hold_ref[pl.ds(step * rows + i, heads, stride=pair_rows), :] = bias[
+            :, i * lanes : (i + 1) * lanes
+        ]
+
+    @pl.when(step == pl.num_programs(0) - 1)
+    def _():
+        out_ref[...] = hold_ref[...].astype(BF16).reshape(heads, pair_rows, lanes)
+
+
+def pair_bias(couple, weights):
+    pair_rows, lanes, channels = couple.shape
+    heads = weights.shape[1]
+    rows = 8
+    return pl.pallas_call(
+        bias_kernel,
+        grid=(pair_rows // rows,),
+        in_specs=[
+            pl.BlockSpec((rows, lanes, channels), lambda t: (t, 0, 0)),
+            whole((heads, channels)),
+        ],
+        out_specs=whole((heads, pair_rows, lanes)),
+        out_shape=jax.ShapeDtypeStruct((heads, pair_rows, lanes), BF16),
+        scratch_shapes=[pltpu.VMEM((heads * pair_rows, lanes), F32)],
+        compiler_params=params(16),
+        name="pair_bias",
+    )(couple, weights.T)
 
 
 def project_kernel(heads, width, x_ref, w_ref, qkv_ref, gate_ref):
@@ -133,7 +168,7 @@
 
 def attend(at, qkv, mine, other, pen, width):
     columns, entries, _, lanes = qkv.shape
-    take = 2
+    take = 4
     return pl.pallas_call(
         functools.partial(attend_kernel, width),
         grid_spec=pltpu.PrefetchScalarGridSpec(
@@ -147,7 +182,7 @@
             ],
         ),
         out_shape=jax.ShapeDtypeStruct((columns, entries, width, lanes), BF16),
-        compiler_params=params(32),
+        compiler_params=params(48),
         name="attend",
     )(at, qkv, mine, other, pen)
 
@@ -241,13 +276,14 @@
 
 
 def outer_kernel(
-    side, at_ref, left_ref, lmask_ref, mine_ref, other_ref, couple_ref, live_ref, we_ref, wt_ref,
+    side, at_ref, left_ref, mine_ref, other_ref, couple_ref, live_ref, we_ref, wt_ref,
     mid_ref, l_ref, r_ref, right_ref, rmask_ref, rows_ref, x_ref, update_ref, count_ref,
 ):
     step = pl.program_id(0)
     rows, lanes = couple_ref.shape[0], couple_ref.shape[1]
     channels = couple_ref.shape[2]
     pair_rows = live_ref.shape[0]
+    entries = rmask_ref.shape[0]
 
     @pl.when(step == 0)
     def _():
@@ -266,9 +302,18 @@
                 else:
                     rmask_ref[at, :] = pair
 
-        count_ref[...] = 1.0 / (dot(lmask_ref[...], rmask_ref[...], (0, 0)) + 1.0)
-        for t in range(left_ref.shape[0]):
-            rows_ref[t * 128 : (t + 1) * 128] = left_ref[t].T
+        columns, tiles, members, _ = left_ref.shape
+        given = lax.broadcasted_iota(jnp.int32, (entries, entries), 0)
+        wanted = lax.broadcasted_iota(jnp.int32, (entries, entries), 1)
+        member = jnp.bitwise_xor(given % members, at_ref[0])
+        order = jnp.where(member * columns + given // members == wanted, 1.0, 0.0).astype(BF16)
+        for t in range(tiles):
+            rows_in = jnp.concatenate([left_ref[c, t] for c in range(columns)], axis=0)
+            turned = dot(rows_in, order, (0, 0)).astype(BF16)
+            if t < tiles - 1:
+                rows_ref[t * 128 : (t + 1) * 128] = turned
+            else:
+                count_ref[...] = 1.0 / (dot(turned, rmask_ref[...], (1, 0)) + 1.0)
 
     @pl.when(step < OUTER_CHUNKS)
     def _():
@@ -310,8 +355,8 @@
                 ref[i] = (both[:, i * lanes : (i + 1) * lanes] * live).astype(BF16)
 
 
-def outer(at, left, lmask, mine, other, couple, live, w_exit, w_tri):
-    _, entries, _ = left.shape
+def outer(at, left, mine, other, couple, live, w_exit, w_tri):
+    entries = left.shape[0] * left.shape[2]
     pair_rows, lanes, channels = couple.shape
     rows = 8
     side = mine.shape[2] // 8 - 1
@@ -327,7 +372,6 @@
             grid=(OUTER_CHUNKS + pair_rows // rows,),
             in_specs=[
                 whole(left.shape),
-                whole(lmask.shape),
                 whole(mine.shape),
                 whole(other.shape),
                 pl.BlockSpec((rows, lanes, channels), move),
@@ -352,7 +396,7 @@
         ],
         compiler_params=params(40),
         name="outer",
-    )(at, left, lmask, mine, other, couple, live, w_exit, w_tri.T)
+    )(at, left, mine, other, couple, live, w_exit, w_tri.T)
 
 
 def triangle_kernel(me_ref, l_ref, mine_ref, other_ref, out_ref):
@@ -536,10 +580,7 @@
     live_cols = lax.dynamic_slice_in_dim(live, lax.axis_index("chan") * pair_cols, pair_cols)
     penalty = ((live - 1.0) * MASKED)[None, :]
 
-    pair_norm = standardize(couple_tensor, -1).astype(BF16)
-    bias = jnp.einsum(
-        "ijc,ch->hij", pair_norm, couple_offset_coefficients, preferred_element_type=F32
-    ).astype(BF16)
+    bias = pair_bias(couple_tensor, couple_offset_coefficients)
     bias = exchange(bias, "chan")
     bias = ring_gather(bias)
     bias_other = swap(bias)
@@ -571,15 +612,11 @@
         axis=1,
     )
     left = exchange(left, BRANCH_ROW)
-    left = left[:, : steps + 1].reshape(planes, 2, steps + 1, 128)
-    left = jnp.where(core == 0, left, left[:, ::-1]).reshape(members, steps + 1, 128)
-    left = repeated(left.transpose(1, 0, 2), chan)
+    left = repeated(left[:, : steps + 1].transpose(1, 0, 2), chan)
     left = exchange(left, "chan")
-    left = left.transpose(1, 2, 0, 3).reshape(steps + 1, members * chan, 128)
     mid, left_tri, right_tri = outer(
         at,
-        left[:steps],
-        left[steps],
+        left,
         right,
         right_other,
         couple_tensor,

time: 290 us -> 283 us (0.976)
  blocking collectives: 72.2 us -> 89.5 us
  starting transfers between devices: 63.7 us -> 53.9 us
  local copies, waits for them, and re-layouts: 22.4 us -> 15.5 us
  other arithmetic: 6.12 us -> 1.12 us
    all_to_all x2 -> x3, blocking collectives: 72.2 us -> 89.5 us  [exchange(): return lax.all_to_all(x, axes, 0, 0, tiled=True)]
    all_to_all x6 -> x5, starting transfers between devices: 30.2 us -> 21.6 us  [exchange(): return lax.all_to_all(x, axes, 0, 0, tiled=True)]
    all_to_all x6 -> x5, waiting for transfers between devices: 61.5 us -> 55.6 us  [exchange(): return lax.all_to_all(x, axes, 0, 0, tiled=True)]
    ppermute x16, waiting for transfers between devices: 4.96 us -> 8.78 us  [shift(): lax.ppermute(y, 'row_0', tuple(((k, (k + by) % n) for k in range(n))))]
    reduce_sum x2 -> x0, other arithmetic: 2.96 us -> none  [the longest x1 1.66 us: standardize(): centered = values - jnp.mean(values, axis=axis, keepdims=True)]
    unnamed x60 -> x64, local copies, waits for them, and re-layouts: 15.1 us -> 12.3 us
  transfers between devices with their start and end apart: 27 -> 26, of which waited for: 12 -> 13; matrix products, arithmetic and copies ran while one was open for 5% -> 1% of each run, Pallas kernels for 2% -> 2%
where the time goes in v4:
time: 283 us; the launch traced here: 281 us
  blocking collectives  89.5 us (32%)
  waiting for transfers between devices  73.1 us (26%)
  starting transfers between devices  53.9 us (19%)
  Pallas kernels  47 us (17%)
  local copies, waits for them, and re-layouts  15.5 us (5%)
    all_to_all x3, blocking collectives, exchange(): return lax.all_to_all(x, axes, 0, 0, tiled=True)  89.5 us
    all_to_all x5, waiting for transfers between devices, exchange(): return lax.all_to_all(x, axes, 0, 0, tiled=True)  55.6 us
    ppermute x16, starting transfers between devices, shift(): lax.ppermute(y, 'row_0', tuple(((k, (k + by) % n) for k in range(n))))  26.5 us
    all_to_all x5, starting transfers between devices, exchange(): return lax.all_to_all(x, axes, 0, 0, tiled=True)  21.6 us
    pallas_call x1, Pallas kernels, attend(): pl.pallas_call(functools.partial(attend_kernel, width), grid_spec=pltpu.P...  17.5 us
    unnamed x64, local copies, waits for them, and re-layouts  12.3 us
    pallas_call x1, Pallas kernels, outer(): pl.pallas_call(functools.partial(outer_kernel, side), grid_spec=pltpu.Pre...  11.1 us
    ppermute x16, waiting for transfers between devices, shift(): lax.ppermute(y, 'row_0', tuple(((k, (k + by) % n) for k in range(n))))  8.78 us
  transfers between devices with their start and end apart: 26, of which 13 were waited for; matrix products, arithmetic and copies ran while one was open for 1% of the time, Pallas kernels for 2%

profile of v4, /device:TPU:32, one launch (start us, length us, event | category | flops | bytes accessed | tf_op | source)
XLA Modules:
  0.0 281.3 jit_solution(13537615252822713782)
XLA Ops:
  0.6 1.2 copy-done.2
  2.5 2.0 pair_bias.1
  4.5 11.5 %all_to_all.40 = bf16[8,32,128]{2,1,0:T(8,128)(2,1)S(1)} all-to-all(bf16[8,32,128]{2,1,0:T(8,128)(2,1)S(1)} %pair_bias.1), channel_id=1, replica_groups=mesh['branch'=2,'row_0'=8,'row_1'=2,'chan'=8] {'chan'}, dimensions={0} | all-to-all | bytes 131072 | tf_op jit(solution)/shard_map/all_to_all | solution.py:528
  16.1 2.7 collective-permute-start
  18.8 3.0 %collective-permute-done = bf16[8,32,128]{2,1,0:T(8,128)(2,1)S(1)} collective-permute-done((bf16[8,32,128]{2,1,0:T(8,128)(2,1)S(1)}, bf16[8,32,128]{2,1,0:T(8,128)(2,1)S(1)}, u32[]{:S(2)}, u32[]{:S(2)}) %collective-permute-start) | collective-permute-done | bytes 65568 | tf_op jit(solution)/shard_map/ppermute | solution.py:537
  22.5 5.4 %collective-permute-start.4 = (bf16[2,8,32,128]{3,2,1,0:T(8,128)(2,1)}, bf16[2,8,32,128]{3,2,1,0:T(8,128)(2,1)S(1)}, u32[]{:S(2)}, u32[]{:S(2)}) collective-permute-start(bf16[2,8,32,128]{3,2,1,0:T(8,128)(2,1)} %pad_maximum_fusion.1), channel_id=1, source_target_pairs={{0,96},{16,112},{32,0},{48,16},{64,32},{80,48},{96,64},{112,80},{1... | collective-permute-start | bytes 393224 | tf_op jit(solution)/shard_map/ppermute | solution.py:535
  27.9 1.0 collective-permute-start.1
  29.1 2.3 project_msa.1
  31.4 1.2 copy-done.7
  33.3 3.6 %all-to-all-start = ((bf16[8,8,96,128]{3,2,1,0:T(8,128)(2,1)}), bf16[8,8,96,128]{3,2,1,0:T(8,128)(2,1)S(1)}, u32[]{:S(2)}, u32[]{:S(2)}) async-start(bf16[8,8,96,128]{3,2,1,0:T(8,128)(2,1)} %copy-done.7), calls=%async_computation | async-start | bytes 3145728 | tf_op jit(solution)/shard_map/all_to_all | solution.py:528
  36.9 1.1 collective-permute-start.2
  38.1 4.2 %collective-permute-start.8 = (bf16[1,8,32,128]{3,2,1,0:T(8,128)(2,1)S(1)}, bf16[1,8,32,128]{3,2,1,0:T(8,128)(2,1)S(1)}, u32[]{:S(2)}, u32[]{:S(2)}) collective-permute-start(bf16[1,8,32,128]{3,2,1,0:T(8,128)(2,1)S(1)} %slice.45), channel_id=1, source_target_pairs={{0,96},{16,112},{32,0},{48,16},{64,32},{80,48},{96,64},{112,80},{1... | collective-permute-start | bytes 196616 | tf_op jit(solution)/shard_map/ppermute | solution.py:535
  42.4 1.0 collective-permute-start.5
  43.4 1.1 collective-permute-start.6
  44.5 0.9 bitcast_dynamic-update-slice_fusion.12
  45.5 2.0 collective-permute-done.5
  48.4 1.1 collective-permute-done.7
  49.9 4.5 %all-to-all-done.qkv_ref = bf16[8,8,96,128]{3,2,1,0:T(8,128)(2,1)S(1)} async-done(((bf16[8,8,96,128]{3,2,1,0:T(8,128)(2,1)}), bf16[8,8,96,128]{3,2,1,0:T(8,128)(2,1)S(1)}, u32[]{:S(2)}, u32[]{:S(2)}) %all-to-all-start) | async-done | bytes 1572896 | tf_op jit(solution)/shard_map/all_to_all | solution.py:528
  54.4 17.5 %attend.1 = bf16[8,8,32,128]{3,2,1,0:T(8,128)(2,1)} custom-call(s32[4]{0:T(128)S(1)} %pad_add_fusion.at_ref, bf16[8,8,96,128]{3,2,1,0:T(8,128)(2,1)S(1)} %all-to-all-done.qkv_ref, bf16[8,2,8,32,128]{4,3,2,1,0:T(8,128)(2,1)S(1)} %fusion.1.mine_ref, bf16[8,2,8,32,128]{4,3,2,1,0:T(8,128)(2,1)} %collective-permute-done.9.other_ref, f32[1,1024]{1,0:T(1,128)S(1)} %bitcast.83), custom_call_target="tpu_custom_call" | custom-call | tf_op jit(solution)/shard_map/attend/pallas_call | solution.py:172
  71.9 3.8 %all-to-all-start.2 = ((bf16[8,8,32,128]{3,2,1,0:T(8,128)(2,1)}), bf16[8,8,32,128]{3,2,1,0:T(8,128)(2,1)S(1)}, u32[]{:S(2)}, u32[]{:S(2)}) async-start(bf16[8,8,32,128]{3,2,1,0:T(8,128)(2,1)} %attend.1), calls=%async_computation.2 | async-start | bytes 1048576 | tf_op jit(solution)/shard_map/all_to_all | solution.py:528
  75.9 9.6 %all-to-all-done.2.att_ref = bf16[8,8,32,128]{3,2,1,0:T(8,128)(2,1)S(1)} async-done(((bf16[8,8,32,128]{3,2,1,0:T(8,128)(2,1)}), bf16[8,8,32,128]{3,2,1,0:T(8,128)(2,1)S(1)}, u32[]{:S(2)}, u32[]{:S(2)}) %all-to-all-start.2) | async-done | bytes 524320 | tf_op jit(solution)/shard_map/all_to_all | solution.py:528
  85.5 2.6 sides.1
  88.1 2.7 collective-permute-start.10
  90.8 3.1 %collective-permute-done.10 = bf16[264,128]{1,0:T(8,128)(2,1)S(1)} collective-permute-done((bf16[264,128]{1,0:T(8,128)(2,1)S(1)}, bf16[264,128]{1,0:T(8,128)(2,1)S(1)}, u32[]{:S(2)}, u32[]{:S(2)}) %collective-permute-start.10) | collective-permute-done | bytes 67616 | tf_op jit(solution)/shard_map/ppermute | solution.py:537
  93.9 3.4 %collective-permute-start.14 = (bf16[2,264,128]{2,1,0:T(8,128)(2,1)S(1)}, bf16[2,264,128]{2,1,0:T(8,128)(2,1)S(1)}, u32[]{:S(2)}, u32[]{:S(2)}) collective-permute-start(bf16[2,264,128]{2,1,0:T(8,128)(2,1)S(1)} %pad_maximum_fusion), channel_id=1, source_target_pairs={{0,96},{16,112},{32,0},{48,16},{64,32},{80,48},{96,64},{112,80},{1... | collective-permute-start | bytes 405512 | tf_op jit(solution)/shard_map/ppermute | solution.py:535
  97.3 1.9 collective-permute-start.11
  99.2 3.4 %all-to-all-start.3 = ((bf16[8,48,128]{2,1,0:T(8,128)(2,1)}), bf16[8,48,128]{2,1,0:T(8,128)(2,1)S(1)}, u32[]{:S(2)}, u32[]{:S(2)}) async-start(bf16[8,48,128]{2,1,0:T(8,128)(2,1)} %get-tuple-element.13), calls=%async_computation.3 | async-start | bytes 196608 | tf_op jit(solution)/shard_map/all_to_all | solution.py:528
  102.8 6.2 %all-to-all-done.3 = bf16[8,48,128]{2,1,0:T(8,128)(2,1)S(1)} async-done(((bf16[8,48,128]{2,1,0:T(8,128)(2,1)}), bf16[8,48,128]{2,1,0:T(8,128)(2,1)S(1)}, u32[]{:S(2)}, u32[]{:S(2)}) %all-to-all-start.3) | async-done | bytes 98336 | tf_op jit(solution)/shard_map/all_to_all | solution.py:528
  109.0 2.8 collective-permute-start.18
  112.3 3.8 %collective-permute-start.15 = (bf16[2,264,128]{2,1,0:T(8,128)(2,1)S(1)}, bf16[2,264,128]{2,1,0:T(8,128)(2,1)S(1)}, u32[]{:S(2)}, u32[]{:S(2)}) collective-permute-start(bf16[2,264,128]{2,1,0:T(8,128)(2,1)S(1)} %collective-permute-done.13), channel_id=1, source_target_pairs={{0,16},{16,32},{32,48},{48,64},{64,80},{80,96},{96,112},{112,0},{1... | collective-permute-start | bytes 405512 | tf_op jit(solution)/shard_map/ppermute | solution.py:535
  116.2 2.4 collective-permute-done.15
  118.7 2.4 collective-permute-done.16
  121.4 17.4 %all_to_all.41 = bf16[32,16,128]{2,1,0:T(8,128)(2,1)S(1)} all-to-all(bf16[32,16,128]{2,1,0:T(8,128)(2,1)S(1)} %pad_maximum_fusion.2), channel_id=1, replica_groups=mesh['branch'=2,'row_0'=8,'row_1'=2,'chan'=8] {'branch','row_0','row_1'}, dimensions={0} | all-to-all | bytes 262144 | tf_op jit(solution)/shard_map/all_to_all | solution.py:528
  139.8 3.7 %all-to-all-start.5 = ((bf16[8,9,32,128]{3,2,1,0:T(8,128)(2,1)}), bf16[8,9,32,128]{3,2,1,0:T(8,128)(2,1)S(1)}, u32[]{:S(2)}, u32[]{:S(2)}) async-start(bf16[8,9,32,128]{3,2,1,0:T(8,128)(2,1)} %broadcast_in_dim.8), calls=%async_computation.5 | async-start | bytes 1179648 | tf_op jit(solution)/shard_map/all_to_all | solution.py:528
  144.1 8.8 %all-to-all-done.5.left_ref = bf16[8,9,32,128]{3,2,1,0:T(8,128)(2,1)S(1)} async-done(((bf16[8,9,32,128]{3,2,1,0:T(8,128)(2,1)}), bf16[8,9,32,128]{3,2,1,0:T(8,128)(2,1)S(1)}, u32[]{:S(2)}, u32[]{:S(2)}) %all-to-all-start.5) | async-done | bytes 589856 | tf_op jit(solution)/shard_map/all_to_all | solution.py:528
  153.7 1.1 copy-done.5
  154.8 1.2 copy-done.9
  156.7 11.1 %outer.1 = (f32[32,128,128]{2,1,0:T(8,128)S(1)}, bf16[32,128,128]{2,1,0:T(8,128)(2,1)S(1)}, bf16[32,128,128]{2,1,0:T(8,128)(2,1)S(1)}) custom-call(s32[4]{0:T(128)S(1)} %copy-done.14, bf16[8,9,32,128]{3,2,1,0:T(8,128)(2,1)S(1)} %copy-done.5, bf16[8,2,264,128]{3,2,1,0:T(8,128)(2,1)S(1)} %copy-done.9, ...), custom_call_target="tpu_custom_call" | custom-call | tf_op jit(solution)/shard_map/outer/pallas_call | solution.py:368
  168.0 1.4 copy.50
  169.4 60.5 %all_to_all.42 = bf16[128,2,32,128]{3,2,1,0:T(8,128)(2,1)S(1)} all-to-all(bf16[128,2,32,128]{3,2,1,0:T(8,128)(2,1)S(1)} %copy.50), channel_id=1, replica_groups=mesh['branch'=2,'row_0'=8,'row_1'=2,'chan'=8] {'branch','row_0','chan'}, dimensions={0} | all-to-all | bytes 4194304 | tf_op jit(solution)/shard_map/all_to_all | solution.py:528
  230.4 2.6 collective-permute-done.20.other_ref
  233.0 3.9 %triangle.1 = bf16[16,8,32,128]{3,2,1,0:T(8,128)(2,1)} custom-call(s32[1]{0:T(128)} %bitcast.me_ref, bf16[16,8,32,128]{3,2,1,0:T(8,128)(2,1)S(1)} %bitcast.72, bf16[16,8,32,128]{3,2,1,0:T(8,128)(2,1)S(1)} %bitcast.71, bf16[16,8,32,128]{3,2,1,0:T(8,128)(2,1)S(1)} %collective-permute-done.20.other_ref), custom_call_target="tpu_custom_call" | custom-call | tf_op jit(solution)/shard_map/triangle/pallas_call | solution.py:427
  237.0 7.1 %all-to-all-start.7 = ((bf16[128,32,128]{2,1,0:T(8,128)(2,1)}), bf16[128,32,128]{2,1,0:T(8,128)(2,1)S(1)}, u32[]{:S(2)}, u32[]{:S(2)}) async-start(bf16[128,32,128]{2,1,0:T(8,128)(2,1)} %bitcast.43), calls=%async_computation.7 | async-start | bytes 2097152 | tf_op jit(solution)/shard_map/all_to_all | solution.py:528
  244.3 3.9 %switch.1.gate_ref = f32[32,128,128]{2,1,0:T(8,128)S(1)} custom-call(f32[32,128,128]{2,1,0:T(8,128)S(1)} %get-tuple-element.17.mid_ref, bf16[128,128]{1,0:T(8,128)(2,1)S(1)} %bitcast.81), custom_call_target="tpu_custom_call" | custom-call | tf_op jit(solution)/shard_map/switch/pallas_call | solution.py:452
  248.2 1.3 copy-done
  249.6 26.4 %all-to-all-done.7.prod_ref = bf16[128,32,128]{2,1,0:T(8,128)(2,1)S(1)} async-done(((bf16[128,32,128]{2,1,0:T(8,128)(2,1)}), bf16[128,32,128]{2,1,0:T(8,128)(2,1)S(1)}, u32[]{:S(2)}, u32[]{:S(2)}) %all-to-all-start.7) | async-done | bytes 1048608 | tf_op jit(solution)/shard_map/all_to_all | solution.py:528
  276.0 1.6 copy-done.1
  277.6 3.7 %finish.1 = bf16[32,128,128]{2,1,0:T(8,128)(2,1)} custom-call(bf16[128,32,128]{2,1,0:T(8,128)(2,1)S(1)} %all-to-all-done.7.prod_ref, f32[32,128,128]{2,1,0:T(8,128)S(1)} %get-tuple-element.17.mid_ref, f32[32,128,128]{2,1,0:T(8,128)S(1)} %copy-done.1, bf16[128,128]{1,0:T(8,128)(2,1)S(1)} %bitcast.80), custom_call_target="tpu_custom_call" | custom-call | tf_op jit(solution)/shard_map/finish/pallas_call | solution.py:511
  (111 shorter events, 9.0 us)
Async XLA Ops:
  0.6 1.2 copy-start.2
  2.5 26.4 %copy-start.16 = (bf16[256,1024]{1,0:T(8,128)(2,1)S(1)}, bf16[256,1024]{1,0:T(8,128)(2,1)}, u32[]{:S(2)}) copy-start(bf16[256,1024]{1,0:T(8,128)(2,1)} %param.16) | copy-start | bytes 1572868
  2.5 26.6 %copy-start.6 = (bf16[8,128,256]{2,1,0:T(8,128)(2,1)S(1)}, bf16[8,128,256]{2,1,0:T(8,128)(2,1)}, u32[]{:S(2)}) copy-start(bf16[8,128,256]{2,1,0:T(8,128)(2,1)} %stack_ref.1) | copy-start | bytes 1572868
  16.1 5.8 %collective-permute-start = (bf16[8,32,128]{2,1,0:T(8,128)(2,1)S(1)}, bf16[8,32,128]{2,1,0:T(8,128)(2,1)S(1)}, u32[]{:S(2)}, u32[]{:S(2)}) collective-permute-start(bf16[8,32,128]{2,1,0:T(8,128)(2,1)S(1)} %all_to_all.40), channel_id=1, source_target_pairs={{0,128},{128,0},{1,129},{129,1},{2,130},{130,2},{3,131},{131,3},{4... | collective-permute-start | bytes 196616 | tf_op jit(solution)/shard_map/ppermute | solution.py:537
  22.5 15.6 %collective-permute-start.4 = (bf16[2,8,32,128]{3,2,1,0:T(8,128)(2,1)}, bf16[2,8,32,128]{3,2,1,0:T(8,128)(2,1)S(1)}, u32[]{:S(2)}, u32[]{:S(2)}) collective-permute-start(bf16[2,8,32,128]{3,2,1,0:T(8,128)(2,1)} %pad_maximum_fusion.1), channel_id=1, source_target_pairs={{0,96},{16,112},{32,0},{48,16},{64,32},{80,48},{96,64},{112,80},{1... | collective-permute-start | bytes 393224 | tf_op jit(solution)/shard_map/ppermute | solution.py:535
  27.9 14.4 %collective-permute-start.3 = (bf16[2,8,32,128]{3,2,1,0:T(8,128)(2,1)}, bf16[2,8,32,128]{3,2,1,0:T(8,128)(2,1)S(1)}, u32[]{:S(2)}, u32[]{:S(2)}) collective-permute-start(bf16[2,8,32,128]{3,2,1,0:T(8,128)(2,1)} %pad_maximum_fusion.1), channel_id=1, source_target_pairs={{0,32},{16,48},{32,64},{48,80},{64,96},{80,112},{96,0},{112,16},{1... | collective-permute-start | bytes 393224 | tf_op jit(solution)/shard_map/ppermute | solution.py:535
  27.9 15.5 %collective-permute-start.1 = (bf16[2,8,32,128]{3,2,1,0:T(8,128)(2,1)}, bf16[2,8,32,128]{3,2,1,0:T(8,128)(2,1)}, u32[]{:S(2)}, u32[]{:S(2)}) collective-permute-start(bf16[2,8,32,128]{3,2,1,0:T(8,128)(2,1)} %pad_maximum_fusion.1), channel_id=1, source_target_pairs={{0,16},{16,32},{32,48},{48,64},{64,80},{80,96},{96,112},{112,0},{1... | collective-permute-start | bytes 393224 | tf_op jit(solution)/shard_map/ppermute | solution.py:535
  31.4 1.2 copy-start.7
  32.6 0.8 copy-start.10
  33.3 21.1 %all-to-all-start = ((bf16[8,8,96,128]{3,2,1,0:T(8,128)(2,1)}), bf16[8,8,96,128]{3,2,1,0:T(8,128)(2,1)S(1)}, u32[]{:S(2)}, u32[]{:S(2)}) async-start(bf16[8,8,96,128]{3,2,1,0:T(8,128)(2,1)} %copy-done.7), calls=%async_computation | async-start | bytes 3145728 | tf_op jit(solution)/shard_map/all_to_all | solution.py:528
  36.9 8.5 %collective-permute-start.2 = (bf16[2,8,32,128]{3,2,1,0:T(8,128)(2,1)}, bf16[2,8,32,128]{3,2,1,0:T(8,128)(2,1)S(1)}, u32[]{:S(2)}, u32[]{:S(2)}) collective-permute-start(bf16[2,8,32,128]{3,2,1,0:T(8,128)(2,1)} %pad_maximum_fusion.1), channel_id=1, source_target_pairs={{0,112},{16,0},{32,16},{48,32},{64,48},{80,64},{96,80},{112,96},{1... | collective-permute-start | bytes 393224 | tf_op jit(solution)/shard_map/ppermute | solution.py:535
  38.1 11.8 %copy-start.22 = (s32[1024]{0:T(1024)S(1)}, s32[1024]{0:T(1024)}, u32[]{:S(2)}) copy-start(s32[1024]{0:T(1024)} %param.14) | copy-start | bytes 12292
  38.1 10.3 %collective-permute-start.8 = (bf16[1,8,32,128]{3,2,1,0:T(8,128)(2,1)S(1)}, bf16[1,8,32,128]{3,2,1,0:T(8,128)(2,1)S(1)}, u32[]{:S(2)}, u32[]{:S(2)}) collective-permute-start(bf16[1,8,32,128]{3,2,1,0:T(8,128)(2,1)S(1)} %slice.45), channel_id=1, source_target_pairs={{0,96},{16,112},{32,0},{48,16},{64,32},{80,48},{96,64},{112,80},{1... | collective-permute-start | bytes 196616 | tf_op jit(solution)/shard_map/ppermute | solution.py:535
  42.3 7.2 %collective-permute-start.7 = (bf16[1,8,32,128]{3,2,1,0:T(8,128)(2,1)S(1)}, bf16[1,8,32,128]{3,2,1,0:T(8,128)(2,1)S(1)}, u32[]{:S(2)}, u32[]{:S(2)}) collective-permute-start(bf16[1,8,32,128]{3,2,1,0:T(8,128)(2,1)S(1)} %slice.44), channel_id=1, source_target_pairs={{0,32},{16,48},{32,64},{48,80},{64,96},{80,112},{96,0},{112,16},{1... | collective-permute-start | bytes 196616 | tf_op jit(solution)/shard_map/ppermute | solution.py:535
  42.4 5.1 %collective-permute-start.5 = (bf16[2,8,32,128]{3,2,1,0:T(8,128)(2,1)S(1)}, bf16[2,8,32,128]{3,2,1,0:T(8,128)(2,1)S(1)}, u32[]{:S(2)}, u32[]{:S(2)}) collective-permute-start(bf16[2,8,32,128]{3,2,1,0:T(8,128)(2,1)S(1)} %collective-permute-done.3), channel_id=1, source_target_pairs={{0,16},{16,32},{32,48},{48,64},{64,80},{80,96},{96,112},{112,0},{1... | collective-permute-start | bytes 393224 | tf_op jit(solution)/shard_map/ppermute | solution.py:535
  43.4 5.0 %collective-permute-start.6 = (bf16[2,8,32,128]{3,2,1,0:T(8,128)(2,1)S(1)}, bf16[2,8,32,128]{3,2,1,0:T(8,128)(2,1)S(1)}, u32[]{:S(2)}, u32[]{:S(2)}) collective-permute-start(bf16[2,8,32,128]{3,2,1,0:T(8,128)(2,1)S(1)} %collective-permute-done.4), channel_id=1, source_target_pairs={{0,112},{16,0},{32,16},{48,32},{64,48},{80,64},{96,80},{112,96},{1... | collective-permute-start | bytes 393224 | tf_op jit(solution)/shard_map/ppermute | solution.py:535
  49.5 4.9 %collective-permute-start.9 = (bf16[8,2,8,32,128]{4,3,2,1,0:T(8,128)(2,1)S(1)}, bf16[8,2,8,32,128]{4,3,2,1,0:T(8,128)(2,1)}, u32[]{:S(2)}, u32[]{:S(2)}) collective-permute-start(bf16[8,2,8,32,128]{4,3,2,1,0:T(8,128)(2,1)S(1)} %fusion.1.mine_ref), channel_id=1, source_target_pairs={{0,8},{8,0},{1,9},{9,1},{2,10},{10,2},{3,11},{11,3},{4,12},{12,4},... | collective-permute-start | bytes 3145736 | tf_op jit(solution)/shard_map/ppermute | solution.py:524
  49.9 22.1 %copy-start.13 = (s32[4]{0:T(128)}, s32[4]{0:T(128)S(1)}, u32[]{:S(2)}) copy-start(s32[4]{0:T(128)S(1)} %pad_add_fusion.at_ref) | copy-start | bytes 52
  54.4 21.4 %copy-start.23 = (s32[8,128]{1,0:T(8,128)S(1)}, s32[8,128]{1,0:T(8,128)}, u32[]{:S(2)}) copy-start(s32[8,128]{1,0:T(8,128)} %param.15) | copy-start | bytes 12292
  54.4 21.4 %copy-start.19 = (bf16[256,64]{0,1:T(8,128)(2,1)S(1)}, bf16[256,64]{0,1:T(8,128)(2,1)}, u32[]{:S(2)}) copy-start(bf16[256,64]{0,1:T(8,128)(2,1)} %param.19) | copy-start | bytes 98308
  71.9 13.6 %copy-start.11 = (bf16[8,256,128]{2,1,0:T(8,128)(2,1)S(1)}, bf16[8,256,128]{2,1,0:T(8,128)(2,1)}, u32[]{:S(2)}) copy-start(bf16[8,256,128]{2,1,0:T(8,128)(2,1)} %copy-done.10) | copy-start | bytes 1572868
  71.9 13.6 %copy-start.12 = (bf16[256,256]{1,0:T(8,128)(2,1)S(1)}, bf16[256,256]{1,0:T(8,128)(2,1)}, u32[]{:S(2)}) copy-start(bf16[256,256]{1,0:T(8,128)(2,1)} %wo_ref.1) | copy-start | bytes 393220
  71.9 13.6 %all-to-all-start.2 = ((bf16[8,8,32,128]{3,2,1,0:T(8,128)(2,1)}), bf16[8,8,32,128]{3,2,1,0:T(8,128)(2,1)S(1)}, u32[]{:S(2)}, u32[]{:S(2)}) async-start(bf16[8,8,32,128]{3,2,1,0:T(8,128)(2,1)} %attend.1), calls=%async_computation.2 | async-start | bytes 1048576 | tf_op jit(solution)/shard_map/all_to_all | solution.py:528
  88.1 5.8 %collective-permute-start.10 = (bf16[264,128]{1,0:T(8,128)(2,1)S(1)}, bf16[264,128]{1,0:T(8,128)(2,1)S(1)}, u32[]{:S(2)}, u32[]{:S(2)}) collective-permute-start(bf16[264,128]{1,0:T(8,128)(2,1)S(1)} %get-tuple-element.14), channel_id=1, source_target_pairs={{0,128},{128,0},{1,129},{129,1},{2,130},{130,2},{3,131},{131,3},{4... | collective-permute-start | bytes 202760 | tf_op jit(solution)/shard_map/ppermute | solution.py:537
  93.9 15.1 %collective-permute-start.14 = (bf16[2,264,128]{2,1,0:T(8,128)(2,1)S(1)}, bf16[2,264,128]{2,1,0:T(8,128)(2,1)S(1)}, u32[]{:S(2)}, u32[]{:S(2)}) collective-permute-start(bf16[2,264,128]{2,1,0:T(8,128)(2,1)S(1)} %pad_maximum_fusion), channel_id=1, source_target_pairs={{0,96},{16,112},{32,0},{48,16},{64,32},{80,48},{96,64},{112,80},{1... | collective-permute-start | bytes 405512 | tf_op jit(solution)/shard_map/ppermute | solution.py:535
  97.3 14.5 %collective-permute-start.13 = (bf16[2,264,128]{2,1,0:T(8,128)(2,1)S(1)}, bf16[2,264,128]{2,1,0:T(8,128)(2,1)S(1)}, u32[]{:S(2)}, u32[]{:S(2)}) collective-permute-start(bf16[2,264,128]{2,1,0:T(8,128)(2,1)S(1)} %pad_maximum_fusion), channel_id=1, source_target_pairs={{0,32},{16,48},{32,64},{48,80},{64,96},{80,112},{96,0},{112,16},{1... | collective-permute-start | bytes 405512 | tf_op jit(solution)/shard_map/ppermute | solution.py:535
  97.3 18.9 %collective-permute-start.11 = (bf16[2,264,128]{2,1,0:T(8,128)(2,1)S(1)}, bf16[2,264,128]{2,1,0:T(8,128)(2,1)S(1)}, u32[]{:S(2)}, u32[]{:S(2)}) collective-permute-start(bf16[2,264,128]{2,1,0:T(8,128)(2,1)S(1)} %pad_maximum_fusion), channel_id=1, source_target_pairs={{0,16},{16,32},{32,48},{48,64},{64,80},{80,96},{96,112},{112,0},{1... | collective-permute-start | bytes 405512 | tf_op jit(solution)/shard_map/ppermute | solution.py:535
  99.2 9.8 %all-to-all-start.3 = ((bf16[8,48,128]{2,1,0:T(8,128)(2,1)}), bf16[8,48,128]{2,1,0:T(8,128)(2,1)S(1)}, u32[]{:S(2)}, u32[]{:S(2)}) async-start(bf16[8,48,128]{2,1,0:T(8,128)(2,1)} %get-tuple-element.13), calls=%async_computation.3 | async-start | bytes 196608 | tf_op jit(solution)/shard_map/all_to_all | solution.py:528
  102.5 13.6 %collective-permute-start.12 = (bf16[2,264,128]{2,1,0:T(8,128)(2,1)S(1)}, bf16[2,264,128]{2,1,0:T(8,128)(2,1)S(1)}, u32[]{:S(2)}, u32[]{:S(2)}) collective-permute-start(bf16[2,264,128]{2,1,0:T(8,128)(2,1)S(1)} %pad_maximum_fusion), channel_id=1, source_target_pairs={{0,112},{16,0},{32,16},{48,32},{64,48},{80,64},{96,80},{112,96},{1... | collective-permute-start | bytes 405512 | tf_op jit(solution)/shard_map/ppermute | solution.py:535
  109.0 12.1 %collective-permute-start.18 = (bf16[1,264,128]{2,1,0:T(8,128)(2,1)S(1)}, bf16[1,264,128]{2,1,0:T(8,128)(2,1)S(1)}, u32[]{:S(2)}, u32[]{:S(2)}) collective-permute-start(bf16[1,264,128]{2,1,0:T(8,128)(2,1)S(1)} %slice.50), channel_id=1, source_target_pairs={{0,96},{16,112},{32,0},{48,16},{64,32},{80,48},{96,64},{112,80},{1... | collective-permute-start | bytes 202760 | tf_op jit(solution)/shard_map/ppermute | solution.py:535
  111.8 9.4 %collective-permute-start.17 = (bf16[1,264,128]{2,1,0:T(8,128)(2,1)S(1)}, bf16[1,264,128]{2,1,0:T(8,128)(2,1)S(1)}, u32[]{:S(2)}, u32[]{:S(2)}) collective-permute-start(bf16[1,264,128]{2,1,0:T(8,128)(2,1)S(1)} %slice.49), channel_id=1, source_target_pairs={{0,32},{16,48},{32,64},{48,80},{64,96},{80,112},{96,0},{112,16},{1... | collective-permute-start | bytes 202760 | tf_op jit(solution)/shard_map/ppermute | solution.py:535
  112.3 6.3 %collective-permute-start.15 = (bf16[2,264,128]{2,1,0:T(8,128)(2,1)S(1)}, bf16[2,264,128]{2,1,0:T(8,128)(2,1)S(1)}, u32[]{:S(2)}, u32[]{:S(2)}) collective-permute-start(bf16[2,264,128]{2,1,0:T(8,128)(2,1)S(1)} %collective-permute-done.13), channel_id=1, source_target_pairs={{0,16},{16,32},{32,48},{48,64},{64,80},{80,96},{96,112},{112,0},{1... | collective-permute-start | bytes 405512 | tf_op jit(solution)/shard_map/ppermute | solution.py:535
  116.1 5.0 %collective-permute-start.16 = (bf16[2,264,128]{2,1,0:T(8,128)(2,1)S(1)}, bf16[2,264,128]{2,1,0:T(8,128)(2,1)S(1)}, u32[]{:S(2)}, u32[]{:S(2)}) collective-permute-start(bf16[2,264,128]{2,1,0:T(8,128)(2,1)S(1)} %collective-permute-done.14), channel_id=1, source_target_pairs={{0,112},{16,0},{32,16},{48,32},{64,48},{80,64},{96,80},{112,96},{1... | collective-permute-start | bytes 405512 | tf_op jit(solution)/shard_map/ppermute | solution.py:535
  121.2 18.6 %copy-start.8 = (bf16[8,2,264,128]{3,2,1,0:T(8,128)(2,1)}, bf16[8,2,264,128]{3,2,1,0:T(8,128)(2,1)S(1)}, u32[]{:S(2)}) copy-start(bf16[8,2,264,128]{3,2,1,0:T(8,128)(2,1)S(1)} %fusion.mine_ref) | copy-start | bytes 3244036
  121.2 32.5 %collective-permute-start.19 = (bf16[8,2,264,128]{3,2,1,0:T(8,128)(2,1)S(1)}, bf16[8,2,264,128]{3,2,1,0:T(8,128)(2,1)}, u32[]{:S(2)}, u32[]{:S(2)}) collective-permute-start(bf16[8,2,264,128]{3,2,1,0:T(8,128)(2,1)S(1)} %fusion.mine_ref), channel_id=1, source_target_pairs={{0,8},{8,0},{1,9},{9,1},{2,10},{10,2},{3,11},{11,3},{4,12},{12,4},... | collective-permute-start | bytes 3244040 | tf_op jit(solution)/shard_map/ppermute | solution.py:524
  138.8 4.8 %copy-start.17 = (bf16[1024,128]{1,0:T(8,128)(2,1)S(1)}, bf16[1024,128]{1,0:T(8,128)(2,1)}, u32[]{:S(2)}) copy-start(bf16[1024,128]{1,0:T(8,128)(2,1)} %param.20) | copy-start | bytes 786436
  139.8 4.1 %copy-start.18 = (bf16[128,512]{1,0:T(8,128)(2,1)S(1)}, bf16[128,512]{1,0:T(8,128)(2,1)}, u32[]{:S(2)}) copy-start(bf16[128,512]{1,0:T(8,128)(2,1)} %param.21) | copy-start | bytes 393220
  139.8 14.0 %copy-start.3 = (bf16[32,128,128]{2,1,0:T(8,128)(2,1)S(1)}, bf16[32,128,128]{2,1,0:T(8,128)(2,1)}, u32[]{:S(2)}) copy-start(bf16[32,128,128]{2,1,0:T(8,128)(2,1)} %couple_ref.1) | copy-start | bytes 3145732
  139.8 13.1 %all-to-all-start.5 = ((bf16[8,9,32,128]{3,2,1,0:T(8,128)(2,1)}), bf16[8,9,32,128]{3,2,1,0:T(8,128)(2,1)S(1)}, u32[]{:S(2)}, u32[]{:S(2)}) async-start(bf16[8,9,32,128]{3,2,1,0:T(8,128)(2,1)} %broadcast_in_dim.8), calls=%async_computation.5 | async-start | bytes 1179648 | tf_op jit(solution)/shard_map/all_to_all | solution.py:528
  152.9 0.8 copy-start.4
  153.7 1.1 copy-start.5
  154.8 1.2 copy-start.9
  230.3 2.7 collective-permute-start.20
  237.0 7.1 %copy-start.20 = (bf16[128,128]{1,0:T(8,128)(2,1)S(1)}, bf16[128,128]{1,0:T(8,128)(2,1)}, u32[]{:S(2)}) copy-start(bf16[128,128]{1,0:T(8,128)(2,1)} %param.22) | copy-start | bytes 98308
  237.0 7.2 %copy-start.21 = (bf16[128,128]{1,0:T(8,128)(2,1)S(1)}, bf16[128,128]{1,0:T(8,128)(2,1)}, u32[]{:S(2)}) copy-start(bf16[128,128]{1,0:T(8,128)(2,1)} %param.23) | copy-start | bytes 98308
  237.0 39.1 %all-to-all-start.7 = ((bf16[128,32,128]{2,1,0:T(8,128)(2,1)}), bf16[128,32,128]{2,1,0:T(8,128)(2,1)S(1)}, u32[]{:S(2)}, u32[]{:S(2)}) async-start(bf16[128,32,128]{2,1,0:T(8,128)(2,1)} %bitcast.43), calls=%async_computation.7 | async-start | bytes 2097152 | tf_op jit(solution)/shard_map/all_to_all | solution.py:528
  248.2 1.4 copy-start
  276.0 1.6 copy-start.1
  (2 other events, 1.3 us)

commit v5 on v4

--- a/solution.py
+++ b/solution.py
@@ -74,7 +74,7 @@
         out_specs=whole((heads, pair_rows, lanes)),
         out_shape=jax.ShapeDtypeStruct((heads, pair_rows, lanes), BF16),
         scratch_shapes=[pltpu.VMEM((heads * pair_rows, lanes), F32)],
-        compiler_params=params(16),
+        compiler_params=params(60),
         name="pair_bias",
     )(couple, weights.T)
 
@@ -272,7 +272,7 @@
     )
 
 
-OUTER_CHUNKS = 4
+OUTER_CHUNKS = 2
 
 
 def outer_kernel(
@@ -394,7 +394,7 @@
             jax.ShapeDtypeStruct((pair_rows, channels, lanes), BF16),
             jax.ShapeDtypeStruct((pair_rows, channels, lanes), BF16),
         ],
-        compiler_params=params(40),
+        compiler_params=params(60),
         name="outer",
     )(at, left, mine, other, couple, live, w_exit, w_tri.T)
 
@@ -534,7 +534,8 @@
     def shift(y, by):
         return lax.ppermute(y, "row_0", tuple((k, (k + by) % n) for k in range(n)))
 
-    pair = jnp.stack([x, lax.ppermute(x, "branch", SWAP)])
+    across = lax.ppermute(x, "branch", SWAP)
+    pair = jnp.stack([x, across])
     above, below, above_2, below_2 = (shift(pair, by) for by in (1, -1, 2, -2))
     above_3, below_3 = shift(above_2, 1), shift(below_2, -1)
     last = [shift(above_2[:1], 2), shift(below_2[1:], -2)]

time: 283 us -> 284 us (level)
  Pallas kernels: 47 us -> 50.8 us
  local copies, waits for them, and re-layouts: 15.5 us -> 12 us
    unnamed x64 -> x54, local copies, waits for them, and re-layouts: 12.3 us -> 8.08 us
  transfers between devices with their start and end apart: 26 -> 26, of which waited for: 13 -> 13; matrix products, arithmetic and copies ran while one was open for 1% -> 2% of each run, Pallas kernels for 2% -> 2%
where the time goes in v5:
time: 284 us; the launch traced here: 282 us
  blocking collectives  89.7 us (32%)
  waiting for transfers between devices  71.2 us (25%)
  starting transfers between devices  54.2 us (19%)
  Pallas kernels  50.8 us (18%)
  local copies, waits for them, and re-layouts  12 us (4%)
  other arithmetic  3.26 us (1%)
    all_to_all x3, blocking collectives, exchange(): return lax.all_to_all(x, axes, 0, 0, tiled=True)  89.7 us
    all_to_all x5, waiting for transfers between devices, exchange(): return lax.all_to_all(x, axes, 0, 0, tiled=True)  53.7 us
    ppermute x16, starting transfers between devices, shift(): lax.ppermute(y, 'row_0', tuple(((k, (k + by) % n) for k in range(n))))  26.5 us
    all_to_all x5, starting transfers between devices, exchange(): return lax.all_to_all(x, axes, 0, 0, tiled=True)  21.6 us
    pallas_call x1, Pallas kernels, attend(): pl.pallas_call(functools.partial(attend_kernel, width), grid_spec=pltpu.P...  17.5 us
    pallas_call x1, Pallas kernels, outer(): pl.pallas_call(functools.partial(outer_kernel, side), grid_spec=pltpu.Pre...  12.8 us
    ppermute x16, waiting for transfers between devices, shift(): lax.ppermute(y, 'row_0', tuple(((k, (k + by) % n) for k in range(n))))  8.78 us
    unnamed x54, local copies, waits for them, and re-layouts  8.08 us
  transfers between devices with their start and end apart: 26, of which 13 were waited for; matrix products, arithmetic and copies ran while one was open for 2% of the time, Pallas kernels for 2%

profile of v5, /device:TPU:32, one launch (start us, length us, event | category | flops | bytes accessed | tf_op | source)
XLA Modules:
  0.0 282.3 jit_solution(11797962326079924812)
XLA Ops:
  0.6 4.1 %pair_bias.1 = bf16[8,32,128]{2,1,0:T(8,128)(2,1)} custom-call(bf16[32,128,128]{2,1,0:T(8,128)(2,1)} %couple_ref.1, bf16[8,128]{1,0:T(8,128)(2,1)} %bitcast.95), custom_call_target="tpu_custom_call" | custom-call | tf_op jit(solution)/shard_map/pair_bias/pallas_call | solution.py:67
  4.8 11.7 %all_to_all.40 = bf16[8,32,128]{2,1,0:T(8,128)(2,1)S(1)} all-to-all(bf16[8,32,128]{2,1,0:T(8,128)(2,1)} %pair_bias.1), channel_id=1, replica_groups=mesh['branch'=2,'row_0'=8,'row_1'=2,'chan'=8] {'chan'}, dimensions={0} | all-to-all | bytes 131072 | tf_op jit(solution)/shard_map/all_to_all | solution.py:528
  16.5 2.7 collective-permute-start
  19.2 3.0 %collective-permute-done = bf16[8,32,128]{2,1,0:T(8,128)(2,1)S(1)} collective-permute-done((bf16[8,32,128]{2,1,0:T(8,128)(2,1)S(1)}, bf16[8,32,128]{2,1,0:T(8,128)(2,1)S(1)}, u32[]{:S(2)}, u32[]{:S(2)}) %collective-permute-start) | collective-permute-done | bytes 65568 | tf_op jit(solution)/shard_map/ppermute | solution.py:537
  23.0 5.4 %collective-permute-start.4 = (bf16[2,8,32,128]{3,2,1,0:T(8,128)(2,1)}, bf16[2,8,32,128]{3,2,1,0:T(8,128)(2,1)S(1)}, u32[]{:S(2)}, u32[]{:S(2)}) collective-permute-start(bf16[2,8,32,128]{3,2,1,0:T(8,128)(2,1)} %pad_maximum_fusion.1), channel_id=1, source_target_pairs={{0,96},{16,112},{32,0},{48,16},{64,32},{80,48},{96,64},{112,80},{1... | collective-permute-start | bytes 393224 | tf_op jit(solution)/shard_map/ppermute | solution.py:535
  28.4 1.0 collective-permute-start.1
  29.6 2.2 project_msa.1
  31.8 1.2 copy-done.4
  33.8 3.6 %all-to-all-start = ((bf16[8,8,96,128]{3,2,1,0:T(8,128)(2,1)}), bf16[8,8,96,128]{3,2,1,0:T(8,128)(2,1)S(1)}, u32[]{:S(2)}, u32[]{:S(2)}) async-start(bf16[8,8,96,128]{3,2,1,0:T(8,128)(2,1)} %copy-done.4), calls=%async_computation | async-start | bytes 3145728 | tf_op jit(solution)/shard_map/all_to_all | solution.py:528
  37.4 1.1 collective-permute-start.2
  38.5 4.2 %collective-permute-start.8 = (bf16[1,8,32,128]{3,2,1,0:T(8,128)(2,1)S(1)}, bf16[1,8,32,128]{3,2,1,0:T(8,128)(2,1)S(1)}, u32[]{:S(2)}, u32[]{:S(2)}) collective-permute-start(bf16[1,8,32,128]{3,2,1,0:T(8,128)(2,1)S(1)} %slice.45), channel_id=1, source_target_pairs={{0,96},{16,112},{32,0},{48,16},{64,32},{80,48},{96,64},{112,80},{1... | collective-permute-start | bytes 196616 | tf_op jit(solution)/shard_map/ppermute | solution.py:535
  42.8 1.0 collective-permute-start.5
  43.9 1.1 collective-permute-start.6
  45.0 0.9 bitcast_dynamic-update-slice_fusion.12
  46.0 2.0 collective-permute-done.5
  48.0 0.9 collective-permute-done.6
  48.9 1.1 collective-permute-done.7
  50.3 4.5 %all-to-all-done.qkv_ref = bf16[8,8,96,128]{3,2,1,0:T(8,128)(2,1)S(1)} async-done(((bf16[8,8,96,128]{3,2,1,0:T(8,128)(2,1)}), bf16[8,8,96,128]{3,2,1,0:T(8,128)(2,1)S(1)}, u32[]{:S(2)}, u32[]{:S(2)}) %all-to-all-start) | async-done | bytes 1572896 | tf_op jit(solution)/shard_map/all_to_all | solution.py:528
  54.9 17.5 %attend.1 = bf16[8,8,32,128]{3,2,1,0:T(8,128)(2,1)} custom-call(s32[4]{0:T(128)S(1)} %pad_add_fusion.at_ref, bf16[8,8,96,128]{3,2,1,0:T(8,128)(2,1)S(1)} %all-to-all-done.qkv_ref, bf16[8,2,8,32,128]{4,3,2,1,0:T(8,128)(2,1)S(1)} %fusion.1.mine_ref, bf16[8,2,8,32,128]{4,3,2,1,0:T(8,128)(2,1)} %collective-permute-done.9.other_ref, f32[1,1024]{1,0:T(1,128)S(1)} %bitcast.79), custom_call_target="tpu_custom_call" | custom-call | tf_op jit(solution)/shard_map/attend/pallas_call | solution.py:172
  72.4 3.8 %all-to-all-start.2 = ((bf16[8,8,32,128]{3,2,1,0:T(8,128)(2,1)}), bf16[8,8,32,128]{3,2,1,0:T(8,128)(2,1)S(1)}, u32[]{:S(2)}, u32[]{:S(2)}) async-start(bf16[8,8,32,128]{3,2,1,0:T(8,128)(2,1)} %attend.1), calls=%async_computation.2 | async-start | bytes 1048576 | tf_op jit(solution)/shard_map/all_to_all | solution.py:528
  76.4 9.6 %all-to-all-done.2.att_ref = bf16[8,8,32,128]{3,2,1,0:T(8,128)(2,1)S(1)} async-done(((bf16[8,8,32,128]{3,2,1,0:T(8,128)(2,1)}), bf16[8,8,32,128]{3,2,1,0:T(8,128)(2,1)S(1)}, u32[]{:S(2)}, u32[]{:S(2)}) %all-to-all-start.2) | async-done | bytes 524320 | tf_op jit(solution)/shard_map/all_to_all | solution.py:528
  85.9 2.6 sides.1
  88.5 2.7 collective-permute-start.10
  91.2 3.1 %collective-permute-done.10 = bf16[264,128]{1,0:T(8,128)(2,1)S(1)} collective-permute-done((bf16[264,128]{1,0:T(8,128)(2,1)S(1)}, bf16[264,128]{1,0:T(8,128)(2,1)S(1)}, u32[]{:S(2)}, u32[]{:S(2)}) %collective-permute-start.10) | collective-permute-done | bytes 67616 | tf_op jit(solution)/shard_map/ppermute | solution.py:537
  94.3 3.4 %collective-permute-start.14 = (bf16[2,264,128]{2,1,0:T(8,128)(2,1)S(1)}, bf16[2,264,128]{2,1,0:T(8,128)(2,1)S(1)}, u32[]{:S(2)}, u32[]{:S(2)}) collective-permute-start(bf16[2,264,128]{2,1,0:T(8,128)(2,1)S(1)} %pad_maximum_fusion), channel_id=1, source_target_pairs={{0,96},{16,112},{32,0},{48,16},{64,32},{80,48},{96,64},{112,80},{1... | collective-permute-start | bytes 405512 | tf_op jit(solution)/shard_map/ppermute | solution.py:535
  97.7 1.9 collective-permute-start.11
  99.6 3.4 %all-to-all-start.3 = ((bf16[8,48,128]{2,1,0:T(8,128)(2,1)}), bf16[8,48,128]{2,1,0:T(8,128)(2,1)S(1)}, u32[]{:S(2)}, u32[]{:S(2)}) async-start(bf16[8,48,128]{2,1,0:T(8,128)(2,1)} %get-tuple-element.13), calls=%async_computation.3 | async-start | bytes 196608 | tf_op jit(solution)/shard_map/all_to_all | solution.py:528
  103.2 6.2 %all-to-all-done.3 = bf16[8,48,128]{2,1,0:T(8,128)(2,1)S(1)} async-done(((bf16[8,48,128]{2,1,0:T(8,128)(2,1)}), bf16[8,48,128]{2,1,0:T(8,128)(2,1)S(1)}, u32[]{:S(2)}, u32[]{:S(2)}) %all-to-all-start.3) | async-done | bytes 98336 | tf_op jit(solution)/shard_map/all_to_all | solution.py:528
  109.4 2.8 collective-permute-start.18
  112.8 3.8 %collective-permute-start.15 = (bf16[2,264,128]{2,1,0:T(8,128)(2,1)S(1)}, bf16[2,264,128]{2,1,0:T(8,128)(2,1)S(1)}, u32[]{:S(2)}, u32[]{:S(2)}) collective-permute-start(bf16[2,264,128]{2,1,0:T(8,128)(2,1)S(1)} %collective-permute-done.13), channel_id=1, source_target_pairs={{0,16},{16,32},{32,48},{48,64},{64,80},{80,96},{96,112},{112,0},{1... | collective-permute-start | bytes 405512 | tf_op jit(solution)/shard_map/ppermute | solution.py:535
  116.7 2.4 collective-permute-done.15
  119.1 2.4 collective-permute-done.16
  121.8 17.4 %all_to_all.41 = bf16[32,16,128]{2,1,0:T(8,128)(2,1)S(1)} all-to-all(bf16[32,16,128]{2,1,0:T(8,128)(2,1)S(1)} %pad_maximum_fusion.2), channel_id=1, replica_groups=mesh['branch'=2,'row_0'=8,'row_1'=2,'chan'=8] {'branch','row_0','row_1'}, dimensions={0} | all-to-all | bytes 262144 | tf_op jit(solution)/shard_map/all_to_all | solution.py:528
  139.3 0.9 broadcast_in_dim.8
  140.2 3.7 %all-to-all-start.5 = ((bf16[8,9,32,128]{3,2,1,0:T(8,128)(2,1)}), bf16[8,9,32,128]{3,2,1,0:T(8,128)(2,1)S(1)}, u32[]{:S(2)}, u32[]{:S(2)}) async-start(bf16[8,9,32,128]{3,2,1,0:T(8,128)(2,1)} %broadcast_in_dim.8), calls=%async_computation.5 | async-start | bytes 1179648 | tf_op jit(solution)/shard_map/all_to_all | solution.py:528
  146.4 6.9 %all-to-all-done.5.left_ref = bf16[8,9,32,128]{3,2,1,0:T(8,128)(2,1)S(1)} async-done(((bf16[8,9,32,128]{3,2,1,0:T(8,128)(2,1)}), bf16[8,9,32,128]{3,2,1,0:T(8,128)(2,1)S(1)}, u32[]{:S(2)}, u32[]{:S(2)}) %all-to-all-start.5) | async-done | bytes 589856 | tf_op jit(solution)/shard_map/all_to_all | solution.py:528
  154.2 12.8 %outer.1 = (f32[32,128,128]{2,1,0:T(8,128)}, bf16[32,128,128]{2,1,0:T(8,128)(2,1)}, bf16[32,128,128]{2,1,0:T(8,128)(2,1)}) custom-call(s32[4]{0:T(128)} %copy-done.8, bf16[8,9,32,128]{3,2,1,0:T(8,128)(2,1)} %copy-done.9, bf16[8,2,264,128]{3,2,1,0:T(8,128)(2,1)} %copy-done.10, bf16[8,2,264,128]{3,2,1,0:T(8,128)(2,1)} %collective-permute-done.19.other_ref, ...), custom_call_target="tpu_custom_call" | custom-call | tf_op jit(solution)/shard_map/outer/pallas_call | solution.py:368
  166.9 1.7 maximum_bitcast_fusion
  168.7 1.4 copy.50
  170.0 60.5 %all_to_all.42 = bf16[128,2,32,128]{3,2,1,0:T(8,128)(2,1)S(1)} all-to-all(bf16[128,2,32,128]{3,2,1,0:T(8,128)(2,1)S(1)} %copy.50), channel_id=1, replica_groups=mesh['branch'=2,'row_0'=8,'row_1'=2,'chan'=8] {'branch','row_0','chan'}, dimensions={0} | all-to-all | bytes 4194304 | tf_op jit(solution)/shard_map/all_to_all | solution.py:528
  231.3 2.6 collective-permute-done.20.other_ref
  233.9 3.9 %triangle.1 = bf16[16,8,32,128]{3,2,1,0:T(8,128)(2,1)} custom-call(s32[1]{0:T(128)} %bitcast.me_ref, bf16[16,8,32,128]{3,2,1,0:T(8,128)(2,1)S(1)} %bitcast.72, bf16[16,8,32,128]{3,2,1,0:T(8,128)(2,1)S(1)} %bitcast.71, bf16[16,8,32,128]{3,2,1,0:T(8,128)(2,1)S(1)} %collective-permute-done.20.other_ref), custom_call_target="tpu_custom_call" | custom-call | tf_op jit(solution)/shard_map/triangle/pallas_call | solution.py:427
  237.9 7.1 %all-to-all-start.7 = ((bf16[128,32,128]{2,1,0:T(8,128)(2,1)}), bf16[128,32,128]{2,1,0:T(8,128)(2,1)S(1)}, u32[]{:S(2)}, u32[]{:S(2)}) async-start(bf16[128,32,128]{2,1,0:T(8,128)(2,1)} %bitcast.43), calls=%async_computation.7 | async-start | bytes 2097152 | tf_op jit(solution)/shard_map/all_to_all | solution.py:528
  245.2 3.9 %switch.1.gate_ref = f32[32,128,128]{2,1,0:T(8,128)S(1)} custom-call(f32[32,128,128]{2,1,0:T(8,128)S(1)} %copy-done, bf16[128,128]{1,0:T(8,128)(2,1)S(1)} %bitcast.77), custom_call_target="tpu_custom_call" | custom-call | tf_op jit(solution)/shard_map/switch/pallas_call | solution.py:452
  249.2 1.3 copy-done.1
  250.5 26.5 %all-to-all-done.7.prod_ref = bf16[128,32,128]{2,1,0:T(8,128)(2,1)S(1)} async-done(((bf16[128,32,128]{2,1,0:T(8,128)(2,1)}), bf16[128,32,128]{2,1,0:T(8,128)(2,1)S(1)}, u32[]{:S(2)}, u32[]{:S(2)}) %all-to-all-start.7) | async-done | bytes 1048608 | tf_op jit(solution)/shard_map/all_to_all | solution.py:528
  277.0 1.6 copy-done.2
  278.6 3.7 %finish.1 = bf16[32,128,128]{2,1,0:T(8,128)(2,1)} custom-call(bf16[128,32,128]{2,1,0:T(8,128)(2,1)S(1)} %all-to-all-done.7.prod_ref, f32[32,128,128]{2,1,0:T(8,128)S(1)} %copy-done, f32[32,128,128]{2,1,0:T(8,128)S(1)} %copy-done.2, bf16[128,128]{1,0:T(8,128)(2,1)S(1)} %bitcast.76), custom_call_target="tpu_custom_call" | custom-call | tf_op jit(solution)/shard_map/finish/pallas_call | solution.py:511
  (101 shorter events, 7.9 us)
Async XLA Ops:
  0.6 28.7 %copy-start.11 = (bf16[256,1024]{1,0:T(8,128)(2,1)S(1)}, bf16[256,1024]{1,0:T(8,128)(2,1)}, u32[]{:S(2)}) copy-start(bf16[256,1024]{1,0:T(8,128)(2,1)} %param.16) | copy-start | bytes 1572868
  0.6 28.9 %copy-start.3 = (bf16[8,128,256]{2,1,0:T(8,128)(2,1)S(1)}, bf16[8,128,256]{2,1,0:T(8,128)(2,1)}, u32[]{:S(2)}) copy-start(bf16[8,128,256]{2,1,0:T(8,128)(2,1)} %stack_ref.1) | copy-start | bytes 1572868
  16.5 5.8 %collective-permute-start = (bf16[8,32,128]{2,1,0:T(8,128)(2,1)S(1)}, bf16[8,32,128]{2,1,0:T(8,128)(2,1)S(1)}, u32[]{:S(2)}, u32[]{:S(2)}) collective-permute-start(bf16[8,32,128]{2,1,0:T(8,128)(2,1)S(1)} %all_to_all.40), channel_id=1, source_target_pairs={{0,128},{128,0},{1,129},{129,1},{2,130},{130,2},{3,131},{131,3},{4... | collective-permute-start | bytes 196616 | tf_op jit(solution)/shard_map/ppermute | solution.py:537
  23.0 15.6 %collective-permute-start.4 = (bf16[2,8,32,128]{3,2,1,0:T(8,128)(2,1)}, bf16[2,8,32,128]{3,2,1,0:T(8,128)(2,1)S(1)}, u32[]{:S(2)}, u32[]{:S(2)}) collective-permute-start(bf16[2,8,32,128]{3,2,1,0:T(8,128)(2,1)} %pad_maximum_fusion.1), channel_id=1, source_target_pairs={{0,96},{16,112},{32,0},{48,16},{64,32},{80,48},{96,64},{112,80},{1... | collective-permute-start | bytes 393224 | tf_op jit(solution)/shard_map/ppermute | solution.py:535
  28.4 14.4 %collective-permute-start.3 = (bf16[2,8,32,128]{3,2,1,0:T(8,128)(2,1)}, bf16[2,8,32,128]{3,2,1,0:T(8,128)(2,1)S(1)}, u32[]{:S(2)}, u32[]{:S(2)}) collective-permute-start(bf16[2,8,32,128]{3,2,1,0:T(8,128)(2,1)} %pad_maximum_fusion.1), channel_id=1, source_target_pairs={{0,32},{16,48},{32,64},{48,80},{64,96},{80,112},{96,0},{112,16},{1... | collective-permute-start | bytes 393224 | tf_op jit(solution)/shard_map/ppermute | solution.py:535
  28.4 15.5 %collective-permute-start.1 = (bf16[2,8,32,128]{3,2,1,0:T(8,128)(2,1)}, bf16[2,8,32,128]{3,2,1,0:T(8,128)(2,1)}, u32[]{:S(2)}, u32[]{:S(2)}) collective-permute-start(bf16[2,8,32,128]{3,2,1,0:T(8,128)(2,1)} %pad_maximum_fusion.1), channel_id=1, source_target_pairs={{0,16},{16,32},{32,48},{48,64},{64,80},{80,96},{96,112},{112,0},{1... | collective-permute-start | bytes 393224 | tf_op jit(solution)/shard_map/ppermute | solution.py:535
  31.8 1.2 copy-start.4
  33.0 0.8 copy-start.5
  33.8 21.1 %all-to-all-start = ((bf16[8,8,96,128]{3,2,1,0:T(8,128)(2,1)}), bf16[8,8,96,128]{3,2,1,0:T(8,128)(2,1)S(1)}, u32[]{:S(2)}, u32[]{:S(2)}) async-start(bf16[8,8,96,128]{3,2,1,0:T(8,128)(2,1)} %copy-done.4), calls=%async_computation | async-start | bytes 3145728 | tf_op jit(solution)/shard_map/all_to_all | solution.py:528
  37.4 8.5 %collective-permute-start.2 = (bf16[2,8,32,128]{3,2,1,0:T(8,128)(2,1)}, bf16[2,8,32,128]{3,2,1,0:T(8,128)(2,1)S(1)}, u32[]{:S(2)}, u32[]{:S(2)}) collective-permute-start(bf16[2,8,32,128]{3,2,1,0:T(8,128)(2,1)} %pad_maximum_fusion.1), channel_id=1, source_target_pairs={{0,112},{16,0},{32,16},{48,32},{64,48},{80,64},{96,80},{112,96},{1... | collective-permute-start | bytes 393224 | tf_op jit(solution)/shard_map/ppermute | solution.py:535
  38.5 11.8 %copy-start.17 = (s32[1024]{0:T(1024)S(1)}, s32[1024]{0:T(1024)}, u32[]{:S(2)}) copy-start(s32[1024]{0:T(1024)} %param.14) | copy-start | bytes 12292
  38.5 10.3 %collective-permute-start.8 = (bf16[1,8,32,128]{3,2,1,0:T(8,128)(2,1)S(1)}, bf16[1,8,32,128]{3,2,1,0:T(8,128)(2,1)S(1)}, u32[]{:S(2)}, u32[]{:S(2)}) collective-permute-start(bf16[1,8,32,128]{3,2,1,0:T(8,128)(2,1)S(1)} %slice.45), channel_id=1, source_target_pairs={{0,96},{16,112},{32,0},{48,16},{64,32},{80,48},{96,64},{112,80},{1... | collective-permute-start | bytes 196616 | tf_op jit(solution)/shard_map/ppermute | solution.py:535
  42.8 7.2 %collective-permute-start.7 = (bf16[1,8,32,128]{3,2,1,0:T(8,128)(2,1)S(1)}, bf16[1,8,32,128]{3,2,1,0:T(8,128)(2,1)S(1)}, u32[]{:S(2)}, u32[]{:S(2)}) collective-permute-start(bf16[1,8,32,128]{3,2,1,0:T(8,128)(2,1)S(1)} %slice.44), channel_id=1, source_target_pairs={{0,32},{16,48},{32,64},{48,80},{64,96},{80,112},{96,0},{112,16},{1... | collective-permute-start | bytes 196616 | tf_op jit(solution)/shard_map/ppermute | solution.py:535
  42.8 5.1 %collective-permute-start.5 = (bf16[2,8,32,128]{3,2,1,0:T(8,128)(2,1)S(1)}, bf16[2,8,32,128]{3,2,1,0:T(8,128)(2,1)S(1)}, u32[]{:S(2)}, u32[]{:S(2)}) collective-permute-start(bf16[2,8,32,128]{3,2,1,0:T(8,128)(2,1)S(1)} %collective-permute-done.3), channel_id=1, source_target_pairs={{0,16},{16,32},{32,48},{48,64},{64,80},{80,96},{96,112},{112,0},{1... | collective-permute-start | bytes 393224 | tf_op jit(solution)/shard_map/ppermute | solution.py:535
  43.9 5.0 %collective-permute-start.6 = (bf16[2,8,32,128]{3,2,1,0:T(8,128)(2,1)S(1)}, bf16[2,8,32,128]{3,2,1,0:T(8,128)(2,1)S(1)}, u32[]{:S(2)}, u32[]{:S(2)}) collective-permute-start(bf16[2,8,32,128]{3,2,1,0:T(8,128)(2,1)S(1)} %collective-permute-done.4), channel_id=1, source_target_pairs={{0,112},{16,0},{32,16},{48,32},{64,48},{80,64},{96,80},{112,96},{1... | collective-permute-start | bytes 393224 | tf_op jit(solution)/shard_map/ppermute | solution.py:535
  49.9 4.9 %collective-permute-start.9 = (bf16[8,2,8,32,128]{4,3,2,1,0:T(8,128)(2,1)S(1)}, bf16[8,2,8,32,128]{4,3,2,1,0:T(8,128)(2,1)}, u32[]{:S(2)}, u32[]{:S(2)}) collective-permute-start(bf16[8,2,8,32,128]{4,3,2,1,0:T(8,128)(2,1)S(1)} %fusion.1.mine_ref), channel_id=1, source_target_pairs={{0,8},{8,0},{1,9},{9,1},{2,10},{10,2},{3,11},{11,3},{4,12},{12,4},... | collective-permute-start | bytes 3145736 | tf_op jit(solution)/shard_map/ppermute | solution.py:524
  50.3 22.1 %copy-start.8 = (s32[4]{0:T(128)}, s32[4]{0:T(128)S(1)}, u32[]{:S(2)}) copy-start(s32[4]{0:T(128)S(1)} %pad_add_fusion.at_ref) | copy-start | bytes 52
  54.8 21.4 %copy-start.18 = (s32[8,128]{1,0:T(8,128)S(1)}, s32[8,128]{1,0:T(8,128)}, u32[]{:S(2)}) copy-start(s32[8,128]{1,0:T(8,128)} %param.15) | copy-start | bytes 12292
  54.9 21.4 %copy-start.14 = (bf16[256,64]{0,1:T(8,128)(2,1)S(1)}, bf16[256,64]{0,1:T(8,128)(2,1)}, u32[]{:S(2)}) copy-start(bf16[256,64]{0,1:T(8,128)(2,1)} %param.19) | copy-start | bytes 98308
  72.4 13.6 %copy-start.6 = (bf16[8,256,128]{2,1,0:T(8,128)(2,1)S(1)}, bf16[8,256,128]{2,1,0:T(8,128)(2,1)}, u32[]{:S(2)}) copy-start(bf16[8,256,128]{2,1,0:T(8,128)(2,1)} %copy-done.5) | copy-start | bytes 1572868
  72.4 13.6 %copy-start.7 = (bf16[256,256]{1,0:T(8,128)(2,1)S(1)}, bf16[256,256]{1,0:T(8,128)(2,1)}, u32[]{:S(2)}) copy-start(bf16[256,256]{1,0:T(8,128)(2,1)} %wo_ref.1) | copy-start | bytes 393220
  72.4 13.6 %all-to-all-start.2 = ((bf16[8,8,32,128]{3,2,1,0:T(8,128)(2,1)}), bf16[8,8,32,128]{3,2,1,0:T(8,128)(2,1)S(1)}, u32[]{:S(2)}, u32[]{:S(2)}) async-start(bf16[8,8,32,128]{3,2,1,0:T(8,128)(2,1)} %attend.1), calls=%async_computation.2 | async-start | bytes 1048576 | tf_op jit(solution)/shard_map/all_to_all | solution.py:528
  88.5 5.8 %collective-permute-start.10 = (bf16[264,128]{1,0:T(8,128)(2,1)S(1)}, bf16[264,128]{1,0:T(8,128)(2,1)S(1)}, u32[]{:S(2)}, u32[]{:S(2)}) collective-permute-start(bf16[264,128]{1,0:T(8,128)(2,1)S(1)} %get-tuple-element.14), channel_id=1, source_target_pairs={{0,128},{128,0},{1,129},{129,1},{2,130},{130,2},{3,131},{131,3},{4... | collective-permute-start | bytes 202760 | tf_op jit(solution)/shard_map/ppermute | solution.py:537
  94.3 15.1 %collective-permute-start.14 = (bf16[2,264,128]{2,1,0:T(8,128)(2,1)S(1)}, bf16[2,264,128]{2,1,0:T(8,128)(2,1)S(1)}, u32[]{:S(2)}, u32[]{:S(2)}) collective-permute-start(bf16[2,264,128]{2,1,0:T(8,128)(2,1)S(1)} %pad_maximum_fusion), channel_id=1, source_target_pairs={{0,96},{16,112},{32,0},{48,16},{64,32},{80,48},{96,64},{112,80},{1... | collective-permute-start | bytes 405512 | tf_op jit(solution)/shard_map/ppermute | solution.py:535
  97.7 14.5 %collective-permute-start.13 = (bf16[2,264,128]{2,1,0:T(8,128)(2,1)S(1)}, bf16[2,264,128]{2,1,0:T(8,128)(2,1)S(1)}, u32[]{:S(2)}, u32[]{:S(2)}) collective-permute-start(bf16[2,264,128]{2,1,0:T(8,128)(2,1)S(1)} %pad_maximum_fusion), channel_id=1, source_target_pairs={{0,32},{16,48},{32,64},{48,80},{64,96},{80,112},{96,0},{112,16},{1... | collective-permute-start | bytes 405512 | tf_op jit(solution)/shard_map/ppermute | solution.py:535
  97.7 18.9 %collective-permute-start.11 = (bf16[2,264,128]{2,1,0:T(8,128)(2,1)S(1)}, bf16[2,264,128]{2,1,0:T(8,128)(2,1)S(1)}, u32[]{:S(2)}, u32[]{:S(2)}) collective-permute-start(bf16[2,264,128]{2,1,0:T(8,128)(2,1)S(1)} %pad_maximum_fusion), channel_id=1, source_target_pairs={{0,16},{16,32},{32,48},{48,64},{64,80},{80,96},{96,112},{112,0},{1... | collective-permute-start | bytes 405512 | tf_op jit(solution)/shard_map/ppermute | solution.py:535
  99.6 9.8 %all-to-all-start.3 = ((bf16[8,48,128]{2,1,0:T(8,128)(2,1)}), bf16[8,48,128]{2,1,0:T(8,128)(2,1)S(1)}, u32[]{:S(2)}, u32[]{:S(2)}) async-start(bf16[8,48,128]{2,1,0:T(8,128)(2,1)} %get-tuple-element.13), calls=%async_computation.3 | async-start | bytes 196608 | tf_op jit(solution)/shard_map/all_to_all | solution.py:528
  103.0 13.6 %collective-permute-start.12 = (bf16[2,264,128]{2,1,0:T(8,128)(2,1)S(1)}, bf16[2,264,128]{2,1,0:T(8,128)(2,1)S(1)}, u32[]{:S(2)}, u32[]{:S(2)}) collective-permute-start(bf16[2,264,128]{2,1,0:T(8,128)(2,1)S(1)} %pad_maximum_fusion), channel_id=1, source_target_pairs={{0,112},{16,0},{32,16},{48,32},{64,48},{80,64},{96,80},{112,96},{1... | collective-permute-start | bytes 405512 | tf_op jit(solution)/shard_map/ppermute | solution.py:535
  109.4 12.2 %collective-permute-start.18 = (bf16[1,264,128]{2,1,0:T(8,128)(2,1)S(1)}, bf16[1,264,128]{2,1,0:T(8,128)(2,1)S(1)}, u32[]{:S(2)}, u32[]{:S(2)}) collective-permute-start(bf16[1,264,128]{2,1,0:T(8,128)(2,1)S(1)} %slice.50), channel_id=1, source_target_pairs={{0,96},{16,112},{32,0},{48,16},{64,32},{80,48},{96,64},{112,80},{1... | collective-permute-start | bytes 202760 | tf_op jit(solution)/shard_map/ppermute | solution.py:535
  112.2 9.4 %collective-permute-start.17 = (bf16[1,264,128]{2,1,0:T(8,128)(2,1)S(1)}, bf16[1,264,128]{2,1,0:T(8,128)(2,1)S(1)}, u32[]{:S(2)}, u32[]{:S(2)}) collective-permute-start(bf16[1,264,128]{2,1,0:T(8,128)(2,1)S(1)} %slice.49), channel_id=1, source_target_pairs={{0,32},{16,48},{32,64},{48,80},{64,96},{80,112},{96,0},{112,16},{1... | collective-permute-start | bytes 202760 | tf_op jit(solution)/shard_map/ppermute | solution.py:535
  112.8 6.4 %collective-permute-start.15 = (bf16[2,264,128]{2,1,0:T(8,128)(2,1)S(1)}, bf16[2,264,128]{2,1,0:T(8,128)(2,1)S(1)}, u32[]{:S(2)}, u32[]{:S(2)}) collective-permute-start(bf16[2,264,128]{2,1,0:T(8,128)(2,1)S(1)} %collective-permute-done.13), channel_id=1, source_target_pairs={{0,16},{16,32},{32,48},{48,64},{64,80},{80,96},{96,112},{112,0},{1... | collective-permute-start | bytes 405512 | tf_op jit(solution)/shard_map/ppermute | solution.py:535
  116.6 5.0 %collective-permute-start.16 = (bf16[2,264,128]{2,1,0:T(8,128)(2,1)S(1)}, bf16[2,264,128]{2,1,0:T(8,128)(2,1)S(1)}, u32[]{:S(2)}, u32[]{:S(2)}) collective-permute-start(bf16[2,264,128]{2,1,0:T(8,128)(2,1)S(1)} %collective-permute-done.14), channel_id=1, source_target_pairs={{0,112},{16,0},{32,16},{48,32},{64,48},{80,64},{96,80},{112,96},{1... | collective-permute-start | bytes 405512 | tf_op jit(solution)/shard_map/ppermute | solution.py:535
  121.6 18.6 %copy-start.10 = (bf16[8,2,264,128]{3,2,1,0:T(8,128)(2,1)}, bf16[8,2,264,128]{3,2,1,0:T(8,128)(2,1)S(1)}, u32[]{:S(2)}) copy-start(bf16[8,2,264,128]{3,2,1,0:T(8,128)(2,1)S(1)} %fusion.mine_ref) | copy-start | bytes 3244036
  121.7 31.7 %collective-permute-start.19 = (bf16[8,2,264,128]{3,2,1,0:T(8,128)(2,1)S(1)}, bf16[8,2,264,128]{3,2,1,0:T(8,128)(2,1)}, u32[]{:S(2)}, u32[]{:S(2)}) collective-permute-start(bf16[8,2,264,128]{3,2,1,0:T(8,128)(2,1)S(1)} %fusion.mine_ref), channel_id=1, source_target_pairs={{0,8},{8,0},{1,9},{9,1},{2,10},{10,2},{3,11},{11,3},{4,12},{12,4},... | collective-permute-start | bytes 3244040 | tf_op jit(solution)/shard_map/ppermute | solution.py:524
  139.3 4.8 %copy-start.12 = (bf16[1024,128]{1,0:T(8,128)(2,1)S(1)}, bf16[1024,128]{1,0:T(8,128)(2,1)}, u32[]{:S(2)}) copy-start(bf16[1024,128]{1,0:T(8,128)(2,1)} %param.20) | copy-start | bytes 786436
  140.2 4.8 %copy-start.13 = (bf16[128,512]{1,0:T(8,128)(2,1)S(1)}, bf16[128,512]{1,0:T(8,128)(2,1)}, u32[]{:S(2)}) copy-start(bf16[128,512]{1,0:T(8,128)(2,1)} %param.21) | copy-start | bytes 393220
  140.2 13.1 %all-to-all-start.5 = ((bf16[8,9,32,128]{3,2,1,0:T(8,128)(2,1)}), bf16[8,9,32,128]{3,2,1,0:T(8,128)(2,1)S(1)}, u32[]{:S(2)}, u32[]{:S(2)}) async-start(bf16[8,9,32,128]{3,2,1,0:T(8,128)(2,1)} %broadcast_in_dim.8), calls=%async_computation.5 | async-start | bytes 1179648 | tf_op jit(solution)/shard_map/all_to_all | solution.py:528
  153.3 0.8 copy-start.9
  230.9 3.0 %collective-permute-start.20 = (bf16[16,8,32,128]{3,2,1,0:T(8,128)(2,1)S(1)}, bf16[16,8,32,128]{3,2,1,0:T(8,128)(2,1)S(1)}, u32[]{:S(2)}, u32[]{:S(2)}) collective-permute-start(bf16[16,8,32,128]{3,2,1,0:T(8,128)(2,1)S(1)} %bitcast.70), channel_id=1, source_target_pairs={{0,8},{8,0},{1,9},{9,1},{2,10},{10,2},{3,11},{11,3},{4,12},{12,4},... | collective-permute-start | bytes 3145736 | tf_op jit(solution)/shard_map/ppermute | solution.py:524
  237.9 7.1 %copy-start.15 = (bf16[128,128]{1,0:T(8,128)(2,1)S(1)}, bf16[128,128]{1,0:T(8,128)(2,1)}, u32[]{:S(2)}) copy-start(bf16[128,128]{1,0:T(8,128)(2,1)} %param.22) | copy-start | bytes 98308
  237.9 7.2 %copy-start.16 = (bf16[128,128]{1,0:T(8,128)(2,1)S(1)}, bf16[128,128]{1,0:T(8,128)(2,1)}, u32[]{:S(2)}) copy-start(bf16[128,128]{1,0:T(8,128)(2,1)} %param.23) | copy-start | bytes 98308
  237.9 7.3 %copy-start = (f32[32,128,128]{2,1,0:T(8,128)S(1)}, f32[32,128,128]{2,1,0:T(8,128)}, u32[]{:S(2)}) copy-start(f32[32,128,128]{2,1,0:T(8,128)} %get-tuple-element.17.mid_ref) | copy-start | bytes 6291460
  237.9 39.1 %all-to-all-start.7 = ((bf16[128,32,128]{2,1,0:T(8,128)(2,1)}), bf16[128,32,128]{2,1,0:T(8,128)(2,1)S(1)}, u32[]{:S(2)}, u32[]{:S(2)}) async-start(bf16[128,32,128]{2,1,0:T(8,128)(2,1)} %bitcast.43), calls=%async_computation.7 | async-start | bytes 2097152 | tf_op jit(solution)/shard_map/all_to_all | solution.py:528
  249.2 1.3 copy-start.1
  277.0 1.6 copy-start.2

commit v6 on v5

--- a/solution.py
+++ b/solution.py
@@ -4,6 +4,7 @@
 import jax.numpy as jnp
 from jax import lax
 from jax.experimental import pallas as pl
+from jax.experimental.layout import Layout, with_layout_constraint
 from jax.experimental.pallas import tpu as pltpu
 from jax.sharding import Mesh
 from jax.sharding import PartitionSpec as P
@@ -277,7 +278,7 @@
 
 def outer_kernel(
     side, at_ref, left_ref, mine_ref, other_ref, couple_ref, live_ref, we_ref, wt_ref,
-    mid_ref, l_ref, r_ref, right_ref, rmask_ref, rows_ref, x_ref, update_ref, count_ref,
+    mid_ref, pair_ref, right_ref, rmask_ref, rows_ref, x_ref, update_ref, count_ref,
 ):
     step = pl.program_id(0)
     rows, lanes = couple_ref.shape[0], couple_ref.shape[1]
@@ -346,13 +347,13 @@
             mid_ref[i] = mid
             normed.append(standardize(mid, 0).astype(BF16))
         normed = jnp.concatenate(normed, axis=1)
-        for part, ref in ((0, l_ref), (2, r_ref)):
+        for part in (0, 2):
             gate = dot(wt_ref[part * channels : (part + 1) * channels], normed, (1, 0))
             value = dot(wt_ref[(part + 1) * channels : (part + 2) * channels], normed, (1, 0))
             both = sigmoid(gate) * value
             for i in range(rows):
                 live = live_ref[pl.ds(first + i, 1), :]
-                ref[i] = (both[:, i * lanes : (i + 1) * lanes] * live).astype(BF16)
+                pair_ref[i, part // 2] = (both[:, i * lanes : (i + 1) * lanes] * live).astype(BF16)
 
 
 def outer(at, left, mine, other, couple, live, w_exit, w_tri):
@@ -379,7 +380,10 @@
                 whole(w_exit.shape),
                 whole((4 * channels, channels)),
             ],
-            out_specs=[tile, tile, tile],
+            out_specs=[
+                tile,
+                pl.BlockSpec((rows, 2, channels, lanes), lambda t, at: (*move(t, at), 0)),
+            ],
             scratch_shapes=[
                 pltpu.VMEM((side // 2, entries, 2 * lanes), BF16),
                 pltpu.VMEM((entries, lanes), BF16),
@@ -391,8 +395,7 @@
         ),
         out_shape=[
             jax.ShapeDtypeStruct((pair_rows, channels, lanes), F32),
-            jax.ShapeDtypeStruct((pair_rows, channels, lanes), BF16),
-            jax.ShapeDtypeStruct((pair_rows, channels, lanes), BF16),
+            jax.ShapeDtypeStruct((pair_rows, 2, channels, lanes), BF16),
         ],
         compiler_params=params(60),
         name="outer",
@@ -615,7 +618,7 @@
     left = exchange(left, BRANCH_ROW)
     left = repeated(left[:, : steps + 1].transpose(1, 0, 2), chan)
     left = exchange(left, "chan")
-    mid, left_tri, right_tri = outer(
+    mid, operands = outer(
         at,
         left,
         right,
@@ -625,8 +628,8 @@
         tensor_exit_coefficients,
         trio_entry_coefficients,
     )
-    operands = jnp.stack([left_tri, right_tri]).transpose(2, 0, 1, 3)
-    operands = exchange(operands, CHIPS)
+    operands = with_layout_constraint(operands.transpose(2, 1, 0, 3), Layout((0, 1, 2, 3)))
+    operands = with_layout_constraint(exchange(operands, CHIPS), Layout((0, 1, 2, 3)))
     grid = (planes, chan, pair_rows, pair_cols)
     left_tri, right_tri = operands[:, 0].reshape(grid), operands[:, 1].reshape(grid)
     product = triangle(me, left_tri, right_tri, swap(right_tri))

time: 284 us -> 284 us (level)
    pallas_call x0 -> x1, local copies, waits for them, and re-layouts: none -> 2.94 us  [outer(): pl.pallas_call(functools.partial(outer_kernel, side), grid_spec=pltpu.Pre...]
where the time goes in v6:
time: 284 us; the launch traced here: 282 us
  blocking collectives  89.7 us (32%)
  waiting for transfers between devices  71.2 us (25%)
  starting transfers between devices  54.2 us (19%)
  Pallas kernels  50.8 us (18%)
  local copies, waits for them, and re-layouts  13.6 us (5%)
    all_to_all x3, blocking collectives, exchange(): return lax.all_to_all(x, axes, 0, 0, tiled=True)  89.7 us
    all_to_all x5, waiting for transfers between devices, exchange(): return lax.all_to_all(x, axes, 0, 0, tiled=True)  53.6 us
    ppermute x16, starting transfers between devices, shift(): lax.ppermute(y, 'row_0', tuple(((k, (k + by) % n) for k in range(n))))  26.5 us
    all_to_all x5, starting transfers between devices, exchange(): return lax.all_to_all(x, axes, 0, 0, tiled=True)  21.8 us
    pallas_call x1, Pallas kernels, attend(): pl.pallas_call(functools.partial(attend_kernel, width), grid_spec=pltpu.P...  17.5 us
    pallas_call x1, Pallas kernels, outer(): pl.pallas_call(functools.partial(outer_kernel, side), grid_spec=pltpu.Pre...  12.7 us
    ppermute x16, waiting for transfers between devices, shift(): lax.ppermute(y, 'row_0', tuple(((k, (k + by) % n) for k in range(n))))  8.78 us
    unnamed x54, local copies, waits for them, and re-layouts  8.07 us
  transfers between devices with their start and end apart: 26, of which 13 were waited for; matrix products, arithmetic and copies ran while one was open for 2% of the time, Pallas kernels for 2%

profile of v6, /device:TPU:32, one launch (start us, length us, event | category | flops | bytes accessed | tf_op | source)
XLA Modules:
  0.0 282.1 jit_solution(16352226421356281352)
XLA Ops:
  0.6 4.1 %pair_bias.1 = bf16[8,32,128]{2,1,0:T(8,128)(2,1)} custom-call(bf16[32,128,128]{2,1,0:T(8,128)(2,1)} %couple_ref.1, bf16[8,128]{1,0:T(8,128)(2,1)} %bitcast.93), custom_call_target="tpu_custom_call" | custom-call | tf_op jit(solution)/shard_map/pair_bias/pallas_call | solution.py:68
  4.8 11.7 %all_to_all.40 = bf16[8,32,128]{2,1,0:T(8,128)(2,1)S(1)} all-to-all(bf16[8,32,128]{2,1,0:T(8,128)(2,1)} %pair_bias.1), channel_id=1, replica_groups=mesh['branch'=2,'row_0'=8,'row_1'=2,'chan'=8] {'chan'}, dimensions={0} | all-to-all | bytes 131072 | tf_op jit(solution)/shard_map/all_to_all | solution.py:531
  16.5 2.7 collective-permute-start
  19.2 3.0 %collective-permute-done = bf16[8,32,128]{2,1,0:T(8,128)(2,1)S(1)} collective-permute-done((bf16[8,32,128]{2,1,0:T(8,128)(2,1)S(1)}, bf16[8,32,128]{2,1,0:T(8,128)(2,1)S(1)}, u32[]{:S(2)}, u32[]{:S(2)}) %collective-permute-start) | collective-permute-done | bytes 65568 | tf_op jit(solution)/shard_map/ppermute | solution.py:540
  23.0 5.4 %collective-permute-start.4 = (bf16[2,8,32,128]{3,2,1,0:T(8,128)(2,1)}, bf16[2,8,32,128]{3,2,1,0:T(8,128)(2,1)S(1)}, u32[]{:S(2)}, u32[]{:S(2)}) collective-permute-start(bf16[2,8,32,128]{3,2,1,0:T(8,128)(2,1)} %pad_maximum_fusion.1), channel_id=1, source_target_pairs={{0,96},{16,112},{32,0},{48,16},{64,32},{80,48},{96,64},{112,80},{1... | collective-permute-start | bytes 393224 | tf_op jit(solution)/shard_map/ppermute | solution.py:538
  28.4 1.0 collective-permute-start.1
  29.6 2.2 project_msa.1
  31.8 1.2 copy-done.4
  33.8 3.6 %all-to-all-start = ((bf16[8,8,96,128]{3,2,1,0:T(8,128)(2,1)}), bf16[8,8,96,128]{3,2,1,0:T(8,128)(2,1)S(1)}, u32[]{:S(2)}, u32[]{:S(2)}) async-start(bf16[8,8,96,128]{3,2,1,0:T(8,128)(2,1)} %copy-done.4), calls=%async_computation | async-start | bytes 3145728 | tf_op jit(solution)/shard_map/all_to_all | solution.py:531
  37.4 1.1 collective-permute-start.2
  38.5 4.2 %collective-permute-start.8 = (bf16[1,8,32,128]{3,2,1,0:T(8,128)(2,1)S(1)}, bf16[1,8,32,128]{3,2,1,0:T(8,128)(2,1)S(1)}, u32[]{:S(2)}, u32[]{:S(2)}) collective-permute-start(bf16[1,8,32,128]{3,2,1,0:T(8,128)(2,1)S(1)} %slice.45), channel_id=1, source_target_pairs={{0,96},{16,112},{32,0},{48,16},{64,32},{80,48},{96,64},{112,80},{1... | collective-permute-start | bytes 196616 | tf_op jit(solution)/shard_map/ppermute | solution.py:538
  42.8 1.0 collective-permute-start.5
  43.9 1.1 collective-permute-start.6
  45.0 0.9 bitcast_dynamic-update-slice_fusion.12
  46.0 2.0 collective-permute-done.5
  48.0 0.9 collective-permute-done.6
  48.9 1.1 collective-permute-done.7
  50.3 4.5 %all-to-all-done.qkv_ref = bf16[8,8,96,128]{3,2,1,0:T(8,128)(2,1)S(1)} async-done(((bf16[8,8,96,128]{3,2,1,0:T(8,128)(2,1)}), bf16[8,8,96,128]{3,2,1,0:T(8,128)(2,1)S(1)}, u32[]{:S(2)}, u32[]{:S(2)}) %all-to-all-start) | async-done | bytes 1572896 | tf_op jit(solution)/shard_map/all_to_all | solution.py:531
  54.9 17.5 %attend.1 = bf16[8,8,32,128]{3,2,1,0:T(8,128)(2,1)} custom-call(s32[4]{0:T(128)S(1)} %pad_add_fusion.at_ref, bf16[8,8,96,128]{3,2,1,0:T(8,128)(2,1)S(1)} %all-to-all-done.qkv_ref, bf16[8,2,8,32,128]{4,3,2,1,0:T(8,128)(2,1)S(1)} %fusion.1.mine_ref, bf16[8,2,8,32,128]{4,3,2,1,0:T(8,128)(2,1)} %collective-permute-done.9.other_ref, f32[1,1024]{1,0:T(1,128)S(1)} %bitcast.78), custom_call_target="tpu_custom_call" | custom-call | tf_op jit(solution)/shard_map/attend/pallas_call | solution.py:173
  72.4 3.8 %all-to-all-start.2 = ((bf16[8,8,32,128]{3,2,1,0:T(8,128)(2,1)}), bf16[8,8,32,128]{3,2,1,0:T(8,128)(2,1)S(1)}, u32[]{:S(2)}, u32[]{:S(2)}) async-start(bf16[8,8,32,128]{3,2,1,0:T(8,128)(2,1)} %attend.1), calls=%async_computation.2 | async-start | bytes 1048576 | tf_op jit(solution)/shard_map/all_to_all | solution.py:531
  76.4 9.6 %all-to-all-done.2.att_ref = bf16[8,8,32,128]{3,2,1,0:T(8,128)(2,1)S(1)} async-done(((bf16[8,8,32,128]{3,2,1,0:T(8,128)(2,1)}), bf16[8,8,32,128]{3,2,1,0:T(8,128)(2,1)S(1)}, u32[]{:S(2)}, u32[]{:S(2)}) %all-to-all-start.2) | async-done | bytes 524320 | tf_op jit(solution)/shard_map/all_to_all | solution.py:531
  85.9 2.6 sides.1
  88.5 2.7 collective-permute-start.10
  91.2 3.1 %collective-permute-done.10 = bf16[264,128]{1,0:T(8,128)(2,1)S(1)} collective-permute-done((bf16[264,128]{1,0:T(8,128)(2,1)S(1)}, bf16[264,128]{1,0:T(8,128)(2,1)S(1)}, u32[]{:S(2)}, u32[]{:S(2)}) %collective-permute-start.10) | collective-permute-done | bytes 67616 | tf_op jit(solution)/shard_map/ppermute | solution.py:540
  94.3 3.4 %collective-permute-start.14 = (bf16[2,264,128]{2,1,0:T(8,128)(2,1)S(1)}, bf16[2,264,128]{2,1,0:T(8,128)(2,1)S(1)}, u32[]{:S(2)}, u32[]{:S(2)}) collective-permute-start(bf16[2,264,128]{2,1,0:T(8,128)(2,1)S(1)} %pad_maximum_fusion), channel_id=1, source_target_pairs={{0,96},{16,112},{32,0},{48,16},{64,32},{80,48},{96,64},{112,80},{1... | collective-permute-start | bytes 405512 | tf_op jit(solution)/shard_map/ppermute | solution.py:538
  97.7 1.9 collective-permute-start.11
  99.6 3.4 %all-to-all-start.3 = ((bf16[8,48,128]{2,1,0:T(8,128)(2,1)}), bf16[8,48,128]{2,1,0:T(8,128)(2,1)S(1)}, u32[]{:S(2)}, u32[]{:S(2)}) async-start(bf16[8,48,128]{2,1,0:T(8,128)(2,1)} %get-tuple-element.12), calls=%async_computation.3 | async-start | bytes 196608 | tf_op jit(solution)/shard_map/all_to_all | solution.py:531
  103.2 6.2 %all-to-all-done.3 = bf16[8,48,128]{2,1,0:T(8,128)(2,1)S(1)} async-done(((bf16[8,48,128]{2,1,0:T(8,128)(2,1)}), bf16[8,48,128]{2,1,0:T(8,128)(2,1)S(1)}, u32[]{:S(2)}, u32[]{:S(2)}) %all-to-all-start.3) | async-done | bytes 98336 | tf_op jit(solution)/shard_map/all_to_all | solution.py:531
  109.4 2.8 collective-permute-start.18
  112.8 3.8 %collective-permute-start.15 = (bf16[2,264,128]{2,1,0:T(8,128)(2,1)S(1)}, bf16[2,264,128]{2,1,0:T(8,128)(2,1)S(1)}, u32[]{:S(2)}, u32[]{:S(2)}) collective-permute-start(bf16[2,264,128]{2,1,0:T(8,128)(2,1)S(1)} %collective-permute-done.13), channel_id=1, source_target_pairs={{0,16},{16,32},{32,48},{48,64},{64,80},{80,96},{96,112},{112,0},{1... | collective-permute-start | bytes 405512 | tf_op jit(solution)/shard_map/ppermute | solution.py:538
  116.7 2.4 collective-permute-done.15
  119.1 2.4 collective-permute-done.16
  121.8 17.4 %all_to_all.41 = bf16[32,16,128]{2,1,0:T(8,128)(2,1)S(1)} all-to-all(bf16[32,16,128]{2,1,0:T(8,128)(2,1)S(1)} %pad_maximum_fusion.2), channel_id=1, replica_groups=mesh['branch'=2,'row_0'=8,'row_1'=2,'chan'=8] {'branch','row_0','row_1'}, dimensions={0} | all-to-all | bytes 262144 | tf_op jit(solution)/shard_map/all_to_all | solution.py:531
  139.3 0.9 broadcast_in_dim.8
  140.2 3.7 %all-to-all-start.5 = ((bf16[8,9,32,128]{3,2,1,0:T(8,128)(2,1)}), bf16[8,9,32,128]{3,2,1,0:T(8,128)(2,1)S(1)}, u32[]{:S(2)}, u32[]{:S(2)}) async-start(bf16[8,9,32,128]{3,2,1,0:T(8,128)(2,1)} %broadcast_in_dim.8), calls=%async_computation.5 | async-start | bytes 1179648 | tf_op jit(solution)/shard_map/all_to_all | solution.py:531
  144.2 0.9 copy.45
  146.4 6.9 %all-to-all-done.5.left_ref = bf16[8,9,32,128]{3,2,1,0:T(8,128)(2,1)S(1)} async-done(((bf16[8,9,32,128]{3,2,1,0:T(8,128)(2,1)}), bf16[8,9,32,128]{3,2,1,0:T(8,128)(2,1)S(1)}, u32[]{:S(2)}, u32[]{:S(2)}) %all-to-all-start.5) | async-done | bytes 589856 | tf_op jit(solution)/shard_map/all_to_all | solution.py:531
  154.2 12.7 %outer.1 = (f32[32,128,128]{2,1,0:T(8,128)}, bf16[32,2,128,128]{3,2,1,0:T(8,128)(2,1)}) custom-call(s32[4]{0:T(128)} %copy-done.8, bf16[8,9,32,128]{3,2,1,0:T(8,128)(2,1)} %copy-done.9, bf16[8,2,264,128]{3,2,1,0:T(8,128)(2,1)} %copy-done.10, bf16[8,2,264,128]{3,2,1,0:T(8,128)(2,1)} %collective-permute-done.19.other_ref, bf16[32,128,128]{2,1,0:T(8,128)(2,1)} %couple_ref.1, ...), custom_call_target="tpu_custom_call" | custom-call | tf_op jit(solution)/shard_map/outer/pallas_call | solution.py:369
  166.9 2.9 %copy.51 = bf16[32,2,128,128]{3,0,1,2:T(8,128)(2,1)S(1)} copy(bf16[32,2,128,128]{3,2,1,0:T(8,128)(2,1)} %get-tuple-element.14) | data formatting | bytes 4194304 | tf_op jit(solution)/shard_map/outer/pallas_call | solution.py:369
  169.8 60.5 %all_to_all.42 = bf16[128,2,32,128]{3,2,1,0:T(8,128)(2,1)S(1)} all-to-all(bf16[128,2,32,128]{3,2,1,0:T(8,128)(2,1)S(1)} %bitcast.79), channel_id=1, replica_groups=mesh['branch'=2,'row_0'=8,'row_1'=2,'chan'=8] {'branch','row_0','chan'}, dimensions={0} | all-to-all | bytes 4194304 | tf_op jit(solution)/shard_map/all_to_all | solution.py:531
  230.8 2.6 collective-permute-done.20.other_ref
  233.5 3.9 %triangle.1 = bf16[16,8,32,128]{3,2,1,0:T(8,128)(2,1)} custom-call(s32[1]{0:T(128)} %bitcast.me_ref, bf16[16,8,32,128]{3,2,1,0:T(8,128)(2,1)S(1)} %bitcast.71, bf16[16,8,32,128]{3,2,1,0:T(8,128)(2,1)S(1)} %bitcast.70, bf16[16,8,32,128]{3,2,1,0:T(8,128)(2,1)S(1)} %collective-permute-done.20.other_ref), custom_call_target="tpu_custom_call" | custom-call | tf_op jit(solution)/shard_map/triangle/pallas_call | solution.py:430
  237.4 7.3 %all-to-all-start.7 = ((bf16[128,32,128]{2,1,0:T(8,128)(2,1)}), bf16[128,32,128]{2,1,0:T(8,128)(2,1)S(1)}, u32[]{:S(2)}, u32[]{:S(2)}) async-start(bf16[128,32,128]{2,1,0:T(8,128)(2,1)} %bitcast.41), calls=%async_computation.7 | async-start | bytes 2097152 | tf_op jit(solution)/shard_map/all_to_all | solution.py:531
  245.0 3.9 %switch.1.gate_ref = f32[32,128,128]{2,1,0:T(8,128)S(1)} custom-call(f32[32,128,128]{2,1,0:T(8,128)S(1)} %copy-done, bf16[128,128]{1,0:T(8,128)(2,1)S(1)} %bitcast.76), custom_call_target="tpu_custom_call" | custom-call | tf_op jit(solution)/shard_map/switch/pallas_call | solution.py:455
  249.0 1.3 copy-done.1
  250.3 26.4 %all-to-all-done.7.prod_ref = bf16[128,32,128]{2,1,0:T(8,128)(2,1)S(1)} async-done(((bf16[128,32,128]{2,1,0:T(8,128)(2,1)}), bf16[128,32,128]{2,1,0:T(8,128)(2,1)S(1)}, u32[]{:S(2)}, u32[]{:S(2)}) %all-to-all-start.7) | async-done | bytes 1048608 | tf_op jit(solution)/shard_map/all_to_all | solution.py:531
  276.8 1.6 copy-done.2
  278.4 3.7 %finish.1 = bf16[32,128,128]{2,1,0:T(8,128)(2,1)} custom-call(bf16[128,32,128]{2,1,0:T(8,128)(2,1)S(1)} %all-to-all-done.7.prod_ref, f32[32,128,128]{2,1,0:T(8,128)S(1)} %copy-done, f32[32,128,128]{2,1,0:T(8,128)S(1)} %copy-done.2, bf16[128,128]{1,0:T(8,128)(2,1)S(1)} %bitcast.75), custom_call_target="tpu_custom_call" | custom-call | tf_op jit(solution)/shard_map/finish/pallas_call | solution.py:514
  (100 shorter events, 6.7 us)
Async XLA Ops:
  0.6 28.7 %copy-start.11 = (bf16[256,1024]{1,0:T(8,128)(2,1)S(1)}, bf16[256,1024]{1,0:T(8,128)(2,1)}, u32[]{:S(2)}) copy-start(bf16[256,1024]{1,0:T(8,128)(2,1)} %param.16) | copy-start | bytes 1572868
  0.6 28.9 %copy-start.3 = (bf16[8,128,256]{2,1,0:T(8,128)(2,1)S(1)}, bf16[8,128,256]{2,1,0:T(8,128)(2,1)}, u32[]{:S(2)}) copy-start(bf16[8,128,256]{2,1,0:T(8,128)(2,1)} %stack_ref.1) | copy-start | bytes 1572868
  16.5 5.8 %collective-permute-start = (bf16[8,32,128]{2,1,0:T(8,128)(2,1)S(1)}, bf16[8,32,128]{2,1,0:T(8,128)(2,1)S(1)}, u32[]{:S(2)}, u32[]{:S(2)}) collective-permute-start(bf16[8,32,128]{2,1,0:T(8,128)(2,1)S(1)} %all_to_all.40), channel_id=1, source_target_pairs={{0,128},{128,0},{1,129},{129,1},{2,130},{130,2},{3,131},{131,3},{4... | collective-permute-start | bytes 196616 | tf_op jit(solution)/shard_map/ppermute | solution.py:540
  23.0 15.6 %collective-permute-start.4 = (bf16[2,8,32,128]{3,2,1,0:T(8,128)(2,1)}, bf16[2,8,32,128]{3,2,1,0:T(8,128)(2,1)S(1)}, u32[]{:S(2)}, u32[]{:S(2)}) collective-permute-start(bf16[2,8,32,128]{3,2,1,0:T(8,128)(2,1)} %pad_maximum_fusion.1), channel_id=1, source_target_pairs={{0,96},{16,112},{32,0},{48,16},{64,32},{80,48},{96,64},{112,80},{1... | collective-permute-start | bytes 393224 | tf_op jit(solution)/shard_map/ppermute | solution.py:538
  28.4 14.4 %collective-permute-start.3 = (bf16[2,8,32,128]{3,2,1,0:T(8,128)(2,1)}, bf16[2,8,32,128]{3,2,1,0:T(8,128)(2,1)S(1)}, u32[]{:S(2)}, u32[]{:S(2)}) collective-permute-start(bf16[2,8,32,128]{3,2,1,0:T(8,128)(2,1)} %pad_maximum_fusion.1), channel_id=1, source_target_pairs={{0,32},{16,48},{32,64},{48,80},{64,96},{80,112},{96,0},{112,16},{1... | collective-permute-start | bytes 393224 | tf_op jit(solution)/shard_map/ppermute | solution.py:538
  28.4 15.5 %collective-permute-start.1 = (bf16[2,8,32,128]{3,2,1,0:T(8,128)(2,1)}, bf16[2,8,32,128]{3,2,1,0:T(8,128)(2,1)}, u32[]{:S(2)}, u32[]{:S(2)}) collective-permute-start(bf16[2,8,32,128]{3,2,1,0:T(8,128)(2,1)} %pad_maximum_fusion.1), channel_id=1, source_target_pairs={{0,16},{16,32},{32,48},{48,64},{64,80},{80,96},{96,112},{112,0},{1... | collective-permute-start | bytes 393224 | tf_op jit(solution)/shard_map/ppermute | solution.py:538
  31.8 1.2 copy-start.4
  33.0 0.8 copy-start.5
  33.8 21.1 %all-to-all-start = ((bf16[8,8,96,128]{3,2,1,0:T(8,128)(2,1)}), bf16[8,8,96,128]{3,2,1,0:T(8,128)(2,1)S(1)}, u32[]{:S(2)}, u32[]{:S(2)}) async-start(bf16[8,8,96,128]{3,2,1,0:T(8,128)(2,1)} %copy-done.4), calls=%async_computation | async-start | bytes 3145728 | tf_op jit(solution)/shard_map/all_to_all | solution.py:531
  37.4 8.5 %collective-permute-start.2 = (bf16[2,8,32,128]{3,2,1,0:T(8,128)(2,1)}, bf16[2,8,32,128]{3,2,1,0:T(8,128)(2,1)S(1)}, u32[]{:S(2)}, u32[]{:S(2)}) collective-permute-start(bf16[2,8,32,128]{3,2,1,0:T(8,128)(2,1)} %pad_maximum_fusion.1), channel_id=1, source_target_pairs={{0,112},{16,0},{32,16},{48,32},{64,48},{80,64},{96,80},{112,96},{1... | collective-permute-start | bytes 393224 | tf_op jit(solution)/shard_map/ppermute | solution.py:538
  38.5 11.8 %copy-start.17 = (s32[1024]{0:T(1024)S(1)}, s32[1024]{0:T(1024)}, u32[]{:S(2)}) copy-start(s32[1024]{0:T(1024)} %param.14) | copy-start | bytes 12292
  38.5 10.3 %collective-permute-start.8 = (bf16[1,8,32,128]{3,2,1,0:T(8,128)(2,1)S(1)}, bf16[1,8,32,128]{3,2,1,0:T(8,128)(2,1)S(1)}, u32[]{:S(2)}, u32[]{:S(2)}) collective-permute-start(bf16[1,8,32,128]{3,2,1,0:T(8,128)(2,1)S(1)} %slice.45), channel_id=1, source_target_pairs={{0,96},{16,112},{32,0},{48,16},{64,32},{80,48},{96,64},{112,80},{1... | collective-permute-start | bytes 196616 | tf_op jit(solution)/shard_map/ppermute | solution.py:538
  42.8 7.2 %collective-permute-start.7 = (bf16[1,8,32,128]{3,2,1,0:T(8,128)(2,1)S(1)}, bf16[1,8,32,128]{3,2,1,0:T(8,128)(2,1)S(1)}, u32[]{:S(2)}, u32[]{:S(2)}) collective-permute-start(bf16[1,8,32,128]{3,2,1,0:T(8,128)(2,1)S(1)} %slice.44), channel_id=1, source_target_pairs={{0,32},{16,48},{32,64},{48,80},{64,96},{80,112},{96,0},{112,16},{1... | collective-permute-start | bytes 196616 | tf_op jit(solution)/shard_map/ppermute | solution.py:538
  42.8 5.1 %collective-permute-start.5 = (bf16[2,8,32,128]{3,2,1,0:T(8,128)(2,1)S(1)}, bf16[2,8,32,128]{3,2,1,0:T(8,128)(2,1)S(1)}, u32[]{:S(2)}, u32[]{:S(2)}) collective-permute-start(bf16[2,8,32,128]{3,2,1,0:T(8,128)(2,1)S(1)} %collective-permute-done.3), channel_id=1, source_target_pairs={{0,16},{16,32},{32,48},{48,64},{64,80},{80,96},{96,112},{112,0},{1... | collective-permute-start | bytes 393224 | tf_op jit(solution)/shard_map/ppermute | solution.py:538
  43.9 5.0 %collective-permute-start.6 = (bf16[2,8,32,128]{3,2,1,0:T(8,128)(2,1)S(1)}, bf16[2,8,32,128]{3,2,1,0:T(8,128)(2,1)S(1)}, u32[]{:S(2)}, u32[]{:S(2)}) collective-permute-start(bf16[2,8,32,128]{3,2,1,0:T(8,128)(2,1)S(1)} %collective-permute-done.4), channel_id=1, source_target_pairs={{0,112},{16,0},{32,16},{48,32},{64,48},{80,64},{96,80},{112,96},{1... | collective-permute-start | bytes 393224 | tf_op jit(solution)/shard_map/ppermute | solution.py:538
  49.9 4.9 %collective-permute-start.9 = (bf16[8,2,8,32,128]{4,3,2,1,0:T(8,128)(2,1)S(1)}, bf16[8,2,8,32,128]{4,3,2,1,0:T(8,128)(2,1)}, u32[]{:S(2)}, u32[]{:S(2)}) collective-permute-start(bf16[8,2,8,32,128]{4,3,2,1,0:T(8,128)(2,1)S(1)} %fusion.1.mine_ref), channel_id=1, source_target_pairs={{0,8},{8,0},{1,9},{9,1},{2,10},{10,2},{3,11},{11,3},{4,12},{12,4},... | collective-permute-start | bytes 3145736 | tf_op jit(solution)/shard_map/ppermute | solution.py:527
  50.3 22.1 %copy-start.8 = (s32[4]{0:T(128)}, s32[4]{0:T(128)S(1)}, u32[]{:S(2)}) copy-start(s32[4]{0:T(128)S(1)} %pad_add_fusion.at_ref) | copy-start | bytes 52
  54.8 21.4 %copy-start.18 = (s32[8,128]{1,0:T(8,128)S(1)}, s32[8,128]{1,0:T(8,128)}, u32[]{:S(2)}) copy-start(s32[8,128]{1,0:T(8,128)} %param.15) | copy-start | bytes 12292
  54.9 21.4 %copy-start.14 = (bf16[256,64]{0,1:T(8,128)(2,1)S(1)}, bf16[256,64]{0,1:T(8,128)(2,1)}, u32[]{:S(2)}) copy-start(bf16[256,64]{0,1:T(8,128)(2,1)} %param.19) | copy-start | bytes 98308
  72.4 13.6 %copy-start.6 = (bf16[8,256,128]{2,1,0:T(8,128)(2,1)S(1)}, bf16[8,256,128]{2,1,0:T(8,128)(2,1)}, u32[]{:S(2)}) copy-start(bf16[8,256,128]{2,1,0:T(8,128)(2,1)} %copy-done.5) | copy-start | bytes 1572868
  72.4 13.6 %copy-start.7 = (bf16[256,256]{1,0:T(8,128)(2,1)S(1)}, bf16[256,256]{1,0:T(8,128)(2,1)}, u32[]{:S(2)}) copy-start(bf16[256,256]{1,0:T(8,128)(2,1)} %wo_ref.1) | copy-start | bytes 393220
  72.4 13.6 %all-to-all-start.2 = ((bf16[8,8,32,128]{3,2,1,0:T(8,128)(2,1)}), bf16[8,8,32,128]{3,2,1,0:T(8,128)(2,1)S(1)}, u32[]{:S(2)}, u32[]{:S(2)}) async-start(bf16[8,8,32,128]{3,2,1,0:T(8,128)(2,1)} %attend.1), calls=%async_computation.2 | async-start | bytes 1048576 | tf_op jit(solution)/shard_map/all_to_all | solution.py:531
  88.5 5.8 %collective-permute-start.10 = (bf16[264,128]{1,0:T(8,128)(2,1)S(1)}, bf16[264,128]{1,0:T(8,128)(2,1)S(1)}, u32[]{:S(2)}, u32[]{:S(2)}) collective-permute-start(bf16[264,128]{1,0:T(8,128)(2,1)S(1)} %get-tuple-element.13), channel_id=1, source_target_pairs={{0,128},{128,0},{1,129},{129,1},{2,130},{130,2},{3,131},{131,3},{4... | collective-permute-start | bytes 202760 | tf_op jit(solution)/shard_map/ppermute | solution.py:540
  94.3 15.1 %collective-permute-start.14 = (bf16[2,264,128]{2,1,0:T(8,128)(2,1)S(1)}, bf16[2,264,128]{2,1,0:T(8,128)(2,1)S(1)}, u32[]{:S(2)}, u32[]{:S(2)}) collective-permute-start(bf16[2,264,128]{2,1,0:T(8,128)(2,1)S(1)} %pad_maximum_fusion), channel_id=1, source_target_pairs={{0,96},{16,112},{32,0},{48,16},{64,32},{80,48},{96,64},{112,80},{1... | collective-permute-start | bytes 405512 | tf_op jit(solution)/shard_map/ppermute | solution.py:538
  97.7 14.5 %collective-permute-start.13 = (bf16[2,264,128]{2,1,0:T(8,128)(2,1)S(1)}, bf16[2,264,128]{2,1,0:T(8,128)(2,1)S(1)}, u32[]{:S(2)}, u32[]{:S(2)}) collective-permute-start(bf16[2,264,128]{2,1,0:T(8,128)(2,1)S(1)} %pad_maximum_fusion), channel_id=1, source_target_pairs={{0,32},{16,48},{32,64},{48,80},{64,96},{80,112},{96,0},{112,16},{1... | collective-permute-start | bytes 405512 | tf_op jit(solution)/shard_map/ppermute | solution.py:538
  97.7 18.9 %collective-permute-start.11 = (bf16[2,264,128]{2,1,0:T(8,128)(2,1)S(1)}, bf16[2,264,128]{2,1,0:T(8,128)(2,1)S(1)}, u32[]{:S(2)}, u32[]{:S(2)}) collective-permute-start(bf16[2,264,128]{2,1,0:T(8,128)(2,1)S(1)} %pad_maximum_fusion), channel_id=1, source_target_pairs={{0,16},{16,32},{32,48},{48,64},{64,80},{80,96},{96,112},{112,0},{1... | collective-permute-start | bytes 405512 | tf_op jit(solution)/shard_map/ppermute | solution.py:538
  99.6 9.8 %all-to-all-start.3 = ((bf16[8,48,128]{2,1,0:T(8,128)(2,1)}), bf16[8,48,128]{2,1,0:T(8,128)(2,1)S(1)}, u32[]{:S(2)}, u32[]{:S(2)}) async-start(bf16[8,48,128]{2,1,0:T(8,128)(2,1)} %get-tuple-element.12), calls=%async_computation.3 | async-start | bytes 196608 | tf_op jit(solution)/shard_map/all_to_all | solution.py:531
  103.0 13.6 %collective-permute-start.12 = (bf16[2,264,128]{2,1,0:T(8,128)(2,1)S(1)}, bf16[2,264,128]{2,1,0:T(8,128)(2,1)S(1)}, u32[]{:S(2)}, u32[]{:S(2)}) collective-permute-start(bf16[2,264,128]{2,1,0:T(8,128)(2,1)S(1)} %pad_maximum_fusion), channel_id=1, source_target_pairs={{0,112},{16,0},{32,16},{48,32},{64,48},{80,64},{96,80},{112,96},{1... | collective-permute-start | bytes 405512 | tf_op jit(solution)/shard_map/ppermute | solution.py:538
  109.4 12.2 %collective-permute-start.18 = (bf16[1,264,128]{2,1,0:T(8,128)(2,1)S(1)}, bf16[1,264,128]{2,1,0:T(8,128)(2,1)S(1)}, u32[]{:S(2)}, u32[]{:S(2)}) collective-permute-start(bf16[1,264,128]{2,1,0:T(8,128)(2,1)S(1)} %slice.50), channel_id=1, source_target_pairs={{0,96},{16,112},{32,0},{48,16},{64,32},{80,48},{96,64},{112,80},{1... | collective-permute-start | bytes 202760 | tf_op jit(solution)/shard_map/ppermute | solution.py:538
  112.2 9.4 %collective-permute-start.17 = (bf16[1,264,128]{2,1,0:T(8,128)(2,1)S(1)}, bf16[1,264,128]{2,1,0:T(8,128)(2,1)S(1)}, u32[]{:S(2)}, u32[]{:S(2)}) collective-permute-start(bf16[1,264,128]{2,1,0:T(8,128)(2,1)S(1)} %slice.49), channel_id=1, source_target_pairs={{0,32},{16,48},{32,64},{48,80},{64,96},{80,112},{96,0},{112,16},{1... | collective-permute-start | bytes 202760 | tf_op jit(solution)/shard_map/ppermute | solution.py:538
  112.8 6.4 %collective-permute-start.15 = (bf16[2,264,128]{2,1,0:T(8,128)(2,1)S(1)}, bf16[2,264,128]{2,1,0:T(8,128)(2,1)S(1)}, u32[]{:S(2)}, u32[]{:S(2)}) collective-permute-start(bf16[2,264,128]{2,1,0:T(8,128)(2,1)S(1)} %collective-permute-done.13), channel_id=1, source_target_pairs={{0,16},{16,32},{32,48},{48,64},{64,80},{80,96},{96,112},{112,0},{1... | collective-permute-start | bytes 405512 | tf_op jit(solution)/shard_map/ppermute | solution.py:538
  116.6 5.0 %collective-permute-start.16 = (bf16[2,264,128]{2,1,0:T(8,128)(2,1)S(1)}, bf16[2,264,128]{2,1,0:T(8,128)(2,1)S(1)}, u32[]{:S(2)}, u32[]{:S(2)}) collective-permute-start(bf16[2,264,128]{2,1,0:T(8,128)(2,1)S(1)} %collective-permute-done.14), channel_id=1, source_target_pairs={{0,112},{16,0},{32,16},{48,32},{64,48},{80,64},{96,80},{112,96},{1... | collective-permute-start | bytes 405512 | tf_op jit(solution)/shard_map/ppermute | solution.py:538
  121.6 18.6 %copy-start.10 = (bf16[8,2,264,128]{3,2,1,0:T(8,128)(2,1)}, bf16[8,2,264,128]{3,2,1,0:T(8,128)(2,1)S(1)}, u32[]{:S(2)}) copy-start(bf16[8,2,264,128]{3,2,1,0:T(8,128)(2,1)S(1)} %fusion.mine_ref) | copy-start | bytes 3244036
  121.7 31.7 %collective-permute-start.19 = (bf16[8,2,264,128]{3,2,1,0:T(8,128)(2,1)S(1)}, bf16[8,2,264,128]{3,2,1,0:T(8,128)(2,1)}, u32[]{:S(2)}, u32[]{:S(2)}) collective-permute-start(bf16[8,2,264,128]{3,2,1,0:T(8,128)(2,1)S(1)} %fusion.mine_ref), channel_id=1, source_target_pairs={{0,8},{8,0},{1,9},{9,1},{2,10},{10,2},{3,11},{11,3},{4,12},{12,4},... | collective-permute-start | bytes 3244040 | tf_op jit(solution)/shard_map/ppermute | solution.py:527
  139.3 4.8 %copy-start.12 = (bf16[1024,128]{1,0:T(8,128)(2,1)S(1)}, bf16[1024,128]{1,0:T(8,128)(2,1)}, u32[]{:S(2)}) copy-start(bf16[1024,128]{1,0:T(8,128)(2,1)} %param.20) | copy-start | bytes 786436
  140.2 4.8 %copy-start.13 = (bf16[128,512]{1,0:T(8,128)(2,1)S(1)}, bf16[128,512]{1,0:T(8,128)(2,1)}, u32[]{:S(2)}) copy-start(bf16[128,512]{1,0:T(8,128)(2,1)} %param.21) | copy-start | bytes 393220
  140.2 13.1 %all-to-all-start.5 = ((bf16[8,9,32,128]{3,2,1,0:T(8,128)(2,1)}), bf16[8,9,32,128]{3,2,1,0:T(8,128)(2,1)S(1)}, u32[]{:S(2)}, u32[]{:S(2)}) async-start(bf16[8,9,32,128]{3,2,1,0:T(8,128)(2,1)} %broadcast_in_dim.8), calls=%async_computation.5 | async-start | bytes 1179648 | tf_op jit(solution)/shard_map/all_to_all | solution.py:531
  153.3 0.8 copy-start.9
  230.7 2.7 collective-permute-start.20
  237.4 7.4 %copy-start.15 = (bf16[128,128]{1,0:T(8,128)(2,1)S(1)}, bf16[128,128]{1,0:T(8,128)(2,1)}, u32[]{:S(2)}) copy-start(bf16[128,128]{1,0:T(8,128)(2,1)} %param.22) | copy-start | bytes 98308
  237.4 7.5 %copy-start.16 = (bf16[128,128]{1,0:T(8,128)(2,1)S(1)}, bf16[128,128]{1,0:T(8,128)(2,1)}, u32[]{:S(2)}) copy-start(bf16[128,128]{1,0:T(8,128)(2,1)} %param.23) | copy-start | bytes 98308
  237.4 7.6 %copy-start = (f32[32,128,128]{2,1,0:T(8,128)S(1)}, f32[32,128,128]{2,1,0:T(8,128)}, u32[]{:S(2)}) copy-start(f32[32,128,128]{2,1,0:T(8,128)} %get-tuple-element.15.mid_ref) | copy-start | bytes 6291460
  237.4 39.3 %all-to-all-start.7 = ((bf16[128,32,128]{2,1,0:T(8,128)(2,1)}), bf16[128,32,128]{2,1,0:T(8,128)(2,1)S(1)}, u32[]{:S(2)}, u32[]{:S(2)}) async-start(bf16[128,32,128]{2,1,0:T(8,128)(2,1)} %bitcast.41), calls=%async_computation.7 | async-start | bytes 2097152 | tf_op jit(solution)/shard_map/all_to_all | solution.py:531
  249.0 1.3 copy-start.1
  276.8 1.6 copy-start.2
